TPU v7x, 512 devices: a whole 4x4x16 slice. The times are simulated.
512 devices in a mesh: gx: 16 (over z), gy: 8 (over x_hi, y), gz: 4 (over x_lo, core).
Axes of the slice: x: 4 (x_hi: 2, x_lo: 2; x = x_hi * 2 + x_lo), y: 4, z: 16, core: 2. Of those that a mesh axis runs over, the one named last changes fastest.
Arguments:
- stress_trial: float32 [6, 12582912], P(None, ('gx', 'gy', 'gz')), may hold values from -6 to 6
- mean_stress: float32 [12582912], P(('gx', 'gy', 'gz')), may hold values from 0.3 to 2
- consolidation: float32 [12582912], P(('gx', 'gy', 'gz')), may hold values from 2.5 to 4
- point_velocity: float32 [3, 12582912], P(None, ('gx', 'gy', 'gz')), may hold values from -6 to 6
- point_weight: float32 [12582912], P(('gx', 'gy', 'gz')), may hold values from 0.5 to 1
- point_cell: int32 [12582912], P(('gx', 'gy', 'gz')), may hold values from 0 to 16383
- yield_flag: int32 [12582912], P(('gx', 'gy', 'gz')), may hold values 0 or 1
- point_count: int32 [16, 8, 4], P('gx', 'gy', 'gz'), may hold values from 12288 to 24576, as said below
- porosity: float32 [64, 128, 1024], P('gz', 'gx', 'gy'), may hold values from 0.2 to 0.5
- permeability: float32 [64, 128, 1024], P('gz', 'gx', 'gy'), may hold values from 1 to 10
Outputs:
- velocity: float32 [3, 64, 128, 1024], P(None, 'gz', 'gx', 'gy')
- pressure: float32 [64, 128, 1024], P('gz', 'gx', 'gy')
Inputs may be any that keep to these rules, and one draw needn't show every extreme that they name: `point_cell`: a cell index within the brick, levels slowest, then rows, then columns. `point_count`: slots below the count hold live points, the rest are empty; some brick is full.
All inputs are finite; a program needn't handle non-finite values. No bound on the sum of `yield_flag` on one device may be relied on, other than what follows from the above.
Results may differ from a plain program's by a relative error of at most 0.0003.
Values sent between devices are 32-bit elements; how exact they have to be, the bound alone decides.
A program may use at most 128 MiB of HBM per device.

v0:
```python
import jax
import jax.numpy as jnp
from jax import lax
from jax.sharding import PartitionSpec as P

time_step = 0.25
storage_rate = 0.002
source_rate = 0.003
critical_slope = 1.2
mass_floor = 0.5
shear_floor = 1.0


def padded_2(cells, sides, width):
    for axis, dim in sides:
        count = lax.axis_size(axis)
        ends = count - 1
        head = lax.slice_in_dim(cells, 0, width, axis=dim)
        tail = lax.slice_in_dim(cells, cells.shape[dim] - width, cells.shape[dim], axis=dim)
        cells = jnp.concatenate(
            [
                lax.ppermute(tail, axis, [(i, (i + 1) % count) for i in range(ends)]),
                cells,
                lax.ppermute(head, axis, [((i + 1) % count, i) for i in range(ends)]),
            ],
            axis=dim,
        )
    return cells


def along_x(padded):
    return (padded[..., 1:-1, 2:, 1:-1] - padded[..., 1:-1, :-2, 1:-1]) * 0.5


def along_y(padded):
    return (padded[..., 1:-1, 1:-1, 2:] - padded[..., 1:-1, 1:-1, :-2]) * 0.5


def along_z(padded):
    return (padded[..., 2:, 1:-1, 1:-1] - padded[..., :-2, 1:-1, 1:-1]) * 0.5


def harmonic(former, latter):
    return 2.0 * former * latter / (former + latter)


def returned_stress(stress_trial, mean_stress, consolidation, yield_flag):
    sq_normal = (
        stress_trial[0] * stress_trial[0]
        + stress_trial[1] * stress_trial[1]
        + stress_trial[2] * stress_trial[2]
    )
    sq_shear = (
        stress_trial[3] * stress_trial[3]
        + stress_trial[4] * stress_trial[4]
        + stress_trial[5] * stress_trial[5]
    )
    shear_size = jnp.sqrt(1.5 * (sq_normal + 2.0 * sq_shear))
    yield_size = critical_slope * jnp.sqrt(mean_stress * (consolidation - mean_stress))
    factor = jnp.where(yield_flag == 1, yield_size / jnp.maximum(shear_size, shear_floor), 1.0)
    isotropic = jnp.array([1.0, 1.0, 1.0, 0.0, 0.0, 0.0], dtype=jnp.float32)[:, None]
    return stress_trial * factor - isotropic * mean_stress


def point_sums(stress, point_velocity, weight, cell_index, segments):
    stacked = jnp.concatenate([stress * weight, point_velocity * weight, weight[None]], axis=0)
    return jax.vmap(
        lambda component: jax.ops.segment_sum(component, cell_index, num_segments=segments)
    )(stacked)


def brick_velocity(cell_sums, padded):
    floored = jnp.maximum(cell_sums[9], mass_floor)
    force_x = along_x(padded[0]) + along_y(padded[3]) + along_z(padded[5])
    force_y = along_x(padded[3]) + along_y(padded[1]) + along_z(padded[4])
    force_z = along_x(padded[5]) + along_y(padded[4]) + along_z(padded[2])
    return jnp.stack(
        [
            (cell_sums[6] + time_step * force_x) / floored,
            (cell_sums[7] + time_step * force_y) / floored,
            (cell_sums[8] + time_step * force_z) / floored,
        ]
    )


def divergence(padded_velocity):
    return along_x(padded_velocity[0]) + along_y(padded_velocity[1]) + along_z(padded_velocity[2])


def band_terms(porosity, permeability, level_below, level_above, at_top, dilation):
    up_face = harmonic(permeability, level_above)
    down_face = harmonic(level_below, permeability)
    top_face = jnp.where(at_top, permeability, up_face)
    lower_band = -time_step * down_face
    upper_band = -time_step * up_face
    main_band = storage_rate * porosity + time_step * (down_face + top_face)
    right_side = -source_rate * (1.0 - porosity) * dilation
    return (lower_band, main_band, upper_band, right_side)


def earlier(values, stride, filler):
    head = jnp.full((stride,) + values.shape[1:], filler, values.dtype)
    return jnp.concatenate([head, values[:-stride]], axis=0)


def later(values, stride, filler):
    tail = jnp.full((stride,) + values.shape[1:], filler, values.dtype)
    return jnp.concatenate([values[stride:], tail], axis=0)


def cyclic_solve(lower_band, main_band, upper_band, right_side):
    length = main_band.shape[0]
    for bit in range((length - 1).bit_length()):
        stride = 1 << bit
        back_weight = -lower_band / earlier(main_band, stride, 1.0)
        ahead_weight = -upper_band / later(main_band, stride, 1.0)
        new_lower = back_weight * earlier(lower_band, stride, 0.0)
        new_upper = ahead_weight * later(upper_band, stride, 0.0)
        new_main = (
            main_band
            + back_weight * earlier(upper_band, stride, 0.0)
            + ahead_weight * later(lower_band, stride, 0.0)
        )
        new_right = (
            right_side
            + back_weight * earlier(right_side, stride, 0.0)
            + ahead_weight * later(right_side, stride, 0.0)
        )
        lower_band, main_band, upper_band, right_side = (new_lower, new_main, new_upper, new_right)
    return right_side / main_band


def brick_bands(porosity, permeability, padded, dilation, levels, layer_count):
    level_index = lax.axis_index("gz") * levels + jnp.arange(levels, dtype=jnp.int32)
    at_top = (level_index == levels * layer_count - 1)[:, None, None]
    return band_terms(
        porosity,
        permeability,
        padded[6, :-2, 1:-1, 1:-1],
        padded[6, 2:, 1:-1, 1:-1],
        at_top,
        dilation,
    )


def shards(
    stress_trial,
    mean_stress,
    consolidation,
    point_velocity,
    point_weight,
    point_cell,
    yield_flag,
    point_count,
    porosity,
    permeability,
):
    levels, extent, breadth = porosity.shape
    slot_index = jnp.arange(mean_stress.shape[0], dtype=jnp.int32)
    weight = jnp.where(slot_index < point_count[0, 0, 0], point_weight, 0.0)
    stress = returned_stress(stress_trial, mean_stress, consolidation, yield_flag)
    cell_sums = point_sums(
        stress, point_velocity, weight, point_cell, levels * extent * breadth
    ).reshape(10, levels, extent, breadth)
    outgoing = jnp.concatenate([cell_sums[:6], permeability[None]], axis=0)
    padded = padded_2(outgoing, (("gx", 2), ("gy", 3), ("gz", 1)), 1)
    velocity = brick_velocity(cell_sums, padded)
    padded_velocity = padded_2(velocity, (("gx", 2), ("gy", 3), ("gz", 1)), 1)
    dilation = divergence(padded_velocity)
    layer_count = lax.axis_size("gz")
    band_set = brick_bands(porosity, permeability, padded, dilation, levels, layer_count)
    columns = lax.all_to_all(jnp.stack(band_set), "gz", split_axis=3, concat_axis=1, tiled=True)
    height = columns.shape[1]
    flattened = columns.reshape(4, height, -1)
    solved = cyclic_solve(flattened[0], flattened[1], flattened[2], flattened[3])
    pressure = lax.all_to_all(
        solved.reshape(height, extent, -1), "gz", split_axis=0, concat_axis=2, tiled=True
    )
    padded_pressure = padded_2(pressure, (("gx", 1), ("gy", 2), ("gz", 0)), 1)
    gradient = jnp.stack(
        [along_x(padded_pressure), along_y(padded_pressure), along_z(padded_pressure)]
    )
    return (velocity - time_step * gradient, pressure)


def solution(mesh):
    placed = (
        P(None, ("gx", "gy", "gz")),
        P(("gx", "gy", "gz")),
        P(("gx", "gy", "gz")),
        P(None, ("gx", "gy", "gz")),
        P(("gx", "gy", "gz")),
        P(("gx", "gy", "gz")),
        P(("gx", "gy", "gz")),
        P("gx", "gy", "gz"),
        P("gz", "gx", "gy"),
        P("gz", "gx", "gy"),
    )
    return jax.shard_map(
        shards,
        mesh=mesh,
        in_specs=placed,
        out_specs=(P(None, "gz", "gx", "gy"), P("gz", "gx", "gy")),
        check_vma=False,
    )
```

profile of v0, /device:TPU:102, one launch (start us, length us, event | category | flops | bytes accessed | tf_op | source)
XLA Modules:
  0.0 308.7 jit_solution(13120438609213550886)
XLA Ops:
  0.7 3.6 %sqrt_maximum_fusion = f32[1,24576]{1,0:T(1,128)S(1)} fusion(f32[6,24576]{1,0:T(8,128)} %param.11), kind=kLoop, calls=%fused_computation.40 | loop fusion | flops 344064 | bytes 688128 | tf_op jit(solution)/shard_map/max | solution.py:60
  4.9 1.1 fusion.7
  6.0 1.1 broadcast_multiply_fusion
  7.2 0.2 subtract_multiply_fusion
  7.4 0.3 maximum_bitcast_fusion
  7.7 7.0 %copy.32 = f32[24576,10]{1,0:T(8,128)} copy(f32[24576,10]{0,1:T(8,128)S(1)} %maximum_bitcast_fusion) | data formatting | bytes 1966080 | tf_op jit(solution)/shard_map/concatenate | solution.py:66
  14.7 134.6 %scatter_custom_fusion = f32[10,16384]{0,1:T(8,128)} fusion(s32[24576]{0:T(1024)} %param.16, f32[24576,10]{1,0:T(8,128)} %copy.32, f32[]{:T(128)} %constant.16.clone.1), kind=kCustom, calls=%fused_computation.6 | custom fusion | flops 245760 | bytes 655872 | tf_op jit(solution)/shard_map/vmap()/scatter-add | solution.py:68
  149.3 5.3 %copy.33 = f32[6,16,8,128]{3,2,1,0:T(8,128)S(1)} copy(f32[6,16,8,128]{0,3,2,1:T(8,128)} %bitcast.83) | data formatting | bytes 786432 | tf_op jit(solution)/shard_map/slice | solution.py:165
  154.7 5.0 %collective-permute-start = (f32[7,16,1,128]{3,2,1,0:T(1,128)S(1)}, f32[7,16,1,128]{3,2,1,0:T(1,128)S(1)}, u32[]{:S(2)}, u32[]{:S(2)}) collective-permute-start(f32[7,16,1,128]{3,2,1,0:T(1,128)S(1)} %get-tuple-element.41), channel_id=1, source_target_pairs={{0,32},{32,64},{64,96},{96,128},{128,160},{160,192},{192,224},{224... | collective-permute-start | bytes 172040 | tf_op jit(solution)/shard_map/ppermute | solution.py:22
  159.7 1.9 collective-permute-start.1
  161.6 5.3 %collective-permute-done.1 = f32[7,16,1,128]{3,2,1,0:T(1,128)S(1)} collective-permute-done((f32[7,16,1,128]{3,2,1,0:T(1,128)S(1)}, f32[7,16,1,128]{3,2,1,0:T(1,128)S(1)}, u32[]{:S(2)}, u32[]{:S(2)}) %collective-permute-start.1) | collective-permute-done | bytes 57376 | tf_op jit(solution)/shard_map/ppermute | solution.py:24
  167.0 0.2 pad_maximum_fusion.1
  167.2 0.3 fusion.44
  167.5 0.5 copy.34
  168.0 3.5 %collective-permute-start.2 = (f32[7,16,10,1]{1,3,2,0:T(1,128)S(1)}, f32[7,16,10,1]{1,3,2,0:T(1,128)S(1)}, u32[]{:S(2)}, u32[]{:S(2)}) collective-permute-start(f32[7,16,10,1]{1,3,2,0:T(1,128)S(1)} %copy.34), channel_id=1, source_target_pairs={{0,4},{4,8},{8,12},{12,16},{16,20},{20,24},{24,28},{1,5},{5,9},{9,... | collective-permute-start | bytes 13448 | tf_op jit(solution)/shard_map/ppermute | solution.py:22
  171.5 0.5 copy.35
  172.0 6.0 %collective-permute-start.3 = (f32[7,16,10,1]{1,3,2,0:T(1,128)S(1)}, f32[7,16,10,1]{1,3,2,0:T(1,128)S(1)}, u32[]{:S(2)}, u32[]{:S(2)}) collective-permute-start(f32[7,16,10,1]{1,3,2,0:T(1,128)S(1)} %copy.35), channel_id=1, source_target_pairs={{4,0},{8,4},{12,8},{16,12},{20,16},{24,20},{28,24},{5,1},{9,5},{13... | collective-permute-start | bytes 13448 | tf_op jit(solution)/shard_map/ppermute | solution.py:24
  177.9 0.5 copy.36
  178.5 1.1 collective-permute-done.3
  179.5 0.5 copy.37
  180.1 0.2 pad_maximum_fusion.12
  180.3 1.9 collective-permute-start.4
  182.2 3.8 %collective-permute-start.5 = (f32[7,1,10,130]{3,2,1,0:T(8,128)S(1)}, f32[7,1,10,130]{3,2,1,0:T(8,128)S(1)}, u32[]{:S(2)}, u32[]{:S(2)}) collective-permute-start(f32[7,1,10,130]{3,2,1,0:T(8,128)S(1)} %get-tuple-element.23), channel_id=1, source_target_pairs={{1,0},{2,1},{3,2},{5,4},{6,5},{7,6},{9,8},{10,9},{11,10},{13,12},{... | collective-permute-start | bytes 109208 | tf_op jit(solution)/shard_map/ppermute | solution.py:24
  186.1 28.1 %slice_reduce_fusion.2 = (f32[16384]{0:T(1024)S(1)}, f32[16384]{0:T(1024)S(1)}, f32[16384]{0:T(1024)S(1)}, f32[16384]{0:T(1024)S(1)}) fusion(f32[10,16384]{0,1:T(8,128)} %scatter_custom_fusion), kind=kLoop, calls=%fused_computation.5 | loop fusion | flops 16384 | bytes 524288 | tf_op jit(solution)/shard_map/slice | solution.py:79
  214.2 1.3 pad_maximum_fusion
  215.7 0.2 fusion.29
  215.8 0.2 fusion.41
  216.1 2.6 collective-permute-start.6
  218.8 3.2 %collective-permute-start.7 = (f32[3,16,1,128]{3,2,1,0:T(1,128)S(1)}, f32[3,16,1,128]{3,2,1,0:T(1,128)S(1)}, u32[]{:S(2)}, u32[]{:S(2)}) collective-permute-start(f32[3,16,1,128]{3,2,1,0:T(1,128)S(1)} %get-tuple-element.52), channel_id=1, source_target_pairs={{32,0},{64,32},{96,64},{128,96},{160,128},{192,160},{224,192},{256... | collective-permute-start | bytes 73736 | tf_op jit(solution)/shard_map/ppermute | solution.py:24
  222.0 3.7 %collective-permute-done.7 = f32[3,16,1,128]{3,2,1,0:T(1,128)S(1)} collective-permute-done((f32[3,16,1,128]{3,2,1,0:T(1,128)S(1)}, f32[3,16,1,128]{3,2,1,0:T(1,128)S(1)}, u32[]{:S(2)}, u32[]{:S(2)}) %collective-permute-start.7) | collective-permute-done | bytes 24608 | tf_op jit(solution)/shard_map/ppermute | solution.py:24
  225.8 0.2 fusion.45
  225.9 1.9 collective-permute-start.8
  227.9 7.8 %collective-permute-start.9 = (f32[3,16,10,1]{3,2,1,0:T(8,128)S(1)}, f32[3,16,10,1]{3,2,1,0:T(8,128)S(1)}, u32[]{:S(2)}, u32[]{:S(2)}) collective-permute-start(f32[3,16,10,1]{3,2,1,0:T(8,128)S(1)} %get-tuple-element.44), channel_id=1, source_target_pairs={{4,0},{8,4},{12,8},{16,12},{20,16},{24,20},{28,24},{5,1},{9,5},{13... | collective-permute-start | bytes 5768 | tf_op jit(solution)/shard_map/ppermute | solution.py:24
  235.7 4.7 %collective-permute-done.8 = f32[3,16,10,1]{3,2,1,0:T(8,128)S(1)} collective-permute-done((f32[3,16,10,1]{3,2,1,0:T(8,128)S(1)}, f32[3,16,10,1]{3,2,1,0:T(8,128)S(1)}, u32[]{:S(2)}, u32[]{:S(2)}) %collective-permute-start.8) | collective-permute-done | bytes 1952 | tf_op jit(solution)/shard_map/ppermute | solution.py:22
  240.4 1.2 collective-permute-done.9
  241.7 1.9 collective-permute-start.10
  243.7 3.9 %collective-permute-start.11 = (f32[3,1,10,130]{3,2,1,0:T(8,128)S(1)}, f32[3,1,10,130]{3,2,1,0:T(8,128)S(1)}, u32[]{:S(2)}, u32[]{:S(2)}) collective-permute-start(f32[3,1,10,130]{3,2,1,0:T(8,128)S(1)} %get-tuple-element.35), channel_id=1, source_target_pairs={{1,0},{2,1},{3,2},{5,4},{6,5},{7,6},{9,8},{10,9},{11,10},{13,12},{... | collective-permute-start | bytes 46808 | tf_op jit(solution)/shard_map/ppermute | solution.py:24
  247.7 1.4 collective-permute-done.11
  249.0 0.6 pad_maximum_fusion.2
  249.7 0.2 add_bitcast_fusion
  249.9 1.8 copy.38
  251.8 0.8 reshape.72
  252.5 7.4 %all_to_all.33 = f32[4,1,16384]{2,1,0:T(1,128)S(1)} all-to-all(f32[4,1,16384]{2,1,0:T(1,128)S(1)} %reshape.72), channel_id=1, replica_groups=mesh['gx'=16,'gy'=8,'gz'=4] {'gz'}, dimensions={0} | all-to-all | bytes 524288 | tf_op jit(solution)/shard_map/all_to_all | solution.py:172
  260.0 0.5 broadcast.169
  260.5 1.4 reduce.8
  261.9 0.7 reshape.73
  262.5 1.4 copy.39
  265.8 0.2 reshape.74
  266.0 6.5 %all_to_all.34 = f32[4,1,4096]{2,1,0:T(1,128)S(1)} all-to-all(f32[4,1,4096]{2,1,0:T(1,128)S(1)} %reshape.74), channel_id=1, replica_groups=mesh['gx'=16,'gy'=8,'gz'=4] {'gz'}, dimensions={0} | all-to-all | bytes 131072 | tf_op jit(solution)/shard_map/all_to_all | solution.py:176
  272.4 0.8 reduce.9
  273.4 0.2 copy.42
  273.6 0.2 all_to_all.30
  273.8 2.0 collective-permute-start.12
  275.8 5.0 %collective-permute-start.13 = (f32[16,1,128]{2,1,0:T(1,128)S(1)}, f32[16,1,128]{2,1,0:T(1,128)S(1)}, u32[]{:S(2)}, u32[]{:S(2)}) collective-permute-start(f32[16,1,128]{2,1,0:T(1,128)S(1)} %get-tuple-element.60), channel_id=1, source_target_pairs={{0,32},{32,64},{64,96},{96,128},{128,160},{160,192},{192,224},{224... | collective-permute-start | bytes 24584 | tf_op jit(solution)/shard_map/ppermute | solution.py:22
  280.8 1.3 collective-permute-done.13
  282.3 8.0 %collective-permute-start.14 = (f32[16,10,1]{2,1,0:T(8,128)S(1)}, f32[16,10,1]{2,1,0:T(8,128)S(1)}, u32[]{:S(2)}, u32[]{:S(2)}) collective-permute-start(f32[16,10,1]{2,1,0:T(8,128)S(1)} %get-tuple-element.54), channel_id=1, source_target_pairs={{4,0},{8,4},{12,8},{16,12},{20,16},{24,20},{28,24},{5,1},{9,5},{13... | collective-permute-start | bytes 1928 | tf_op jit(solution)/shard_map/ppermute | solution.py:24
  290.3 1.9 collective-permute-start.15
  292.2 0.6 collective-permute-done.14
  292.8 8.0 %collective-permute-done.15 = f32[16,10,1]{2,1,0:T(8,128)S(1)} collective-permute-done((f32[16,10,1]{2,1,0:T(8,128)S(1)}, f32[16,10,1]{2,1,0:T(8,128)S(1)}, u32[]{:S(2)}, u32[]{:S(2)}) %collective-permute-start.15) | collective-permute-done | bytes 672 | tf_op jit(solution)/shard_map/ppermute | solution.py:22
  300.9 1.9 collective-permute-start.16
  302.8 2.4 collective-permute-start.17
  305.2 0.2 fusion.17
  305.4 2.5 collective-permute-done.17
  308.0 0.7 fusion.3
  (78 shorter events, 2.8 us)
Async XLA Ops:
  0.6 6.5 %copy-start.5 = (f32[6]{0:T(128)S(1)}, f32[6]{0:T(128)}, u32[]{:S(2)}) copy-start(f32[6]{0:T(128)} %constant.31.clone) | copy-start | bytes 76
  0.6 6.5 %copy-start.1 = (f32[6,24576]{1,0:T(8,128)S(1)}, f32[6,24576]{1,0:T(8,128)}, u32[]{:S(2)}) copy-start(f32[6,24576]{1,0:T(8,128)} %param.11) | copy-start | bytes 1769476
  0.7 6.5 %copy-start.3 = (f32[24576]{0:T(1024)S(1)}, f32[24576]{0:T(1024)}, u32[]{:S(2)}) copy-start(f32[24576]{0:T(1024)} %param.12) | copy-start | bytes 294916
  149.3 5.3 %copy-start = (f32[16,8,128]{2,1,0:T(8,128)S(1)}, f32[16,8,128]{2,1,0:T(8,128)}, u32[]{:S(2)}) copy-start(f32[16,8,128]{2,1,0:T(8,128)} %param.20) | copy-start | bytes 196612
  154.7 7.0 %collective-permute-start = (f32[7,16,1,128]{3,2,1,0:T(1,128)S(1)}, f32[7,16,1,128]{3,2,1,0:T(1,128)S(1)}, u32[]{:S(2)}, u32[]{:S(2)}) collective-permute-start(f32[7,16,1,128]{3,2,1,0:T(1,128)S(1)} %get-tuple-element.41), channel_id=1, source_target_pairs={{0,32},{32,64},{64,96},{96,128},{128,160},{160,192},{192,224},{224... | collective-permute-start | bytes 172040 | tf_op jit(solution)/shard_map/ppermute | solution.py:22
  159.7 7.3 %collective-permute-start.1 = (f32[7,16,1,128]{3,2,1,0:T(1,128)S(1)}, f32[7,16,1,128]{3,2,1,0:T(1,128)S(1)}, u32[]{:S(2)}, u32[]{:S(2)}) collective-permute-start(f32[7,16,1,128]{3,2,1,0:T(1,128)S(1)} %get-tuple-element.42), channel_id=1, source_target_pairs={{32,0},{64,32},{96,64},{128,96},{160,128},{192,160},{224,192},{256... | collective-permute-start | bytes 172040 | tf_op jit(solution)/shard_map/ppermute | solution.py:24
  168.0 10.0 %collective-permute-start.2 = (f32[7,16,10,1]{1,3,2,0:T(1,128)S(1)}, f32[7,16,10,1]{1,3,2,0:T(1,128)S(1)}, u32[]{:S(2)}, u32[]{:S(2)}) collective-permute-start(f32[7,16,10,1]{1,3,2,0:T(1,128)S(1)} %copy.34), channel_id=1, source_target_pairs={{0,4},{4,8},{8,12},{12,16},{16,20},{20,24},{24,28},{1,5},{5,9},{9,... | collective-permute-start | bytes 13448 | tf_op jit(solution)/shard_map/ppermute | solution.py:22
  172.0 7.6 %collective-permute-start.3 = (f32[7,16,10,1]{1,3,2,0:T(1,128)S(1)}, f32[7,16,10,1]{1,3,2,0:T(1,128)S(1)}, u32[]{:S(2)}, u32[]{:S(2)}) collective-permute-start(f32[7,16,10,1]{1,3,2,0:T(1,128)S(1)} %copy.35), channel_id=1, source_target_pairs={{4,0},{8,4},{12,8},{16,12},{20,16},{24,20},{28,24},{5,1},{9,5},{13... | collective-permute-start | bytes 13448 | tf_op jit(solution)/shard_map/ppermute | solution.py:24
  180.3 33.9 %collective-permute-start.4 = (f32[7,1,10,130]{3,2,1,0:T(8,128)S(1)}, f32[7,1,10,130]{3,2,1,0:T(8,128)S(1)}, u32[]{:S(2)}, u32[]{:S(2)}) collective-permute-start(f32[7,1,10,130]{3,2,1,0:T(8,128)S(1)} %get-tuple-element.22), channel_id=1, source_target_pairs={{0,1},{1,2},{2,3},{4,5},{5,6},{6,7},{8,9},{9,10},{10,11},{12,13},{... | collective-permute-start | bytes 109208 | tf_op jit(solution)/shard_map/ppermute | solution.py:22
  182.2 32.0 %collective-permute-start.5 = (f32[7,1,10,130]{3,2,1,0:T(8,128)S(1)}, f32[7,1,10,130]{3,2,1,0:T(8,128)S(1)}, u32[]{:S(2)}, u32[]{:S(2)}) collective-permute-start(f32[7,1,10,130]{3,2,1,0:T(8,128)S(1)} %get-tuple-element.23), channel_id=1, source_target_pairs={{1,0},{2,1},{3,2},{5,4},{6,5},{7,6},{9,8},{10,9},{11,10},{13,12},{... | collective-permute-start | bytes 109208 | tf_op jit(solution)/shard_map/ppermute | solution.py:24
  216.1 5.9 %collective-permute-start.6 = (f32[3,16,1,128]{3,2,1,0:T(1,128)S(1)}, f32[3,16,1,128]{3,2,1,0:T(1,128)S(1)}, u32[]{:S(2)}, u32[]{:S(2)}) collective-permute-start(f32[3,16,1,128]{3,2,1,0:T(1,128)S(1)} %get-tuple-element.51), channel_id=1, source_target_pairs={{0,32},{32,64},{64,96},{96,128},{128,160},{160,192},{192,224},{224... | collective-permute-start | bytes 73736 | tf_op jit(solution)/shard_map/ppermute | solution.py:22
  218.8 6.9 %collective-permute-start.7 = (f32[3,16,1,128]{3,2,1,0:T(1,128)S(1)}, f32[3,16,1,128]{3,2,1,0:T(1,128)S(1)}, u32[]{:S(2)}, u32[]{:S(2)}) collective-permute-start(f32[3,16,1,128]{3,2,1,0:T(1,128)S(1)} %get-tuple-element.52), channel_id=1, source_target_pairs={{32,0},{64,32},{96,64},{128,96},{160,128},{192,160},{224,192},{256... | collective-permute-start | bytes 73736 | tf_op jit(solution)/shard_map/ppermute | solution.py:24
  225.9 14.5 %collective-permute-start.8 = (f32[3,16,10,1]{3,2,1,0:T(8,128)S(1)}, f32[3,16,10,1]{3,2,1,0:T(8,128)S(1)}, u32[]{:S(2)}, u32[]{:S(2)}) collective-permute-start(f32[3,16,10,1]{3,2,1,0:T(8,128)S(1)} %get-tuple-element.43), channel_id=1, source_target_pairs={{0,4},{4,8},{8,12},{12,16},{16,20},{20,24},{24,28},{1,5},{5,9},{9,... | collective-permute-start | bytes 5768 | tf_op jit(solution)/shard_map/ppermute | solution.py:22
  227.9 13.7 %collective-permute-start.9 = (f32[3,16,10,1]{3,2,1,0:T(8,128)S(1)}, f32[3,16,10,1]{3,2,1,0:T(8,128)S(1)}, u32[]{:S(2)}, u32[]{:S(2)}) collective-permute-start(f32[3,16,10,1]{3,2,1,0:T(8,128)S(1)} %get-tuple-element.44), channel_id=1, source_target_pairs={{4,0},{8,4},{12,8},{16,12},{20,16},{24,20},{28,24},{5,1},{9,5},{13... | collective-permute-start | bytes 5768 | tf_op jit(solution)/shard_map/ppermute | solution.py:24
  241.7 5.9 %collective-permute-start.10 = (f32[3,1,10,130]{3,2,1,0:T(8,128)S(1)}, f32[3,1,10,130]{3,2,1,0:T(8,128)S(1)}, u32[]{:S(2)}, u32[]{:S(2)}) collective-permute-start(f32[3,1,10,130]{3,2,1,0:T(8,128)S(1)} %get-tuple-element.34), channel_id=1, source_target_pairs={{0,1},{1,2},{2,3},{4,5},{5,6},{6,7},{8,9},{9,10},{10,11},{12,13},{... | collective-permute-start | bytes 46808 | tf_op jit(solution)/shard_map/ppermute | solution.py:22
  243.7 5.4 %collective-permute-start.11 = (f32[3,1,10,130]{3,2,1,0:T(8,128)S(1)}, f32[3,1,10,130]{3,2,1,0:T(8,128)S(1)}, u32[]{:S(2)}, u32[]{:S(2)}) collective-permute-start(f32[3,1,10,130]{3,2,1,0:T(8,128)S(1)} %get-tuple-element.35), channel_id=1, source_target_pairs={{1,0},{2,1},{3,2},{5,4},{6,5},{7,6},{9,8},{10,9},{11,10},{13,12},{... | collective-permute-start | bytes 46808 | tf_op jit(solution)/shard_map/ppermute | solution.py:24
  247.6 2.1 copy-start.4
  273.7 35.0 %copy-start.2 = (f32[16,8,128]{2,1,0:T(8,128)}, f32[16,8,128]{2,1,0:T(8,128)S(1)}, u32[]{:S(2)}) copy-start(f32[16,8,128]{2,1,0:T(8,128)S(1)} %all_to_all.30) | copy-start | bytes 196612
  273.8 7.1 %collective-permute-start.12 = (f32[16,1,128]{2,1,0:T(1,128)S(1)}, f32[16,1,128]{2,1,0:T(1,128)S(1)}, u32[]{:S(2)}, u32[]{:S(2)}) collective-permute-start(f32[16,1,128]{2,1,0:T(1,128)S(1)} %get-tuple-element.61), channel_id=1, source_target_pairs={{32,0},{64,32},{96,64},{128,96},{160,128},{192,160},{224,192},{256... | collective-permute-start | bytes 24584 | tf_op jit(solution)/shard_map/ppermute | solution.py:24
  275.8 6.4 %collective-permute-start.13 = (f32[16,1,128]{2,1,0:T(1,128)S(1)}, f32[16,1,128]{2,1,0:T(1,128)S(1)}, u32[]{:S(2)}, u32[]{:S(2)}) collective-permute-start(f32[16,1,128]{2,1,0:T(1,128)S(1)} %get-tuple-element.60), channel_id=1, source_target_pairs={{0,32},{32,64},{64,96},{96,128},{128,160},{160,192},{192,224},{224... | collective-permute-start | bytes 24584 | tf_op jit(solution)/shard_map/ppermute | solution.py:22
  282.3 10.5 %collective-permute-start.14 = (f32[16,10,1]{2,1,0:T(8,128)S(1)}, f32[16,10,1]{2,1,0:T(8,128)S(1)}, u32[]{:S(2)}, u32[]{:S(2)}) collective-permute-start(f32[16,10,1]{2,1,0:T(8,128)S(1)} %get-tuple-element.54), channel_id=1, source_target_pairs={{4,0},{8,4},{12,8},{16,12},{20,16},{24,20},{28,24},{5,1},{9,5},{13... | collective-permute-start | bytes 1928 | tf_op jit(solution)/shard_map/ppermute | solution.py:24
  290.3 10.5 %collective-permute-start.15 = (f32[16,10,1]{2,1,0:T(8,128)S(1)}, f32[16,10,1]{2,1,0:T(8,128)S(1)}, u32[]{:S(2)}, u32[]{:S(2)}) collective-permute-start(f32[16,10,1]{2,1,0:T(8,128)S(1)} %get-tuple-element.53), channel_id=1, source_target_pairs={{0,4},{4,8},{8,12},{12,16},{16,20},{20,24},{24,28},{1,5},{5,9},{9,... | collective-permute-start | bytes 1928 | tf_op jit(solution)/shard_map/ppermute | solution.py:22
  300.9 4.5 %collective-permute-start.16 = (f32[1,10,130]{2,1,0:T(8,128)S(1)}, f32[1,10,130]{2,1,0:T(8,128)S(1)}, u32[]{:S(2)}, u32[]{:S(2)}) collective-permute-start(f32[1,10,130]{2,1,0:T(8,128)S(1)} %get-tuple-element.47), channel_id=1, source_target_pairs={{1,0},{2,1},{3,2},{5,4},{6,5},{7,6},{9,8},{10,9},{11,10},{13,12},{... | collective-permute-start | bytes 15608 | tf_op jit(solution)/shard_map/ppermute | solution.py:24
  302.8 5.1 %collective-permute-start.17 = (f32[1,10,130]{2,1,0:T(8,128)S(1)}, f32[1,10,130]{2,1,0:T(8,128)S(1)}, u32[]{:S(2)}, u32[]{:S(2)}) collective-permute-start(f32[1,10,130]{2,1,0:T(8,128)S(1)} %get-tuple-element.48), channel_id=1, source_target_pairs={{0,1},{1,2},{2,3},{4,5},{5,6},{6,7},{8,9},{9,10},{10,11},{12,13},{... | collective-permute-start | bytes 15608 | tf_op jit(solution)/shard_map/ppermute | solution.py:22
where the time goes:
time: 310 us; the launch traced here: 309 us
  other arithmetic  176 us (57%)
  starting transfers between devices  64.8 us (21%)
  waiting for transfers between devices  29.7 us (10%)
  local copies, waits for them, and re-layouts  22.1 us (7%)
  blocking collectives  13.9 us (4%)
    scatter-add x1, other arithmetic, point_sums(): jax.ops.segment_sum(component, cell_index, num_segments=segments)  135 us
    ppermute x9, starting transfers between devices, padded_2(): lax.ppermute(head, axis, [((i + 1) % count, i) for i in range(ends)])  38.6 us
    slice x1, other arithmetic, brick_velocity(): cell_sums[6] + time_step * force_x  28.1 us
    ppermute x9, starting transfers between devices, padded_2(): lax.ppermute(tail, axis, [(i, (i + 1) % count) for i in range(ends)])  26.3 us
    ppermute x9, waiting for transfers between devices, padded_2(): lax.ppermute(tail, axis, [(i, (i + 1) % count) for i in range(ends)])  16.5 us
    ppermute x9, waiting for transfers between devices, padded_2(): lax.ppermute(head, axis, [((i + 1) % count, i) for i in range(ends)])  13.2 us
    all_to_all x1, blocking collectives, shards(): lax.all_to_all(jnp.stack(band_set), 'gz', split_axis=3, concat_axis=1, ti...  7.43 us
    concatenate x1, local copies, waits for them, and re-layouts, point_sums(): jnp.concatenate([stress * weight, point_velocity * weight, weight[None]],...  6.96 us
  transfers between devices with their start and end apart: 18, of which 10 were waited for; matrix products, arithmetic and copies ran while one was open for 10% of the time, Pallas kernels for 0%

commit v1 on v0

--- a/solution.py
+++ b/solution.py
@@ -9,6 +9,93 @@
 critical_slope = 1.2
 mass_floor = 0.5
 shear_floor = 1.0
+
+from jax.experimental import pallas as pl
+from jax.experimental.pallas import tpu as pltpu
+
+CHUNK = 1024
+M_ROWS = 32
+N_COLS = 512
+
+
+def _split3(v):
+    hi = v.astype(jnp.bfloat16)
+    rest = v - hi.astype(jnp.float32)
+    mid = rest.astype(jnp.bfloat16)
+    lo = (rest - mid.astype(jnp.float32)).astype(jnp.bfloat16)
+    return [hi, mid, lo]
+
+
+def sums_kernel(count_ref, st_ref, ms_ref, cons_ref, vel_ref, w_ref, cell_ref, yf_ref, out_ref, acc_ref):
+    count = count_ref[0, 0]
+    acc_ref[...] = jnp.zeros_like(acc_ref)
+    chunks = st_ref.shape[1] // CHUNK
+
+    def body(k, carry):
+        start = pl.multiple_of(k * CHUNK, CHUNK)
+        span = pl.ds(start, CHUNK)
+        st = [st_ref[pl.ds(i, 1), span] for i in range(6)]
+        ms = ms_ref[:, span]
+        cons = cons_ref[:, span]
+        yf = yf_ref[:, span]
+        slot = start + lax.broadcasted_iota(jnp.int32, (1, CHUNK), 1)
+        weight = jnp.where(slot < count, w_ref[:, span], 0.0)
+        sq_normal = st[0] * st[0] + st[1] * st[1] + st[2] * st[2]
+        sq_shear = st[3] * st[3] + st[4] * st[4] + st[5] * st[5]
+        shear_size = jnp.sqrt(1.5 * (sq_normal + 2.0 * sq_shear))
+        yield_size = critical_slope * jnp.sqrt(ms * (cons - ms))
+        factor = jnp.where(yf == 1, yield_size / jnp.maximum(shear_size, shear_floor), 1.0)
+        stress = [st[i] * factor - ms if i < 3 else st[i] * factor for i in range(6)]
+        values = [s * weight for s in stress]
+        values += [vel_ref[pl.ds(i, 1), span] * weight for i in range(3)]
+        values.append(weight)
+        cell = cell_ref[:, span]
+        m_key = (cell >> 12) * 8 + ((cell >> 7) & 7)
+        n_key = ((cell >> 10) & 3) * 128 + (cell & 127)
+        m_mask = lax.broadcasted_iota(jnp.int32, (M_ROWS, CHUNK), 0) == m_key
+        zero = jnp.zeros((M_ROWS, CHUNK), jnp.bfloat16)
+        pieces = []
+        for v in values:
+            for part in _split3(v):
+                pieces.append(jnp.where(m_mask, jnp.broadcast_to(part, (M_ROWS, CHUNK)), zero))
+        lhs = jnp.concatenate(pieces, axis=0)
+        one_hot = jnp.where(
+            lax.broadcasted_iota(jnp.int32, (N_COLS, CHUNK), 0) == n_key, 1.0, 0.0
+        ).astype(jnp.bfloat16)
+        acc_ref[...] += lax.dot_general(
+            lhs, one_hot, (((1,), (1,)), ((), ())), preferred_element_type=jnp.float32
+        )
+        return carry
+
+    lax.fori_loop(0, chunks, body, 0)
+    for comp in range(10):
+        for level in range(16):
+            rows = pl.ds((comp * 3) * M_ROWS + (level >> 2) * 8, 8)
+            lanes = pl.ds((level & 3) * 128, 128)
+            total = acc_ref[rows, lanes]
+            for s in (1, 2):
+                total = total + acc_ref[pl.ds((comp * 3 + s) * M_ROWS + (level >> 2) * 8, 8), lanes]
+            out_ref[comp, level] = total
+
+
+def cell_sums_of(stress_trial, mean_stress, consolidation, point_velocity, point_weight, point_cell, yield_flag, point_count, levels, extent, breadth):
+    n = mean_stress.shape[0]
+    row = lambda a: a.reshape(1, n)
+    vmem = pl.BlockSpec(memory_space=pltpu.VMEM)
+    return pl.pallas_call(
+        sums_kernel,
+        out_shape=jax.ShapeDtypeStruct((10, levels, extent, breadth), jnp.float32),
+        in_specs=[pl.BlockSpec(memory_space=pltpu.SMEM)] + [vmem] * 7,
+        out_specs=vmem,
+        scratch_shapes=[pltpu.VMEM((30 * M_ROWS, N_COLS), jnp.float32)],
+        cost_estimate=pl.CostEstimate(
+            flops=2 * 30 * M_ROWS * N_COLS * n, bytes_accessed=13 * 4 * n + 10 * 4 * levels * extent * breadth,
+            transcendentals=3 * n,
+        ),
+    )(
+        point_count.reshape(1, 1), stress_trial, row(mean_stress), row(consolidation), point_velocity,
+        row(point_weight), row(point_cell), row(yield_flag),
+    )
 
 
 def padded_2(cells, sides, width):
@@ -156,12 +243,10 @@
     permeability,
 ):
     levels, extent, breadth = porosity.shape
-    slot_index = jnp.arange(mean_stress.shape[0], dtype=jnp.int32)
-    weight = jnp.where(slot_index < point_count[0, 0, 0], point_weight, 0.0)
-    stress = returned_stress(stress_trial, mean_stress, consolidation, yield_flag)
-    cell_sums = point_sums(
-        stress, point_velocity, weight, point_cell, levels * extent * breadth
-    ).reshape(10, levels, extent, breadth)
+    cell_sums = cell_sums_of(
+        stress_trial, mean_stress, consolidation, point_velocity, point_weight, point_cell,
+        yield_flag, point_count, levels, extent, breadth,
+    )
     outgoing = jnp.concatenate([cell_sums[:6], permeability[None]], axis=0)
     padded = padded_2(outgoing, (("gx", 2), ("gy", 3), ("gz", 1)), 1)
     velocity = brick_velocity(cell_sums, padded)

time: 310 us -> 165 us (0.53)
  the two profiles are of different devices: /device:TPU:102 before, /device:TPU:134 now
where the time goes in v1:
time: 165 us; the launch traced here: 164 us
  starting transfers between devices  66.8 us (40%)
  Pallas kernels  32.2 us (20%)
  waiting for transfers between devices  30.7 us (19%)
  blocking collectives  13.9 us (8%)
  local copies, waits for them, and re-layouts  11.7 us (7%)
  other arithmetic  7.05 us (4%)
  between operations  2 us (1%)
    ppermute x9, starting transfers between devices, padded_2(): lax.ppermute(head, axis, [((i + 1) % count, i) for i in range(ends)])  41.9 us
    pallas_call x1, Pallas kernels, cell_sums_of(): pl.pallas_call(sums_kernel, out_shape=jax.ShapeDtypeStruct((10, levels, e...  32.2 us
    ppermute x9, starting transfers between devices, padded_2(): lax.ppermute(tail, axis, [(i, (i + 1) % count) for i in range(ends)])  24.9 us
    ppermute x9, waiting for transfers between devices, padded_2(): lax.ppermute(tail, axis, [(i, (i + 1) % count) for i in range(ends)])  18.1 us
    ppermute x9, waiting for transfers between devices, padded_2(): lax.ppermute(head, axis, [((i + 1) % count, i) for i in range(ends)])  12.6 us
    all_to_all x1, blocking collectives, shards(): lax.all_to_all(jnp.stack(band_set), 'gz', split_axis=3, concat_axis=1, ti...  7.43 us
    all_to_all x1, blocking collectives, shards(): lax.all_to_all(solved.reshape(height, extent, -1), 'gz', split_axis=0, co...  6.46 us
  transfers between devices with their start and end apart: 18, of which 13 were waited for; matrix products, arithmetic and copies ran while one was open for 1% of the time, Pallas kernels for 0%

profile of v1, /device:TPU:134, one launch (start us, length us, event | category | flops | bytes accessed | tf_op | source)
XLA Modules:
  0.0 164.4 jit_solution(10391687383399916726)
XLA Ops:
  1.3 32.2 %shard_map.113 = f32[10,16,8,128]{3,2,1,0:T(8,128)} custom-call(s32[1,1]{1,0:T(1,128)} %bitcast.91.count_ref, f32[6,24576]{1,0:T(8,128)} %st_ref.1, f32[1,24576]{1,0:T(1,128)} %bitcast.103, f32[1,24576]{1,0:T(1,128)} %bitcast.104, f32[3,24576]{1,0:T(4,128)} %vel_ref.1, f32[1,24576]{1,0:T(1,128)} %bitcast.105, s32[1,24576]{1,0:T(1,128)} %bitcast.106, ...), custom_call_target="tpu_custom_call" | custom-call | flops 24159191040 | bytes 1933312 | tf_op jit(solution)/shard_map/pallas_call | solution.py:85
  33.5 1.0 slice.472
  34.6 3.8 %collective-permute-start = (f32[7,16,1,128]{3,2,1,0:T(1,128)S(1)}, f32[7,16,1,128]{3,2,1,0:T(1,128)S(1)}, u32[]{:S(2)}, u32[]{:S(2)}) collective-permute-start(f32[7,16,1,128]{3,2,1,0:T(1,128)S(1)} %get-tuple-element.39), channel_id=1, source_target_pairs={{0,32},{32,64},{64,96},{96,128},{128,160},{160,192},{192,224},{224... | collective-permute-start | bytes 172040 | tf_op jit(solution)/shard_map/ppermute | solution.py:109
  38.5 3.2 %collective-permute-start.1 = (f32[7,16,1,128]{3,2,1,0:T(1,128)S(1)}, f32[7,16,1,128]{3,2,1,0:T(1,128)S(1)}, u32[]{:S(2)}, u32[]{:S(2)}) collective-permute-start(f32[7,16,1,128]{3,2,1,0:T(1,128)S(1)} %get-tuple-element.40), channel_id=1, source_target_pairs={{32,0},{64,32},{96,64},{128,96},{160,128},{192,160},{224,192},{256... | collective-permute-start | bytes 172040 | tf_op jit(solution)/shard_map/ppermute | solution.py:111
  41.7 0.2 collective-permute-done
  41.9 2.6 %collective-permute-done.1 = f32[7,16,1,128]{3,2,1,0:T(1,128)S(1)} collective-permute-done((f32[7,16,1,128]{3,2,1,0:T(1,128)S(1)}, f32[7,16,1,128]{3,2,1,0:T(1,128)S(1)}, u32[]{:S(2)}, u32[]{:S(2)}) %collective-permute-start.1) | collective-permute-done | bytes 57376 | tf_op jit(solution)/shard_map/ppermute | solution.py:111
  44.5 0.2 pad_maximum_fusion.1
  44.7 0.3 fusion.37
  45.0 0.5 copy.25
  45.5 3.5 %collective-permute-start.2 = (f32[7,16,10,1]{1,3,2,0:T(1,128)S(1)}, f32[7,16,10,1]{1,3,2,0:T(1,128)S(1)}, u32[]{:S(2)}, u32[]{:S(2)}) collective-permute-start(f32[7,16,10,1]{1,3,2,0:T(1,128)S(1)} %copy.25), channel_id=1, source_target_pairs={{0,4},{4,8},{8,12},{12,16},{16,20},{20,24},{24,28},{1,5},{5,9},{9,... | collective-permute-start | bytes 13448 | tf_op jit(solution)/shard_map/ppermute | solution.py:109
  49.0 0.5 copy.26
  49.5 6.0 %collective-permute-start.3 = (f32[7,16,10,1]{1,3,2,0:T(1,128)S(1)}, f32[7,16,10,1]{1,3,2,0:T(1,128)S(1)}, u32[]{:S(2)}, u32[]{:S(2)}) collective-permute-start(f32[7,16,10,1]{1,3,2,0:T(1,128)S(1)} %copy.26), channel_id=1, source_target_pairs={{4,0},{8,4},{12,8},{16,12},{20,16},{24,20},{28,24},{5,1},{9,5},{13... | collective-permute-start | bytes 13448 | tf_op jit(solution)/shard_map/ppermute | solution.py:111
  55.5 0.5 copy.27
  56.0 1.1 collective-permute-done.3
  57.1 0.5 copy.28
  57.6 0.2 pad_maximum_fusion.12
  57.9 1.9 %collective-permute-start.4 = (f32[7,1,10,130]{3,2,1,0:T(8,128)S(1)}, f32[7,1,10,130]{3,2,1,0:T(8,128)S(1)}, u32[]{:S(2)}, u32[]{:S(2)}) collective-permute-start(f32[7,1,10,130]{3,2,1,0:T(8,128)S(1)} %get-tuple-element.18), channel_id=1, source_target_pairs={{0,1},{1,2},{2,3},{4,5},{5,6},{6,7},{8,9},{9,10},{10,11},{12,13},{... | collective-permute-start | bytes 109208 | tf_op jit(solution)/shard_map/ppermute | solution.py:109
  59.8 3.6 %collective-permute-start.5 = (f32[7,1,10,130]{3,2,1,0:T(8,128)S(1)}, f32[7,1,10,130]{3,2,1,0:T(8,128)S(1)}, u32[]{:S(2)}, u32[]{:S(2)}) collective-permute-start(f32[7,1,10,130]{3,2,1,0:T(8,128)S(1)} %get-tuple-element.19), channel_id=1, source_target_pairs={{1,0},{2,1},{3,2},{5,4},{6,5},{7,6},{9,8},{10,9},{11,10},{13,12},{... | collective-permute-start | bytes 109208 | tf_op jit(solution)/shard_map/ppermute | solution.py:111
  63.4 0.5 collective-permute-done.4
  64.0 1.8 %collective-permute-done.5 = f32[7,1,10,130]{3,2,1,0:T(8,128)S(1)} collective-permute-done((f32[7,1,10,130]{3,2,1,0:T(8,128)S(1)}, f32[7,1,10,130]{3,2,1,0:T(8,128)S(1)}, u32[]{:S(2)}, u32[]{:S(2)}) %collective-permute-start.5) | collective-permute-done | bytes 36432 | tf_op jit(solution)/shard_map/ppermute | solution.py:111
  65.8 1.3 pad_maximum_fusion
  67.1 0.1 slice_bitcast_fusion.8
  67.2 0.9 copy-done.2
  68.1 0.2 fusion.21
  68.3 0.2 fusion.34
  68.6 3.8 %collective-permute-start.6 = (f32[3,16,1,128]{3,2,1,0:T(1,128)S(1)}, f32[3,16,1,128]{3,2,1,0:T(1,128)S(1)}, u32[]{:S(2)}, u32[]{:S(2)}) collective-permute-start(f32[3,16,1,128]{3,2,1,0:T(1,128)S(1)} %get-tuple-element.47), channel_id=1, source_target_pairs={{0,32},{32,64},{64,96},{96,128},{128,160},{160,192},{192,224},{224... | collective-permute-start | bytes 73736 | tf_op jit(solution)/shard_map/ppermute | solution.py:109
  72.4 3.2 %collective-permute-start.7 = (f32[3,16,1,128]{3,2,1,0:T(1,128)S(1)}, f32[3,16,1,128]{3,2,1,0:T(1,128)S(1)}, u32[]{:S(2)}, u32[]{:S(2)}) collective-permute-start(f32[3,16,1,128]{3,2,1,0:T(1,128)S(1)} %get-tuple-element.48), channel_id=1, source_target_pairs={{32,0},{64,32},{96,64},{128,96},{160,128},{192,160},{224,192},{256... | collective-permute-start | bytes 73736 | tf_op jit(solution)/shard_map/ppermute | solution.py:111
  75.7 3.5 %collective-permute-done.7 = f32[3,16,1,128]{3,2,1,0:T(1,128)S(1)} collective-permute-done((f32[3,16,1,128]{3,2,1,0:T(1,128)S(1)}, f32[3,16,1,128]{3,2,1,0:T(1,128)S(1)}, u32[]{:S(2)}, u32[]{:S(2)}) %collective-permute-start.7) | collective-permute-done | bytes 24608 | tf_op jit(solution)/shard_map/ppermute | solution.py:111
  79.2 0.2 fusion.38
  79.4 1.9 %collective-permute-start.8 = (f32[3,16,10,1]{3,2,1,0:T(8,128)S(1)}, f32[3,16,10,1]{3,2,1,0:T(8,128)S(1)}, u32[]{:S(2)}, u32[]{:S(2)}) collective-permute-start(f32[3,16,10,1]{3,2,1,0:T(8,128)S(1)} %get-tuple-element.41), channel_id=1, source_target_pairs={{0,4},{4,8},{8,12},{12,16},{16,20},{20,24},{24,28},{1,5},{5,9},{9,... | collective-permute-start | bytes 5768 | tf_op jit(solution)/shard_map/ppermute | solution.py:109
  81.4 7.8 %collective-permute-start.9 = (f32[3,16,10,1]{3,2,1,0:T(8,128)S(1)}, f32[3,16,10,1]{3,2,1,0:T(8,128)S(1)}, u32[]{:S(2)}, u32[]{:S(2)}) collective-permute-start(f32[3,16,10,1]{3,2,1,0:T(8,128)S(1)} %get-tuple-element.42), channel_id=1, source_target_pairs={{4,0},{8,4},{12,8},{16,12},{20,16},{24,20},{28,24},{5,1},{9,5},{13... | collective-permute-start | bytes 5768 | tf_op jit(solution)/shard_map/ppermute | solution.py:111
  89.2 3.8 %collective-permute-done.8 = f32[3,16,10,1]{3,2,1,0:T(8,128)S(1)} collective-permute-done((f32[3,16,10,1]{3,2,1,0:T(8,128)S(1)}, f32[3,16,10,1]{3,2,1,0:T(8,128)S(1)}, u32[]{:S(2)}, u32[]{:S(2)}) %collective-permute-start.8) | collective-permute-done | bytes 1952 | tf_op jit(solution)/shard_map/ppermute | solution.py:109
  93.0 1.5 collective-permute-done.9
  94.6 1.9 %collective-permute-start.10 = (f32[3,1,10,130]{3,2,1,0:T(8,128)S(1)}, f32[3,1,10,130]{3,2,1,0:T(8,128)S(1)}, u32[]{:S(2)}, u32[]{:S(2)}) collective-permute-start(f32[3,1,10,130]{3,2,1,0:T(8,128)S(1)} %get-tuple-element.30), channel_id=1, source_target_pairs={{0,1},{1,2},{2,3},{4,5},{5,6},{6,7},{8,9},{9,10},{10,11},{12,13},{... | collective-permute-start | bytes 46808 | tf_op jit(solution)/shard_map/ppermute | solution.py:109
  96.5 4.4 %collective-permute-start.11 = (f32[3,1,10,130]{3,2,1,0:T(8,128)S(1)}, f32[3,1,10,130]{3,2,1,0:T(8,128)S(1)}, u32[]{:S(2)}, u32[]{:S(2)}) collective-permute-start(f32[3,1,10,130]{3,2,1,0:T(8,128)S(1)} %get-tuple-element.31), channel_id=1, source_target_pairs={{1,0},{2,1},{3,2},{5,4},{6,5},{7,6},{9,8},{10,9},{11,10},{13,12},{... | collective-permute-start | bytes 46808 | tf_op jit(solution)/shard_map/ppermute | solution.py:111
  101.1 1.6 collective-permute-done.11
  102.7 0.6 pad_maximum_fusion.2
  103.3 0.2 add_bitcast_fusion
  103.6 1.8 %copy.29 = f32[4,16,8,128]{1,2,0,3:T(8,128)S(1)} copy(f32[4,16,8,128]{3,2,1,0:T(8,128)S(1)} %pad_maximum_fusion.4) | data formatting | bytes 524288 | tf_op jit(solution)/shard_map/stack | solution.py:257
  105.4 0.8 reshape.49
  106.2 7.4 %all_to_all.33 = f32[4,1,16384]{2,1,0:T(1,128)S(1)} all-to-all(f32[4,1,16384]{2,1,0:T(1,128)S(1)} %reshape.49), channel_id=1, replica_groups=mesh['gx'=16,'gy'=8,'gz'=4] {'gz'}, dimensions={0} | all-to-all | bytes 524288 | tf_op jit(solution)/shard_map/all_to_all | solution.py:257
  113.6 0.5 broadcast.155
  114.1 1.4 reduce
  115.5 0.7 reshape.50
  116.2 1.4 copy.30
  117.6 0.1 squeeze.72
  119.3 0.2 copy.32
  119.4 0.2 reshape.51
  119.6 6.5 %all_to_all.34 = f32[4,1,4096]{2,1,0:T(1,128)S(1)} all-to-all(f32[4,1,4096]{2,1,0:T(1,128)S(1)} %reshape.51), channel_id=1, replica_groups=mesh['gx'=16,'gy'=8,'gz'=4] {'gz'}, dimensions={0} | all-to-all | bytes 131072 | tf_op jit(solution)/shard_map/all_to_all | solution.py:261
  126.1 0.8 reduce.1
  127.0 0.2 copy.33
  127.2 0.2 all_to_all.30
  127.4 3.4 %collective-permute-start.12 = (f32[16,1,128]{2,1,0:T(1,128)S(1)}, f32[16,1,128]{2,1,0:T(1,128)S(1)}, u32[]{:S(2)}, u32[]{:S(2)}) collective-permute-start(f32[16,1,128]{2,1,0:T(1,128)S(1)} %get-tuple-element.57), channel_id=1, source_target_pairs={{32,0},{64,32},{96,64},{128,96},{160,128},{192,160},{224,192},{256... | collective-permute-start | bytes 24584 | tf_op jit(solution)/shard_map/ppermute | solution.py:111
  130.8 3.6 %collective-permute-start.13 = (f32[16,1,128]{2,1,0:T(1,128)S(1)}, f32[16,1,128]{2,1,0:T(1,128)S(1)}, u32[]{:S(2)}, u32[]{:S(2)}) collective-permute-start(f32[16,1,128]{2,1,0:T(1,128)S(1)} %get-tuple-element.56), channel_id=1, source_target_pairs={{0,32},{32,64},{64,96},{96,128},{128,160},{160,192},{192,224},{224... | collective-permute-start | bytes 24584 | tf_op jit(solution)/shard_map/ppermute | solution.py:109
  134.5 3.1 %collective-permute-done.13 = f32[16,1,128]{2,1,0:T(1,128)S(1)} collective-permute-done((f32[16,1,128]{2,1,0:T(1,128)S(1)}, f32[16,1,128]{2,1,0:T(1,128)S(1)}, u32[]{:S(2)}, u32[]{:S(2)}) %collective-permute-start.13) | collective-permute-done | bytes 8224 | tf_op jit(solution)/shard_map/ppermute | solution.py:109
  137.7 8.3 %collective-permute-start.14 = (f32[16,10,1]{2,1,0:T(8,128)S(1)}, f32[16,10,1]{2,1,0:T(8,128)S(1)}, u32[]{:S(2)}, u32[]{:S(2)}) collective-permute-start(f32[16,10,1]{2,1,0:T(8,128)S(1)} %get-tuple-element.50), channel_id=1, source_target_pairs={{4,0},{8,4},{12,8},{16,12},{20,16},{24,20},{28,24},{5,1},{9,5},{13... | collective-permute-start | bytes 1928 | tf_op jit(solution)/shard_map/ppermute | solution.py:111
  146.0 1.9 %collective-permute-start.15 = (f32[16,10,1]{2,1,0:T(8,128)S(1)}, f32[16,10,1]{2,1,0:T(8,128)S(1)}, u32[]{:S(2)}, u32[]{:S(2)}) collective-permute-start(f32[16,10,1]{2,1,0:T(8,128)S(1)} %get-tuple-element.49), channel_id=1, source_target_pairs={{0,4},{4,8},{8,12},{12,16},{16,20},{20,24},{24,28},{1,5},{5,9},{9,... | collective-permute-start | bytes 1928 | tf_op jit(solution)/shard_map/ppermute | solution.py:109
  148.0 0.6 collective-permute-done.14
  148.5 8.0 %collective-permute-done.15 = f32[16,10,1]{2,1,0:T(8,128)S(1)} collective-permute-done((f32[16,10,1]{2,1,0:T(8,128)S(1)}, f32[16,10,1]{2,1,0:T(8,128)S(1)}, u32[]{:S(2)}, u32[]{:S(2)}) %collective-permute-start.15) | collective-permute-done | bytes 672 | tf_op jit(solution)/shard_map/ppermute | solution.py:109
  156.6 1.9 %collective-permute-start.16 = (f32[1,10,130]{2,1,0:T(8,128)S(1)}, f32[1,10,130]{2,1,0:T(8,128)S(1)}, u32[]{:S(2)}, u32[]{:S(2)}) collective-permute-start(f32[1,10,130]{2,1,0:T(8,128)S(1)} %get-tuple-element.43), channel_id=1, source_target_pairs={{1,0},{2,1},{3,2},{5,4},{6,5},{7,6},{9,8},{10,9},{11,10},{13,12},{... | collective-permute-start | bytes 15608 | tf_op jit(solution)/shard_map/ppermute | solution.py:111
  158.5 2.4 %collective-permute-start.17 = (f32[1,10,130]{2,1,0:T(8,128)S(1)}, f32[1,10,130]{2,1,0:T(8,128)S(1)}, u32[]{:S(2)}, u32[]{:S(2)}) collective-permute-start(f32[1,10,130]{2,1,0:T(8,128)S(1)} %get-tuple-element.44), channel_id=1, source_target_pairs={{0,1},{1,2},{2,3},{4,5},{5,6},{6,7},{8,9},{9,10},{10,11},{12,13},{... | collective-permute-start | bytes 15608 | tf_op jit(solution)/shard_map/ppermute | solution.py:109
  160.9 0.2 fusion.9
  161.1 2.5 %collective-permute-done.17 = f32[1,10,130]{2,1,0:T(8,128)S(1)} collective-permute-done((f32[1,10,130]{2,1,0:T(8,128)S(1)}, f32[1,10,130]{2,1,0:T(8,128)S(1)}, u32[]{:S(2)}, u32[]{:S(2)}) %collective-permute-start.17) | collective-permute-done | bytes 5232 | tf_op jit(solution)/shard_map/ppermute | solution.py:109
  163.7 0.7 fusion
  (66 shorter events, 2.3 us)
Async XLA Ops:
  1.3 33.3 %copy-start = (f32[16,8,128]{2,1,0:T(8,128)S(1)}, f32[16,8,128]{2,1,0:T(8,128)}, u32[]{:S(2)}) copy-start(f32[16,8,128]{2,1,0:T(8,128)} %param.19) | copy-start | bytes 196612
  34.6 7.3 %collective-permute-start = (f32[7,16,1,128]{3,2,1,0:T(1,128)S(1)}, f32[7,16,1,128]{3,2,1,0:T(1,128)S(1)}, u32[]{:S(2)}, u32[]{:S(2)}) collective-permute-start(f32[7,16,1,128]{3,2,1,0:T(1,128)S(1)} %get-tuple-element.39), channel_id=1, source_target_pairs={{0,32},{32,64},{64,96},{96,128},{128,160},{160,192},{192,224},{224... | collective-permute-start | bytes 172040 | tf_op jit(solution)/shard_map/ppermute | solution.py:109
  38.5 6.1 %collective-permute-start.1 = (f32[7,16,1,128]{3,2,1,0:T(1,128)S(1)}, f32[7,16,1,128]{3,2,1,0:T(1,128)S(1)}, u32[]{:S(2)}, u32[]{:S(2)}) collective-permute-start(f32[7,16,1,128]{3,2,1,0:T(1,128)S(1)} %get-tuple-element.40), channel_id=1, source_target_pairs={{32,0},{64,32},{96,64},{128,96},{160,128},{192,160},{224,192},{256... | collective-permute-start | bytes 172040 | tf_op jit(solution)/shard_map/ppermute | solution.py:111
  45.5 10.0 %collective-permute-start.2 = (f32[7,16,10,1]{1,3,2,0:T(1,128)S(1)}, f32[7,16,10,1]{1,3,2,0:T(1,128)S(1)}, u32[]{:S(2)}, u32[]{:S(2)}) collective-permute-start(f32[7,16,10,1]{1,3,2,0:T(1,128)S(1)} %copy.25), channel_id=1, source_target_pairs={{0,4},{4,8},{8,12},{12,16},{16,20},{20,24},{24,28},{1,5},{5,9},{9,... | collective-permute-start | bytes 13448 | tf_op jit(solution)/shard_map/ppermute | solution.py:109
  49.5 7.6 %collective-permute-start.3 = (f32[7,16,10,1]{1,3,2,0:T(1,128)S(1)}, f32[7,16,10,1]{1,3,2,0:T(1,128)S(1)}, u32[]{:S(2)}, u32[]{:S(2)}) collective-permute-start(f32[7,16,10,1]{1,3,2,0:T(1,128)S(1)} %copy.26), channel_id=1, source_target_pairs={{4,0},{8,4},{12,8},{16,12},{20,16},{24,20},{28,24},{5,1},{9,5},{13... | collective-permute-start | bytes 13448 | tf_op jit(solution)/shard_map/ppermute | solution.py:111
  57.9 6.1 %collective-permute-start.4 = (f32[7,1,10,130]{3,2,1,0:T(8,128)S(1)}, f32[7,1,10,130]{3,2,1,0:T(8,128)S(1)}, u32[]{:S(2)}, u32[]{:S(2)}) collective-permute-start(f32[7,1,10,130]{3,2,1,0:T(8,128)S(1)} %get-tuple-element.18), channel_id=1, source_target_pairs={{0,1},{1,2},{2,3},{4,5},{5,6},{6,7},{8,9},{9,10},{10,11},{12,13},{... | collective-permute-start | bytes 109208 | tf_op jit(solution)/shard_map/ppermute | solution.py:109
  59.8 6.0 %collective-permute-start.5 = (f32[7,1,10,130]{3,2,1,0:T(8,128)S(1)}, f32[7,1,10,130]{3,2,1,0:T(8,128)S(1)}, u32[]{:S(2)}, u32[]{:S(2)}) collective-permute-start(f32[7,1,10,130]{3,2,1,0:T(8,128)S(1)} %get-tuple-element.19), channel_id=1, source_target_pairs={{1,0},{2,1},{3,2},{5,4},{6,5},{7,6},{9,8},{10,9},{11,10},{13,12},{... | collective-permute-start | bytes 109208 | tf_op jit(solution)/shard_map/ppermute | solution.py:111
  67.0 1.1 copy-start.2
  68.6 7.1 %collective-permute-start.6 = (f32[3,16,1,128]{3,2,1,0:T(1,128)S(1)}, f32[3,16,1,128]{3,2,1,0:T(1,128)S(1)}, u32[]{:S(2)}, u32[]{:S(2)}) collective-permute-start(f32[3,16,1,128]{3,2,1,0:T(1,128)S(1)} %get-tuple-element.47), channel_id=1, source_target_pairs={{0,32},{32,64},{64,96},{96,128},{128,160},{160,192},{192,224},{224... | collective-permute-start | bytes 73736 | tf_op jit(solution)/shard_map/ppermute | solution.py:109
  72.4 6.7 %collective-permute-start.7 = (f32[3,16,1,128]{3,2,1,0:T(1,128)S(1)}, f32[3,16,1,128]{3,2,1,0:T(1,128)S(1)}, u32[]{:S(2)}, u32[]{:S(2)}) collective-permute-start(f32[3,16,1,128]{3,2,1,0:T(1,128)S(1)} %get-tuple-element.48), channel_id=1, source_target_pairs={{32,0},{64,32},{96,64},{128,96},{160,128},{192,160},{224,192},{256... | collective-permute-start | bytes 73736 | tf_op jit(solution)/shard_map/ppermute | solution.py:111
  79.4 13.6 %collective-permute-start.8 = (f32[3,16,10,1]{3,2,1,0:T(8,128)S(1)}, f32[3,16,10,1]{3,2,1,0:T(8,128)S(1)}, u32[]{:S(2)}, u32[]{:S(2)}) collective-permute-start(f32[3,16,10,1]{3,2,1,0:T(8,128)S(1)} %get-tuple-element.41), channel_id=1, source_target_pairs={{0,4},{4,8},{8,12},{12,16},{16,20},{20,24},{24,28},{1,5},{5,9},{9,... | collective-permute-start | bytes 5768 | tf_op jit(solution)/shard_map/ppermute | solution.py:109
  81.4 13.1 %collective-permute-start.9 = (f32[3,16,10,1]{3,2,1,0:T(8,128)S(1)}, f32[3,16,10,1]{3,2,1,0:T(8,128)S(1)}, u32[]{:S(2)}, u32[]{:S(2)}) collective-permute-start(f32[3,16,10,1]{3,2,1,0:T(8,128)S(1)} %get-tuple-element.42), channel_id=1, source_target_pairs={{4,0},{8,4},{12,8},{16,12},{20,16},{24,20},{28,24},{5,1},{9,5},{13... | collective-permute-start | bytes 5768 | tf_op jit(solution)/shard_map/ppermute | solution.py:111
  94.6 6.4 %collective-permute-start.10 = (f32[3,1,10,130]{3,2,1,0:T(8,128)S(1)}, f32[3,1,10,130]{3,2,1,0:T(8,128)S(1)}, u32[]{:S(2)}, u32[]{:S(2)}) collective-permute-start(f32[3,1,10,130]{3,2,1,0:T(8,128)S(1)} %get-tuple-element.30), channel_id=1, source_target_pairs={{0,1},{1,2},{2,3},{4,5},{5,6},{6,7},{8,9},{9,10},{10,11},{12,13},{... | collective-permute-start | bytes 46808 | tf_op jit(solution)/shard_map/ppermute | solution.py:109
  96.5 6.1 %collective-permute-start.11 = (f32[3,1,10,130]{3,2,1,0:T(8,128)S(1)}, f32[3,1,10,130]{3,2,1,0:T(8,128)S(1)}, u32[]{:S(2)}, u32[]{:S(2)}) collective-permute-start(f32[3,1,10,130]{3,2,1,0:T(8,128)S(1)} %get-tuple-element.31), channel_id=1, source_target_pairs={{1,0},{2,1},{3,2},{5,4},{6,5},{7,6},{9,8},{10,9},{11,10},{13,12},{... | collective-permute-start | bytes 46808 | tf_op jit(solution)/shard_map/ppermute | solution.py:111
  101.0 2.3 %copy-start.3 = (f32[16,8,128]{2,1,0:T(8,128)S(1)}, f32[16,8,128]{2,1,0:T(8,128)}, u32[]{:S(2)}) copy-start(f32[16,8,128]{2,1,0:T(8,128)} %param.18) | copy-start | bytes 196612
  127.4 37.0 %copy-start.1 = (f32[16,8,128]{2,1,0:T(8,128)}, f32[16,8,128]{2,1,0:T(8,128)S(1)}, u32[]{:S(2)}) copy-start(f32[16,8,128]{2,1,0:T(8,128)S(1)} %all_to_all.30) | copy-start | bytes 196612
  127.4 7.1 %collective-permute-start.12 = (f32[16,1,128]{2,1,0:T(1,128)S(1)}, f32[16,1,128]{2,1,0:T(1,128)S(1)}, u32[]{:S(2)}, u32[]{:S(2)}) collective-permute-start(f32[16,1,128]{2,1,0:T(1,128)S(1)} %get-tuple-element.57), channel_id=1, source_target_pairs={{32,0},{64,32},{96,64},{128,96},{160,128},{192,160},{224,192},{256... | collective-permute-start | bytes 24584 | tf_op jit(solution)/shard_map/ppermute | solution.py:111
  130.8 6.8 %collective-permute-start.13 = (f32[16,1,128]{2,1,0:T(1,128)S(1)}, f32[16,1,128]{2,1,0:T(1,128)S(1)}, u32[]{:S(2)}, u32[]{:S(2)}) collective-permute-start(f32[16,1,128]{2,1,0:T(1,128)S(1)} %get-tuple-element.56), channel_id=1, source_target_pairs={{0,32},{32,64},{64,96},{96,128},{128,160},{160,192},{192,224},{224... | collective-permute-start | bytes 24584 | tf_op jit(solution)/shard_map/ppermute | solution.py:109
  137.7 10.8 %collective-permute-start.14 = (f32[16,10,1]{2,1,0:T(8,128)S(1)}, f32[16,10,1]{2,1,0:T(8,128)S(1)}, u32[]{:S(2)}, u32[]{:S(2)}) collective-permute-start(f32[16,10,1]{2,1,0:T(8,128)S(1)} %get-tuple-element.50), channel_id=1, source_target_pairs={{4,0},{8,4},{12,8},{16,12},{20,16},{24,20},{28,24},{5,1},{9,5},{13... | collective-permute-start | bytes 1928 | tf_op jit(solution)/shard_map/ppermute | solution.py:111
  146.0 10.5 %collective-permute-start.15 = (f32[16,10,1]{2,1,0:T(8,128)S(1)}, f32[16,10,1]{2,1,0:T(8,128)S(1)}, u32[]{:S(2)}, u32[]{:S(2)}) collective-permute-start(f32[16,10,1]{2,1,0:T(8,128)S(1)} %get-tuple-element.49), channel_id=1, source_target_pairs={{0,4},{4,8},{8,12},{12,16},{16,20},{20,24},{24,28},{1,5},{5,9},{9,... | collective-permute-start | bytes 1928 | tf_op jit(solution)/shard_map/ppermute | solution.py:109
  156.6 4.5 %collective-permute-start.16 = (f32[1,10,130]{2,1,0:T(8,128)S(1)}, f32[1,10,130]{2,1,0:T(8,128)S(1)}, u32[]{:S(2)}, u32[]{:S(2)}) collective-permute-start(f32[1,10,130]{2,1,0:T(8,128)S(1)} %get-tuple-element.43), channel_id=1, source_target_pairs={{1,0},{2,1},{3,2},{5,4},{6,5},{7,6},{9,8},{10,9},{11,10},{13,12},{... | collective-permute-start | bytes 15608 | tf_op jit(solution)/shard_map/ppermute | solution.py:111
  158.5 5.1 %collective-permute-start.17 = (f32[1,10,130]{2,1,0:T(8,128)S(1)}, f32[1,10,130]{2,1,0:T(8,128)S(1)}, u32[]{:S(2)}, u32[]{:S(2)}) collective-permute-start(f32[1,10,130]{2,1,0:T(8,128)S(1)} %get-tuple-element.44), channel_id=1, source_target_pairs={{0,1},{1,2},{2,3},{4,5},{5,6},{6,7},{8,9},{9,10},{10,11},{12,13},{... | collective-permute-start | bytes 15608 | tf_op jit(solution)/shard_map/ppermute | solution.py:109

commit v2 on v1

--- a/solution.py
+++ b/solution.py
@@ -217,17 +217,32 @@
     return right_side / main_band
 
 
-def brick_bands(porosity, permeability, padded, dilation, levels, layer_count):
-    level_index = lax.axis_index("gz") * levels + jnp.arange(levels, dtype=jnp.int32)
-    at_top = (level_index == levels * layer_count - 1)[:, None, None]
-    return band_terms(
-        porosity,
-        permeability,
-        padded[6, :-2, 1:-1, 1:-1],
-        padded[6, 2:, 1:-1, 1:-1],
-        at_top,
-        dilation,
-    )
+def face_from(part, axis, from_lower):
+    count = lax.axis_size(axis)
+    if from_lower:
+        pairs = [(i, i + 1) for i in range(count - 1)]
+    else:
+        pairs = [(i + 1, i) for i in range(count - 1)]
+    return lax.ppermute(part, axis, pairs)
+
+
+def faces_of(cells, sides):
+    got = {}
+    for axis, dim in sides:
+        size = cells.shape[dim]
+        got[dim] = (
+            face_from(lax.slice_in_dim(cells, size - 1, size, axis=dim), axis, True),
+            face_from(lax.slice_in_dim(cells, 0, 1, axis=dim), axis, False),
+        )
+    return got
+
+
+def along(cells, faces, dim):
+    size = cells.shape[dim]
+    lower, upper = faces[dim]
+    ahead = jnp.concatenate([lax.slice_in_dim(cells, 1, size, axis=dim), upper], axis=dim)
+    behind = jnp.concatenate([lower, lax.slice_in_dim(cells, 0, size - 1, axis=dim)], axis=dim)
+    return (ahead - behind) * 0.5
 
 
 def shards(
@@ -243,27 +258,65 @@
     permeability,
 ):
     levels, extent, breadth = porosity.shape
+    all_porosity = lax.all_gather(porosity, "gz", axis=0, tiled=True)
+    all_permeability = lax.all_gather(permeability, "gz", axis=0, tiled=True)
+    height = all_porosity.shape[0]
     cell_sums = cell_sums_of(
         stress_trial, mean_stress, consolidation, point_velocity, point_weight, point_cell,
         yield_flag, point_count, levels, extent, breadth,
     )
-    outgoing = jnp.concatenate([cell_sums[:6], permeability[None]], axis=0)
-    padded = padded_2(outgoing, (("gx", 2), ("gy", 3), ("gz", 1)), 1)
-    velocity = brick_velocity(cell_sums, padded)
-    padded_velocity = padded_2(velocity, (("gx", 2), ("gy", 3), ("gz", 1)), 1)
-    dilation = divergence(padded_velocity)
-    layer_count = lax.axis_size("gz")
-    band_set = brick_bands(porosity, permeability, padded, dilation, levels, layer_count)
-    columns = lax.all_to_all(jnp.stack(band_set), "gz", split_axis=3, concat_axis=1, tiled=True)
-    height = columns.shape[1]
-    flattened = columns.reshape(4, height, -1)
-    solved = cyclic_solve(flattened[0], flattened[1], flattened[2], flattened[3])
-    pressure = lax.all_to_all(
-        solved.reshape(height, extent, -1), "gz", split_axis=0, concat_axis=2, tiled=True
-    )
-    padded_pressure = padded_2(pressure, (("gx", 1), ("gy", 2), ("gz", 0)), 1)
+    sides = (("gx", 2), ("gy", 3), ("gz", 1))
+    stress_sums = cell_sums[:6]
+    sf = faces_of(stress_sums, sides)
+    d_x = lambda c: along(stress_sums[c:c + 1], {2: (sf[2][0][c:c + 1], sf[2][1][c:c + 1])}, 2)[0]
+    d_y = lambda c: along(stress_sums[c:c + 1], {3: (sf[3][0][c:c + 1], sf[3][1][c:c + 1])}, 3)[0]
+    d_z = lambda c: along(stress_sums[c:c + 1], {1: (sf[1][0][c:c + 1], sf[1][1][c:c + 1])}, 1)[0]
+    floored = jnp.maximum(cell_sums[9], mass_floor)
+    force_x = d_x(0) + d_y(3) + d_z(5)
+    force_y = d_x(3) + d_y(1) + d_z(4)
+    force_z = d_x(5) + d_y(4) + d_z(2)
+    velocity = jnp.stack(
+        [
+            (cell_sums[6] + time_step * force_x) / floored,
+            (cell_sums[7] + time_step * force_y) / floored,
+            (cell_sums[8] + time_step * force_z) / floored,
+        ]
+    )
+    vf = faces_of(velocity, sides)
+    dilation = (
+        along(velocity[0:1], {2: (vf[2][0][0:1], vf[2][1][0:1])}, 2)[0]
+        + along(velocity[1:2], {3: (vf[3][0][1:2], vf[3][1][1:2])}, 3)[0]
+        + along(velocity[2:3], {1: (vf[1][0][2:3], vf[1][1][2:3])}, 1)[0]
+    )
+    right_side = -source_rate * (1.0 - porosity) * dilation
+    all_right = lax.all_gather(right_side, "gz", axis=0, tiled=True)
+    zero_level = jnp.zeros((1, extent, breadth), jnp.float32)
+    level_above = jnp.concatenate([all_permeability[1:], zero_level], axis=0)
+    level_below = jnp.concatenate([zero_level, all_permeability[:-1]], axis=0)
+    at_top = (jnp.arange(height, dtype=jnp.int32) == height - 1)[:, None, None]
+    up_face = harmonic(all_permeability, level_above)
+    down_face = harmonic(level_below, all_permeability)
+    top_face = jnp.where(at_top, all_permeability, up_face)
+    lower_band = -time_step * down_face
+    upper_band = -time_step * up_face
+    main_band = storage_rate * all_porosity + time_step * (down_face + top_face)
+    column = height, extent * breadth
+    solved = cyclic_solve(
+        lower_band.reshape(column), main_band.reshape(column), upper_band.reshape(column),
+        all_right.reshape(column),
+    ).reshape(height, extent, breadth)
+    first = lax.axis_index("gz") * levels
+    around = lax.dynamic_slice_in_dim(
+        jnp.concatenate([zero_level, solved, zero_level], axis=0), first, levels + 2, axis=0
+    )
+    pressure = around[1:-1]
+    pf = faces_of(pressure, (("gx", 1), ("gy", 2)))
     gradient = jnp.stack(
-        [along_x(padded_pressure), along_y(padded_pressure), along_z(padded_pressure)]
+        [
+            along(pressure, pf, 1),
+            along(pressure, pf, 2),
+            (around[2:] - around[:-2]) * 0.5,
+        ]
     )
     return (velocity - time_step * gradient, pressure)
 

time: 165 us -> 133 us (0.81)
  the two profiles are of different devices: /device:TPU:134 before, /device:TPU:410 now
where the time goes in v2:
time: 133 us; the launch traced here: 132 us
  starting transfers between devices  55 us (41%)
  Pallas kernels  32.2 us (24%)
  blocking collectives  17.7 us (13%)
  local copies, waits for them, and re-layouts  17.3 us (13%)
  other arithmetic  4.71 us (4%)
  waiting for transfers between devices  2.48 us (2%)
  between operations  2.16 us (2%)
    ppermute x16, starting transfers between devices, face_from(): return lax.ppermute(part, axis, pairs)  55 us
    pallas_call x1, Pallas kernels, cell_sums_of(): pl.pallas_call(sums_kernel, out_shape=jax.ShapeDtypeStruct((10, levels, e...  32.2 us
    all_gather x1, blocking collectives, shards(): all_porosity = lax.all_gather(porosity, 'gz', axis=0, tiled=True)  5.98 us
    all_gather x1, blocking collectives, shards(): all_permeability = lax.all_gather(permeability, 'gz', axis=0, tiled=True)  5.89 us
    all_gather x1, blocking collectives, shards(): all_right = lax.all_gather(right_side, 'gz', axis=0, tiled=True)  5.79 us
    unnamed x53, local copies, waits for them, and re-layouts  4.42 us
    slice x8, local copies, waits for them, and re-layouts, faces_of(): lax.slice_in_dim(cells, size - 1, size, axis=dim)  3.75 us
  transfers between devices with their start and end apart: 16, of which 1 were waited for; matrix products, arithmetic and copies ran while one was open for 7% of the time, Pallas kernels for 0%

profile of v2, /device:TPU:410, one launch (start us, length us, event | category | flops | bytes accessed | tf_op | source)
XLA Modules:
  0.0 131.6 jit_solution(14231007549544503845)
XLA Ops:
  1.3 32.2 %shard_map.113 = f32[10,16,8,128]{3,2,1,0:T(8,128)} custom-call(s32[1,1]{1,0:T(1,128)} %bitcast.105.count_ref, f32[6,24576]{1,0:T(8,128)} %st_ref.1, f32[1,24576]{1,0:T(1,128)} %bitcast.139, f32[1,24576]{1,0:T(1,128)} %bitcast.140, f32[3,24576]{1,0:T(4,128)} %vel_ref.1, f32[1,24576]{1,0:T(1,128)} %bitcast.141, s32[1,24576]{1,0:T(1,128)} %bitcast.142, ...), custom_call_target="tpu_custom_call" | custom-call | flops 24159191040 | bytes 1933312 | tf_op jit(solution)/shard_map/pallas_call | solution.py:85
  33.5 2.2 %fusion.31 = (f32[6,16,8,1]{3,2,1,0:T(8,128)}, f32[6,16,8,1]{3,2,1,0:T(8,128)}) fusion(f32[10,16,8,128]{3,2,1,0:T(8,128)} %shard_map.113), kind=kLoop, calls=%fused_computation.106 | loop fusion | bytes 12288 | tf_op jit(solution)/shard_map/slice | solution.py:234
  35.7 3.7 %collective-permute-start.3 = (f32[6,16,8,1]{3,2,1,0:T(8,128)}, f32[6,16,8,1]{3,2,1,0:T(8,128)}, u32[]{:S(2)}, u32[]{:S(2)}) collective-permute-start(f32[6,16,8,1]{3,2,1,0:T(8,128)} %get-tuple-element.40), channel_id=1, source_target_pairs={{0,4},{4,8},{8,12},{12,16},{16,20},{20,24},{24,28},{1,5},{5,9},{9,... | collective-permute-start | bytes 9224 | tf_op jit(solution)/shard_map/ppermute | solution.py:226
  39.4 2.2 %collective-permute-start.2 = (f32[6,16,8,1]{3,2,1,0:T(8,128)}, f32[6,16,8,1]{3,2,1,0:T(8,128)}, u32[]{:S(2)}, u32[]{:S(2)}) collective-permute-start(f32[6,16,8,1]{3,2,1,0:T(8,128)} %get-tuple-element.41), channel_id=1, source_target_pairs={{4,0},{8,4},{12,8},{16,12},{20,16},{24,20},{28,24},{5,1},{9,5},{13... | collective-permute-start | bytes 9224 | tf_op jit(solution)/shard_map/ppermute | solution.py:226
  41.6 0.7 fusion.32
  42.3 2.9 %collective-permute-start.1 = (f32[6,16,1,128]{3,2,1,0:T(1,128)}, f32[6,16,1,128]{3,2,1,0:T(1,128)}, u32[]{:S(2)}, u32[]{:S(2)}) collective-permute-start(f32[6,16,1,128]{3,2,1,0:T(1,128)} %get-tuple-element.42), channel_id=1, source_target_pairs={{0,32},{32,64},{64,96},{96,128},{128,160},{160,192},{192,224},{224... | collective-permute-start | bytes 147464 | tf_op jit(solution)/shard_map/ppermute | solution.py:226
  45.2 4.1 %collective-permute-start = (f32[6,16,1,128]{3,2,1,0:T(1,128)}, f32[6,16,1,128]{3,2,1,0:T(1,128)}, u32[]{:S(2)}, u32[]{:S(2)}) collective-permute-start(f32[6,16,1,128]{3,2,1,0:T(1,128)} %get-tuple-element.43), channel_id=1, source_target_pairs={{32,0},{64,32},{96,64},{128,96},{160,128},{192,160},{224,192},{256... | collective-permute-start | bytes 147464 | tf_op jit(solution)/shard_map/ppermute | solution.py:226
  49.3 0.6 fusion.30
  49.9 1.9 %collective-permute-start.5 = (f32[6,1,8,128]{3,2,1,0:T(8,128)}, f32[6,1,8,128]{3,2,1,0:T(8,128)}, u32[]{:S(2)}, u32[]{:S(2)}) collective-permute-start(f32[6,1,8,128]{3,2,1,0:T(8,128)} %get-tuple-element.38), channel_id=1, source_target_pairs={{0,1},{1,2},{2,3},{4,5},{5,6},{6,7},{8,9},{9,10},{10,11},{12,13},{... | collective-permute-start | bytes 73736 | tf_op jit(solution)/shard_map/ppermute | solution.py:226
  51.9 0.7 fusion.28
  52.6 0.7 fusion.29
  53.3 0.2 copy-done.16
  53.5 5.9 %all_gather.10 = f32[64,8,128]{2,1,0:T(8,128)S(1)} all-gather(f32[16,8,128]{2,1,0:T(8,128)S(1)} %copy-done.16), channel_id=1, replica_groups=mesh['gx'=16,'gy'=8,'gz'=4] {'gz'}, dimensions={0}, use_global_device_ids=true | all-gather | bytes 327680 | tf_op jit(solution)/shard_map/all_gather | solution.py:262
  59.4 0.8 copy-done.8
  60.2 6.0 %all_gather.11 = f32[64,8,128]{2,1,0:T(8,128)S(1)} all-gather(f32[16,8,128]{2,1,0:T(8,128)S(1)} %copy-done.8), channel_id=1, replica_groups=mesh['gx'=16,'gy'=8,'gz'=4] {'gz'}, dimensions={0}, use_global_device_ids=true | all-gather | bytes 327680 | tf_op jit(solution)/shard_map/all_gather | solution.py:261
  66.2 0.2 fusion.25
  66.5 0.7 fusion.27
  67.8 0.7 copy-done.17
  68.4 3.5 %collective-permute-start.4 = (f32[6,1,8,128]{3,2,1,0:T(8,128)S(1)}, f32[6,1,8,128]{3,2,1,0:T(8,128)S(1)}, u32[]{:S(2)}, u32[]{:S(2)}) collective-permute-start(f32[6,1,8,128]{3,2,1,0:T(8,128)S(1)} %copy-done.17), channel_id=1, source_target_pairs={{1,0},{2,1},{3,2},{5,4},{6,5},{7,6},{9,8},{10,9},{11,10},{13,12},{... | collective-permute-start | bytes 73736 | tf_op jit(solution)/shard_map/ppermute | solution.py:226
  71.9 0.9 fusion.33
  72.8 1.0 fusion.34
  73.8 0.7 fusion.66
  74.6 0.8 fusion.64
  75.3 0.7 fusion.65
  76.2 0.1 fusion.9
  76.3 0.7 copy-done.1
  77.1 0.1 fusion.8
  77.2 0.7 copy-done.10
  77.9 0.1 fusion.7
  78.3 1.9 %collective-permute-start.8 = (f32[3,16,8,1]{3,2,1,0:T(8,128)S(1)}, f32[3,16,8,1]{3,2,1,0:T(8,128)S(1)}, u32[]{:S(2)}, u32[]{:S(2)}) collective-permute-start(f32[3,16,8,1]{3,2,1,0:T(8,128)S(1)} %get-tuple-element.105), channel_id=1, source_target_pairs={{4,0},{8,4},{12,8},{16,12},{20,16},{24,20},{28,24},{5,1},{9,5},{13... | collective-permute-start | bytes 4616 | tf_op jit(solution)/shard_map/ppermute | solution.py:226
  80.3 7.5 %collective-permute-start.9 = (f32[3,16,8,1]{3,2,1,0:T(8,128)S(1)}, f32[3,16,8,1]{3,2,1,0:T(8,128)}, u32[]{:S(2)}, u32[]{:S(2)}) collective-permute-start(f32[3,16,8,1]{3,2,1,0:T(8,128)S(1)} %get-tuple-element.104), channel_id=1, source_target_pairs={{0,4},{4,8},{8,12},{12,16},{16,20},{20,24},{24,28},{1,5},{5,9},{9,... | collective-permute-start | bytes 4616 | tf_op jit(solution)/shard_map/ppermute | solution.py:226
  87.8 1.9 %collective-permute-start.11 = (f32[3,1,8,128]{3,2,1,0:T(8,128)S(1)}, f32[3,1,8,128]{3,2,1,0:T(8,128)S(1)}, u32[]{:S(2)}, u32[]{:S(2)}) collective-permute-start(f32[3,1,8,128]{3,2,1,0:T(8,128)S(1)} %get-tuple-element.102), channel_id=1, source_target_pairs={{0,1},{1,2},{2,3},{4,5},{5,6},{6,7},{8,9},{9,10},{10,11},{12,13},{... | collective-permute-start | bytes 36872 | tf_op jit(solution)/shard_map/ppermute | solution.py:226
  89.8 1.9 %collective-permute-start.7 = (f32[3,16,1,128]{3,2,1,0:T(1,128)S(1)}, f32[3,16,1,128]{3,2,1,0:T(1,128)S(1)}, u32[]{:S(2)}, u32[]{:S(2)}) collective-permute-start(f32[3,16,1,128]{3,2,1,0:T(1,128)S(1)} %get-tuple-element.106), channel_id=1, source_target_pairs={{0,32},{32,64},{64,96},{96,128},{128,160},{160,192},{192,224},{224... | collective-permute-start | bytes 73736 | tf_op jit(solution)/shard_map/ppermute | solution.py:226
  91.7 5.1 %collective-permute-start.6 = (f32[3,16,1,128]{3,2,1,0:T(1,128)S(1)}, f32[3,16,1,128]{3,2,1,0:T(1,128)S(1)}, u32[]{:S(2)}, u32[]{:S(2)}) collective-permute-start(f32[3,16,1,128]{3,2,1,0:T(1,128)S(1)} %get-tuple-element.107), channel_id=1, source_target_pairs={{32,0},{64,32},{96,64},{128,96},{160,128},{192,160},{224,192},{256... | collective-permute-start | bytes 73736 | tf_op jit(solution)/shard_map/ppermute | solution.py:226
  96.8 3.1 %collective-permute-start.10 = (f32[3,1,8,128]{3,2,1,0:T(8,128)S(1)}, f32[3,1,8,128]{3,2,1,0:T(8,128)S(1)}, u32[]{:S(2)}, u32[]{:S(2)}) collective-permute-start(f32[3,1,8,128]{3,2,1,0:T(8,128)S(1)} %get-tuple-element.103), channel_id=1, source_target_pairs={{1,0},{2,1},{3,2},{5,4},{6,5},{7,6},{9,8},{10,9},{11,10},{13,12},{... | collective-permute-start | bytes 36872 | tf_op jit(solution)/shard_map/ppermute | solution.py:226
  99.9 0.1 copy.26
  100.1 0.1 copy.27
  100.2 0.8 slice.628
  101.1 0.1 copy.28
  101.2 0.1 copy.29
  101.4 0.6 copy-done.9
  102.0 0.1 fusion.22
  102.1 5.8 %all_gather.9 = f32[64,8,128]{2,1,0:T(8,128)S(1)} all-gather(f32[16,8,128]{2,1,0:T(8,128)S(1)} %fusion.22), channel_id=1, replica_groups=mesh['gx'=16,'gy'=8,'gz'=4] {'gz'}, dimensions={0}, use_global_device_ids=true | all-gather | bytes 327680 | tf_op jit(solution)/shard_map/all_gather | solution.py:292
  108.1 0.4 fusion
  108.6 0.4 multiply_add_fusion.7
  109.1 0.2 multiply_add_fusion.6
  109.4 0.3 multiply_add_fusion.5
  109.8 0.2 multiply_add_fusion.4
  110.1 0.3 multiply_add_fusion.3
  110.5 0.1 multiply_add_fusion.2
  110.7 0.3 multiply_add_fusion.1
  111.0 0.2 pad_multiply_fusion
  111.3 0.2 divide_bitcast_fusion
  111.7 0.6 fusion.61
  112.4 1.9 %collective-permute-start.14 = (f32[16,8,1]{2,1,0:T(8,128)S(1)}, f32[16,8,1]{2,1,0:T(8,128)S(1)}, u32[]{:S(2)}, u32[]{:S(2)}) collective-permute-start(f32[16,8,1]{2,1,0:T(8,128)S(1)} %get-tuple-element.115), channel_id=1, source_target_pairs={{4,0},{8,4},{12,8},{16,12},{20,16},{24,20},{28,24},{5,1},{9,5},{13... | collective-permute-start | bytes 1544 | tf_op jit(solution)/shard_map/ppermute | solution.py:226
  114.3 7.5 %collective-permute-start.15 = (f32[16,8,1]{2,1,0:T(8,128)S(1)}, f32[16,8,1]{2,1,0:T(8,128)S(1)}, u32[]{:S(2)}, u32[]{:S(2)}) collective-permute-start(f32[16,8,1]{2,1,0:T(8,128)S(1)} %get-tuple-element.114), channel_id=1, source_target_pairs={{0,4},{4,8},{8,12},{12,16},{16,20},{20,24},{24,28},{1,5},{5,9},{9,... | collective-permute-start | bytes 1544 | tf_op jit(solution)/shard_map/ppermute | solution.py:226
  121.9 2.2 %collective-permute-start.12 = (f32[16,1,128]{2,0,1:T(8,128)S(1)}, f32[16,1,128]{2,0,1:T(8,128)S(1)}, u32[]{:S(2)}, u32[]{:S(2)}) collective-permute-start(f32[16,1,128]{2,0,1:T(8,128)S(1)} %bitcast.136), channel_id=1, source_target_pairs={{32,0},{64,32},{96,64},{128,96},{160,128},{192,160},{224,192},{256... | collective-permute-start | bytes 24584 | tf_op jit(solution)/shard_map/ppermute | solution.py:226
  124.1 3.6 %collective-permute-start.13 = (f32[16,1,128]{2,0,1:T(8,128)S(1)}, f32[16,1,128]{2,0,1:T(8,128)S(1)}, u32[]{:S(2)}, u32[]{:S(2)}) collective-permute-start(f32[16,1,128]{2,0,1:T(8,128)S(1)} %bitcast.135), channel_id=1, source_target_pairs={{0,32},{32,64},{64,96},{96,128},{128,160},{160,192},{192,224},{224... | collective-permute-start | bytes 24584 | tf_op jit(solution)/shard_map/ppermute | solution.py:226
  127.7 0.1 copy.32
  127.9 0.1 copy.33
  128.0 0.1 copy.34
  128.1 0.1 copy.35
  128.4 2.4 %collective-permute-done.13 = f32[16,1,128]{2,0,1:T(8,128)S(1)} collective-permute-done((f32[16,1,128]{2,0,1:T(8,128)S(1)}, f32[16,1,128]{2,0,1:T(8,128)S(1)}, u32[]{:S(2)}, u32[]{:S(2)}) %collective-permute-start.13) | collective-permute-done | bytes 8224 | tf_op jit(solution)/shard_map/ppermute | solution.py:226
  130.9 0.7 fusion.2
  (108 shorter events, 2.3 us)
Async XLA Ops:
  33.5 8.1 %copy-start = (f32[10,16,8,128]{3,2,1,0:T(8,128)S(1)}, f32[10,16,8,128]{3,2,1,0:T(8,128)}, u32[]{:S(2)}) copy-start(f32[10,16,8,128]{3,2,1,0:T(8,128)} %shard_map.113) | copy-start | bytes 1966084
  35.7 32.0 %collective-permute-start.3 = (f32[6,16,8,1]{3,2,1,0:T(8,128)}, f32[6,16,8,1]{3,2,1,0:T(8,128)}, u32[]{:S(2)}, u32[]{:S(2)}) collective-permute-start(f32[6,16,8,1]{3,2,1,0:T(8,128)} %get-tuple-element.40), channel_id=1, source_target_pairs={{0,4},{4,8},{8,12},{12,16},{16,20},{20,24},{24,28},{1,5},{5,9},{9,... | collective-permute-start | bytes 9224 | tf_op jit(solution)/shard_map/ppermute | solution.py:226
  39.4 33.4 %collective-permute-start.2 = (f32[6,16,8,1]{3,2,1,0:T(8,128)}, f32[6,16,8,1]{3,2,1,0:T(8,128)}, u32[]{:S(2)}, u32[]{:S(2)}) collective-permute-start(f32[6,16,8,1]{3,2,1,0:T(8,128)} %get-tuple-element.41), channel_id=1, source_target_pairs={{4,0},{8,4},{12,8},{16,12},{20,16},{24,20},{28,24},{5,1},{9,5},{13... | collective-permute-start | bytes 9224 | tf_op jit(solution)/shard_map/ppermute | solution.py:226
  42.3 32.3 %collective-permute-start.1 = (f32[6,16,1,128]{3,2,1,0:T(1,128)}, f32[6,16,1,128]{3,2,1,0:T(1,128)}, u32[]{:S(2)}, u32[]{:S(2)}) collective-permute-start(f32[6,16,1,128]{3,2,1,0:T(1,128)} %get-tuple-element.42), channel_id=1, source_target_pairs={{0,32},{32,64},{64,96},{96,128},{128,160},{160,192},{192,224},{224... | collective-permute-start | bytes 147464 | tf_op jit(solution)/shard_map/ppermute | solution.py:226
  45.2 30.1 %collective-permute-start = (f32[6,16,1,128]{3,2,1,0:T(1,128)}, f32[6,16,1,128]{3,2,1,0:T(1,128)}, u32[]{:S(2)}, u32[]{:S(2)}) collective-permute-start(f32[6,16,1,128]{3,2,1,0:T(1,128)} %get-tuple-element.43), channel_id=1, source_target_pairs={{32,0},{64,32},{96,64},{128,96},{160,128},{192,160},{224,192},{256... | collective-permute-start | bytes 147464 | tf_op jit(solution)/shard_map/ppermute | solution.py:226
  49.9 23.9 %collective-permute-start.5 = (f32[6,1,8,128]{3,2,1,0:T(8,128)}, f32[6,1,8,128]{3,2,1,0:T(8,128)}, u32[]{:S(2)}, u32[]{:S(2)}) collective-permute-start(f32[6,1,8,128]{3,2,1,0:T(8,128)} %get-tuple-element.38), channel_id=1, source_target_pairs={{0,1},{1,2},{2,3},{4,5},{5,6},{6,7},{8,9},{9,10},{10,11},{12,13},{... | collective-permute-start | bytes 73736 | tf_op jit(solution)/shard_map/ppermute | solution.py:226
  52.6 0.9 copy-start.16
  59.4 0.8 copy-start.8
  67.7 0.7 copy-start.17
  68.4 6.1 %collective-permute-start.4 = (f32[6,1,8,128]{3,2,1,0:T(8,128)S(1)}, f32[6,1,8,128]{3,2,1,0:T(8,128)S(1)}, u32[]{:S(2)}, u32[]{:S(2)}) collective-permute-start(f32[6,1,8,128]{3,2,1,0:T(8,128)S(1)} %copy-done.17), channel_id=1, source_target_pairs={{1,0},{2,1},{3,2},{5,4},{6,5},{7,6},{9,8},{10,9},{11,10},{13,12},{... | collective-permute-start | bytes 73736 | tf_op jit(solution)/shard_map/ppermute | solution.py:226
  72.8 3.3 %copy-start.6 = (f32[1,16,7,128]{3,2,1,0:T(8,128)S(1)}, f32[1,16,7,128]{3,2,1,0:T(8,128)}, u32[]{:S(2)}) copy-start(f32[1,16,7,128]{3,2,1,0:T(8,128)} %get-tuple-element.32) | copy-start | bytes 172036
  72.8 3.2 %copy-start.7 = (f32[1,16,7,128]{3,2,1,0:T(8,128)S(1)}, f32[1,16,7,128]{3,2,1,0:T(8,128)}, u32[]{:S(2)}) copy-start(f32[1,16,7,128]{3,2,1,0:T(8,128)} %get-tuple-element.37) | copy-start | bytes 172036
  72.8 3.2 %copy-start.14 = (f32[1,15,8,128]{3,2,1,0:T(8,128)S(1)}, f32[1,15,8,128]{3,2,1,0:T(8,128)}, u32[]{:S(2)}) copy-start(f32[1,15,8,128]{3,2,1,0:T(8,128)} %get-tuple-element.20) | copy-start | bytes 184324
  72.8 3.2 %copy-start.15 = (f32[1,15,8,128]{3,2,1,0:T(8,128)S(1)}, f32[1,15,8,128]{3,2,1,0:T(8,128)}, u32[]{:S(2)}) copy-start(f32[1,15,8,128]{3,2,1,0:T(8,128)} %get-tuple-element.25) | copy-start | bytes 184324
  74.5 1.6 %copy-start.5 = (f32[1,16,8,127]{3,2,1,0:T(8,128)S(1)}, f32[1,16,8,127]{3,2,1,0:T(8,128)}, u32[]{:S(2)}) copy-start(f32[1,16,8,127]{3,2,1,0:T(8,128)} %get-tuple-element.31) | copy-start | bytes 195076
  74.5 1.6 %copy-start.4 = (f32[1,16,8,127]{3,2,1,0:T(8,128)S(1)}, f32[1,16,8,127]{3,2,1,0:T(8,128)}, u32[]{:S(2)}) copy-start(f32[1,16,8,127]{3,2,1,0:T(8,128)} %get-tuple-element.26) | copy-start | bytes 195076
  76.1 0.8 copy-start.1
  76.1 0.9 copy-start.2
  76.1 0.9 copy-start.3
  76.1 0.9 copy-start.12
  76.1 0.9 copy-start.13
  77.1 0.8 copy-start.10
  77.1 0.9 copy-start.11
  78.3 18.5 %collective-permute-start.8 = (f32[3,16,8,1]{3,2,1,0:T(8,128)S(1)}, f32[3,16,8,1]{3,2,1,0:T(8,128)S(1)}, u32[]{:S(2)}, u32[]{:S(2)}) collective-permute-start(f32[3,16,8,1]{3,2,1,0:T(8,128)S(1)} %get-tuple-element.105), channel_id=1, source_target_pairs={{4,0},{8,4},{12,8},{16,12},{20,16},{24,20},{28,24},{5,1},{9,5},{13... | collective-permute-start | bytes 4616 | tf_op jit(solution)/shard_map/ppermute | solution.py:226
  80.3 19.9 %collective-permute-start.9 = (f32[3,16,8,1]{3,2,1,0:T(8,128)S(1)}, f32[3,16,8,1]{3,2,1,0:T(8,128)}, u32[]{:S(2)}, u32[]{:S(2)}) collective-permute-start(f32[3,16,8,1]{3,2,1,0:T(8,128)S(1)} %get-tuple-element.104), channel_id=1, source_target_pairs={{0,4},{4,8},{8,12},{12,16},{16,20},{20,24},{24,28},{1,5},{5,9},{9,... | collective-permute-start | bytes 4616 | tf_op jit(solution)/shard_map/ppermute | solution.py:226
  87.8 13.5 %collective-permute-start.11 = (f32[3,1,8,128]{3,2,1,0:T(8,128)S(1)}, f32[3,1,8,128]{3,2,1,0:T(8,128)S(1)}, u32[]{:S(2)}, u32[]{:S(2)}) collective-permute-start(f32[3,1,8,128]{3,2,1,0:T(8,128)S(1)} %get-tuple-element.102), channel_id=1, source_target_pairs={{0,1},{1,2},{2,3},{4,5},{5,6},{6,7},{8,9},{9,10},{10,11},{12,13},{... | collective-permute-start | bytes 36872 | tf_op jit(solution)/shard_map/ppermute | solution.py:226
  89.8 11.6 %collective-permute-start.7 = (f32[3,16,1,128]{3,2,1,0:T(1,128)S(1)}, f32[3,16,1,128]{3,2,1,0:T(1,128)S(1)}, u32[]{:S(2)}, u32[]{:S(2)}) collective-permute-start(f32[3,16,1,128]{3,2,1,0:T(1,128)S(1)} %get-tuple-element.106), channel_id=1, source_target_pairs={{0,32},{32,64},{64,96},{96,128},{128,160},{160,192},{192,224},{224... | collective-permute-start | bytes 73736 | tf_op jit(solution)/shard_map/ppermute | solution.py:226
  91.7 9.7 %collective-permute-start.6 = (f32[3,16,1,128]{3,2,1,0:T(1,128)S(1)}, f32[3,16,1,128]{3,2,1,0:T(1,128)S(1)}, u32[]{:S(2)}, u32[]{:S(2)}) collective-permute-start(f32[3,16,1,128]{3,2,1,0:T(1,128)S(1)} %get-tuple-element.107), channel_id=1, source_target_pairs={{32,0},{64,32},{96,64},{128,96},{160,128},{192,160},{224,192},{256... | collective-permute-start | bytes 73736 | tf_op jit(solution)/shard_map/ppermute | solution.py:226
  96.8 4.5 %collective-permute-start.10 = (f32[3,1,8,128]{3,2,1,0:T(8,128)S(1)}, f32[3,1,8,128]{3,2,1,0:T(8,128)S(1)}, u32[]{:S(2)}, u32[]{:S(2)}) collective-permute-start(f32[3,1,8,128]{3,2,1,0:T(8,128)S(1)} %get-tuple-element.103), channel_id=1, source_target_pairs={{1,0},{2,1},{3,2},{5,4},{6,5},{7,6},{9,8},{10,9},{11,10},{13,12},{... | collective-permute-start | bytes 36872 | tf_op jit(solution)/shard_map/ppermute | solution.py:226
  101.2 0.8 copy-start.9
  112.4 15.3 %collective-permute-start.14 = (f32[16,8,1]{2,1,0:T(8,128)S(1)}, f32[16,8,1]{2,1,0:T(8,128)S(1)}, u32[]{:S(2)}, u32[]{:S(2)}) collective-permute-start(f32[16,8,1]{2,1,0:T(8,128)S(1)} %get-tuple-element.115), channel_id=1, source_target_pairs={{4,0},{8,4},{12,8},{16,12},{20,16},{24,20},{28,24},{5,1},{9,5},{13... | collective-permute-start | bytes 1544 | tf_op jit(solution)/shard_map/ppermute | solution.py:226
  114.3 13.7 %collective-permute-start.15 = (f32[16,8,1]{2,1,0:T(8,128)S(1)}, f32[16,8,1]{2,1,0:T(8,128)S(1)}, u32[]{:S(2)}, u32[]{:S(2)}) collective-permute-start(f32[16,8,1]{2,1,0:T(8,128)S(1)} %get-tuple-element.114), channel_id=1, source_target_pairs={{0,4},{4,8},{8,12},{12,16},{16,20},{20,24},{24,28},{1,5},{5,9},{9,... | collective-permute-start | bytes 1544 | tf_op jit(solution)/shard_map/ppermute | solution.py:226
  121.9 6.5 %collective-permute-start.12 = (f32[16,1,128]{2,0,1:T(8,128)S(1)}, f32[16,1,128]{2,0,1:T(8,128)S(1)}, u32[]{:S(2)}, u32[]{:S(2)}) collective-permute-start(f32[16,1,128]{2,0,1:T(8,128)S(1)} %bitcast.136), channel_id=1, source_target_pairs={{32,0},{64,32},{96,64},{128,96},{160,128},{192,160},{224,192},{256... | collective-permute-start | bytes 24584 | tf_op jit(solution)/shard_map/ppermute | solution.py:226
  124.1 6.8 %collective-permute-start.13 = (f32[16,1,128]{2,0,1:T(8,128)S(1)}, f32[16,1,128]{2,0,1:T(8,128)S(1)}, u32[]{:S(2)}, u32[]{:S(2)}) collective-permute-start(f32[16,1,128]{2,0,1:T(8,128)S(1)} %bitcast.135), channel_id=1, source_target_pairs={{0,32},{32,64},{64,96},{96,128},{128,160},{160,192},{192,224},{224... | collective-permute-start | bytes 24584 | tf_op jit(solution)/shard_map/ppermute | solution.py:226

commit v3 on v2

--- a/solution.py
+++ b/solution.py
@@ -1,3 +1,5 @@
+import functools
+
 import jax
 import jax.numpy as jnp
 from jax import lax
@@ -217,6 +219,83 @@
     return right_side / main_band
 
 
+MESH_AXES = ("gx", "gy", "gz")
+
+
+def halo_kernel(sides, sizes, *refs):
+    count = len(sides)
+    sends = refs[:2 * count]
+    recvs = refs[2 * count:4 * count]
+    send_sem, recv_sem = refs[4 * count:]
+    me = {a: lax.axis_index(a) for a in MESH_AXES}
+
+    def peer(axis, delta):
+        return tuple(me[a] + delta if a == axis else me[a] for a in MESH_AXES)
+
+    links = []
+    for i, axis in enumerate(sides):
+        links.append((axis, -1, me[axis] > 0, 2 * i, 2 * i + 1))
+        links.append((axis, 1, me[axis] < sizes[i] - 1, 2 * i + 1, 2 * i))
+    barrier = pltpu.get_barrier_semaphore()
+    for axis, delta, present, _, _ in links:
+        @pl.when(present)
+        def _():
+            pl.semaphore_signal(barrier, 1, device_id=peer(axis, delta), device_id_type=pl.DeviceIdType.MESH)
+    peers = sum(present.astype(jnp.int32) for _, _, present, _, _ in links)
+    pl.semaphore_wait(barrier, peers)
+    copies = []
+    for axis, delta, present, src, dst in links:
+        copy = pltpu.make_async_remote_copy(
+            src_ref=sends[src], dst_ref=recvs[dst], send_sem=send_sem.at[src], recv_sem=recv_sem.at[dst],
+            device_id=peer(axis, delta), device_id_type=pl.DeviceIdType.MESH,
+        )
+        copies.append((present, copy))
+
+        @pl.when(present)
+        def _():
+            copy.start()
+    for axis, delta, present, src, dst in links:
+        incoming = pltpu.make_async_remote_copy(
+            src_ref=sends[dst], dst_ref=recvs[src], send_sem=send_sem.at[dst], recv_sem=recv_sem.at[src],
+            device_id=peer(axis, delta), device_id_type=pl.DeviceIdType.MESH,
+        )
+
+        @pl.when(present)
+        def _():
+            incoming.wait_recv()
+
+        @pl.when(jnp.logical_not(present))
+        def _():
+            recvs[src][...] = jnp.zeros(recvs[src].shape, recvs[src].dtype)
+    for present, copy in copies:
+        @pl.when(present)
+        def _():
+            copy.wait_send()
+
+
+def exchange(cells, sides, collective):
+    sends = []
+    for axis, dim in sides:
+        size = cells.shape[dim]
+        sends.append(lax.index_in_dim(cells, 0, axis=dim, keepdims=False))
+        sends.append(lax.index_in_dim(cells, size - 1, axis=dim, keepdims=False))
+    axes = tuple(axis for axis, _ in sides)
+    sizes = tuple(lax.axis_size(axis) for axis in axes)
+    vmem = pl.BlockSpec(memory_space=pltpu.VMEM)
+    recvs = pl.pallas_call(
+        functools.partial(halo_kernel, axes, sizes),
+        out_shape=[jax.ShapeDtypeStruct(s.shape, s.dtype) for s in sends],
+        in_specs=[vmem] * len(sends),
+        out_specs=[vmem] * len(sends),
+        scratch_shapes=[pltpu.SemaphoreType.DMA((len(sends),)), pltpu.SemaphoreType.DMA((len(sends),))],
+        compiler_params=pltpu.CompilerParams(collective_id=collective, has_side_effects=True),
+    )(*sends)
+    return {
+        dim: (jnp.expand_dims(recvs[2 * i], dim), jnp.expand_dims(recvs[2 * i + 1], dim))
+        for i, (axis, dim) in enumerate(sides)
+    }
+
+
 def face_from(part, axis, from_lower):
     count = lax.axis_size(axis)
     if from_lower:
@@ -267,7 +346,7 @@
     )
     sides = (("gx", 2), ("gy", 3), ("gz", 1))
     stress_sums = cell_sums[:6]
-    sf = faces_of(stress_sums, sides)
+    sf = exchange(stress_sums, sides, 0)
     d_x = lambda c: along(stress_sums[c:c + 1], {2: (sf[2][0][c:c + 1], sf[2][1][c:c + 1])}, 2)[0]
     d_y = lambda c: along(stress_sums[c:c + 1], {3: (sf[3][0][c:c + 1], sf[3][1][c:c + 1])}, 3)[0]
     d_z = lambda c: along(stress_sums[c:c + 1], {1: (sf[1][0][c:c + 1], sf[1][1][c:c + 1])}, 1)[0]
@@ -282,7 +361,7 @@
             (cell_sums[8] + time_step * force_z) / floored,
         ]
     )
-    vf = faces_of(velocity, sides)
+    vf = exchange(velocity, sides, 1)
     dilation = (
         along(velocity[0:1], {2: (vf[2][0][0:1], vf[2][1][0:1])}, 2)[0]
         + along(velocity[1:2], {3: (vf[3][0][1:2], vf[3][1][1:2])}, 3)[0]
@@ -310,7 +389,7 @@
         jnp.concatenate([zero_level, solved, zero_level], axis=0), first, levels + 2, axis=0
     )
     pressure = around[1:-1]
-    pf = faces_of(pressure, (("gx", 1), ("gy", 2)))
+    pf = exchange(pressure, (("gx", 1), ("gy", 2)), 2)
     gradient = jnp.stack(
         [
             along(pressure, pf, 1),

time: 133 us -> 113 us (0.85)
  the two profiles are of different devices: /device:TPU:410 before, /device:TPU:102 now
where the time goes in v3:
time: 113 us; the launch traced here: 111 us
  Pallas kernels  62.8 us (56%)
  local copies, waits for them, and re-layouts  25.8 us (23%)
  blocking collectives  17.5 us (15%)
  other arithmetic  3.31 us (3%)
  between operations  2.02 us (2%)
    pallas_call x1, Pallas kernels, cell_sums_of(): pl.pallas_call(sums_kernel, out_shape=jax.ShapeDtypeStruct((10, levels, e...  32.2 us
    pallas_call x3, Pallas kernels, exchange(): pl.pallas_call(functools.partial(halo_kernel, axes, sizes), out_shape=[ja...  30.6 us
    unnamed x58, local copies, waits for them, and re-layouts  8.88 us
    all_gather x1, blocking collectives, shards(): all_porosity = lax.all_gather(porosity, 'gz', axis=0, tiled=True)  5.87 us
    all_gather x1, blocking collectives, shards(): all_permeability = lax.all_gather(permeability, 'gz', axis=0, tiled=True)  5.85 us
    all_gather x1, blocking collectives, shards(): all_right = lax.all_gather(right_side, 'gz', axis=0, tiled=True)  5.79 us
    squeeze x5, local copies, waits for them, and re-layouts, exchange(): sends.append(lax.index_in_dim(cells, size - 1, axis=dim, keepdims=False))  3.58 us
    concatenate x14, local copies, waits for them, and re-layouts, along(): jnp.concatenate([lower, lax.slice_in_dim(cells, 0, size - 1, axis=dim)],...  3.2 us

profile of v3, /device:TPU:102, one launch (start us, length us, event | category | flops | bytes accessed | tf_op | source)
XLA Modules:
  0.0 111.4 jit_solution(12946432217852640838)
XLA Ops:
  1.3 32.2 %shard_map.113 = f32[10,16,8,128]{3,2,1,0:T(8,128)} custom-call(s32[1,1]{1,0:T(1,128)} %bitcast.163.count_ref, f32[6,24576]{1,0:T(8,128)} %st_ref.1, f32[1,24576]{1,0:T(1,128)} %bitcast.209, f32[1,24576]{1,0:T(1,128)} %bitcast.210, f32[3,24576]{1,0:T(4,128)} %vel_ref.1, f32[1,24576]{1,0:T(1,128)} %bitcast.211, s32[1,24576]{1,0:T(1,128)} %bitcast.212, ...), custom_call_target="tpu_custom_call" | custom-call | flops 24159191040 | bytes 1933312 | tf_op jit(solution)/shard_map/pallas_call | solution.py:87
  33.5 1.3 %fusion.35 = (f32[6,16,8,1]{3,2,1,0:T(8,128)S(1)}, f32[6,16,8,1]{3,2,1,0:T(8,128)S(1)}) fusion(f32[10,16,8,128]{3,2,1,0:T(8,128)} %shard_map.113), kind=kLoop, calls=%fused_computation.127 | loop fusion | bytes 12288 | tf_op jit(solution)/shard_map/slice | solution.py:281
  34.8 1.2 %copy.219 = f32[6,16,8,1]{2,1,0,3:T(8,128)} copy(f32[6,16,8,1]{3,2,1,0:T(8,128)S(1)} %get-tuple-element.83) | data formatting | bytes 6144
  36.0 1.2 %copy.220 = f32[6,16,8,1]{2,1,0,3:T(8,128)} copy(f32[6,16,8,1]{3,2,1,0:T(8,128)S(1)} %get-tuple-element.82) | data formatting | bytes 6144
  37.3 0.7 fusion.36
  38.0 0.6 slice_bitcast_fusion.12
  38.6 11.4 %shard_map.114 = (f32[6,16,128]{2,1,0:T(8,128)}, f32[6,16,128]{2,1,0:T(8,128)}, f32[6,16,8]{2,1,0:T(8,128)}, f32[6,16,8]{2,1,0:T(8,128)}, f32[6,8,128]{2,1,0:T(8,128)}, /*index=5*/f32[6,8,128]{2,1,0:T(8,128)}) custom-call(f32[6,16,128]{2,1,0:T(8,128)} %bitcast.190, f32[6,16,128]{2,1,0:T(8,128)} %bitcast.189, f32[6,16,8]{2,1,0:T(8,128)} %bitcast.187, ...), custom_call_target="tpu_custom_call" | custom-call | tf_op jit(solution)/shard_map/pallas_call | solution.py:285
  50.1 0.7 fusion.64
  50.8 0.7 slice_bitcast_fusion.28
  51.6 0.2 copy.141
  51.8 0.2 copy.144
  51.9 0.4 copy-done.4
  52.4 0.2 copy-done.3
  52.9 0.1 fusion.11
  53.0 0.2 copy.153
  53.2 0.2 copy.156
  53.5 0.1 fusion.16
  53.6 0.2 copy.164
  53.8 0.2 copy.167
  54.1 0.1 fusion.21
  54.3 0.1 fusion.61
  54.4 1.0 copy.203
  55.3 1.0 copy.204
  56.3 0.6 slice_bitcast_fusion.10
  56.9 0.6 fusion.60
  57.6 9.7 %shard_map.115 = (f32[3,16,128]{2,1,0:T(8,128)}, f32[3,16,128]{2,1,0:T(8,128)}, f32[3,16,8]{2,1,0:T(8,128)}, f32[3,16,8]{2,1,0:T(8,128)}, f32[3,8,128]{2,1,0:T(8,128)}, /*index=5*/f32[3,8,128]{2,1,0:T(8,128)}) custom-call(f32[3,16,128]{2,1,0:T(8,128)} %get-tuple-element.143.refs_0_, f32[3,16,128]{2,1,0:T(8,128)} %get-tuple-element.142.refs_1_, ...), custom_call_target="tpu_custom_call" | custom-call | tf_op jit(solution)/shard_map/pallas_call | solution.py:285
  67.3 0.7 slice_bitcast_fusion.17
  68.0 0.2 copy.174
  68.2 0.7 slice_bitcast_fusion.16
  68.9 0.2 copy.176
  69.0 0.7 slice_bitcast_fusion.18
  69.7 0.7 slice_bitcast_fusion.19
  70.4 0.7 slice.526
  71.1 0.7 slice.527
  71.9 0.8 copy-done.1
  72.7 0.1 fusion.25
  72.9 5.8 %all_gather.9 = f32[64,8,128]{2,0,1:T(8,128)S(1)} all-gather(f32[16,8,128]{2,0,1:T(8,128)S(1)} %fusion.25), channel_id=1, replica_groups=mesh['gx'=16,'gy'=8,'gz'=4] {'gz'}, dimensions={0}, use_global_device_ids=true | all-gather | bytes 327680 | tf_op jit(solution)/shard_map/all_gather | solution.py:371
  78.7 0.2 copy.180
  78.9 0.2 copy.181
  79.2 0.8 copy-done.2
  80.0 5.8 %all_gather.10 = f32[64,8,128]{2,1,0:T(8,128)S(1)} all-gather(f32[16,8,128]{2,1,0:T(8,128)S(1)} %copy-done.2), channel_id=1, replica_groups=mesh['gx'=16,'gy'=8,'gz'=4] {'gz'}, dimensions={0}, use_global_device_ids=true | all-gather | bytes 327680 | tf_op jit(solution)/shard_map/all_gather | solution.py:341
  85.9 5.9 %all_gather.11 = f32[64,8,128]{2,1,0:T(8,128)S(1)} all-gather(f32[16,8,128]{2,1,0:T(8,128)S(1)} %copy-done.1), channel_id=1, replica_groups=mesh['gx'=16,'gy'=8,'gz'=4] {'gz'}, dimensions={0}, use_global_device_ids=true | all-gather | bytes 327680 | tf_op jit(solution)/shard_map/all_gather | solution.py:340
  91.7 0.2 fusion.29
  92.4 0.4 fusion
  93.0 0.4 multiply_add_fusion.7
  93.5 0.2 multiply_add_fusion.6
  93.7 0.3 multiply_add_fusion.5
  94.2 0.2 multiply_add_fusion.4
  94.4 0.3 multiply_add_fusion.3
  94.8 0.1 multiply_add_fusion.2
  95.0 0.3 multiply_add_fusion.1
  95.4 0.2 pad_multiply_fusion
  95.6 0.1 copy_bitcast_fusion
  96.0 0.8 copy.209
  96.7 0.8 copy.210
  97.5 0.6 slice_bitcast_fusion.14
  98.1 9.4 %shard_map.116 = (f32[16,128]{1,0:T(8,128)}, f32[16,128]{1,0:T(8,128)}, f32[16,8]{1,0:T(8,128)}, f32[16,8]{1,0:T(8,128)}) custom-call(f32[16,128]{1,0:T(8,128)} %get-tuple-element.153.refs_0_, f32[16,128]{1,0:T(8,128)} %get-tuple-element.152.refs_1_, f32[16,8]{1,0:T(8,128)} %bitcast.195, f32[16,8]{1,0:T(8,128)} %bitcast.196), custom_call_target="tpu_custom_call" | custom-call | tf_op jit(solution)/shard_map/pallas_call | solution.py:285
  107.5 0.7 copy-done.8
  108.2 0.7 copy-done.7
  108.9 0.2 copy.186
  109.1 0.5 copy-done.6
  109.6 0.2 copy.188
  110.0 0.7 copy.189
  110.8 0.7 copy.190
  (90 shorter events, 2.4 us)
Async XLA Ops:
  34.8 2.5 %copy-start = (f32[10,16,8,128]{3,2,1,0:T(8,128)S(1)}, f32[10,16,8,128]{3,2,1,0:T(8,128)}, u32[]{:S(2)}) copy-start(f32[10,16,8,128]{3,2,1,0:T(8,128)} %shard_map.113) | copy-start | bytes 1966084
  50.0 0.8 copy-start.5
  51.6 0.8 copy-start.4
  51.8 0.8 copy-start.3
  71.9 0.8 copy-start.1
  79.1 0.8 copy-start.2
  107.5 0.7 copy-start.8
  107.5 0.7 copy-start.9
  108.2 0.7 copy-start.7
  108.9 0.7 copy-start.6

commit v4 on v3

--- a/solution.py
+++ b/solution.py
@@ -20,12 +20,13 @@
 N_COLS = 512
 
 
-def _split3(v):
+SPLITS = 2
+
+
+def _split(v):
     hi = v.astype(jnp.bfloat16)
-    rest = v - hi.astype(jnp.float32)
-    mid = rest.astype(jnp.bfloat16)
-    lo = (rest - mid.astype(jnp.float32)).astype(jnp.bfloat16)
-    return [hi, mid, lo]
+    lo = (v - hi.astype(jnp.float32)).astype(jnp.bfloat16)
+    return [hi, lo]
 
 
 def sums_kernel(count_ref, st_ref, ms_ref, cons_ref, vel_ref, w_ref, cell_ref, yf_ref, out_ref, acc_ref):
@@ -58,7 +59,7 @@
         zero = jnp.zeros((M_ROWS, CHUNK), jnp.bfloat16)
         pieces = []
         for v in values:
-            for part in _split3(v):
+            for part in _split(v):
                 pieces.append(jnp.where(m_mask, jnp.broadcast_to(part, (M_ROWS, CHUNK)), zero))
         lhs = jnp.concatenate(pieces, axis=0)
         one_hot = jnp.where(
@@ -72,11 +73,11 @@
     lax.fori_loop(0, chunks, body, 0)
     for comp in range(10):
         for level in range(16):
-            rows = pl.ds((comp * 3) * M_ROWS + (level >> 2) * 8, 8)
+            rows = pl.ds((comp * SPLITS) * M_ROWS + (level >> 2) * 8, 8)
             lanes = pl.ds((level & 3) * 128, 128)
             total = acc_ref[rows, lanes]
-            for s in (1, 2):
-                total = total + acc_ref[pl.ds((comp * 3 + s) * M_ROWS + (level >> 2) * 8, 8), lanes]
+            for s in range(1, SPLITS):
+                total = total + acc_ref[pl.ds((comp * SPLITS + s) * M_ROWS + (level >> 2) * 8, 8), lanes]
             out_ref[comp, level] = total
 
 
@@ -89,9 +90,9 @@
         out_shape=jax.ShapeDtypeStruct((10, levels, extent, breadth), jnp.float32),
         in_specs=[pl.BlockSpec(memory_space=pltpu.SMEM)] + [vmem] * 7,
         out_specs=vmem,
-        scratch_shapes=[pltpu.VMEM((30 * M_ROWS, N_COLS), jnp.float32)],
+        scratch_shapes=[pltpu.VMEM((10 * SPLITS * M_ROWS, N_COLS), jnp.float32)],
         cost_estimate=pl.CostEstimate(
-            flops=2 * 30 * M_ROWS * N_COLS * n, bytes_accessed=13 * 4 * n + 10 * 4 * levels * extent * breadth,
+            flops=2 * 10 * SPLITS * M_ROWS * N_COLS * n, bytes_accessed=13 * 4 * n + 10 * 4 * levels * extent * breadth,
             transcendentals=3 * n,
         ),
     )(

time: 113 us -> 104 us (0.920)
  Pallas kernels: 62.8 us -> 54.4 us
    pallas_call x1, Pallas kernels: 32.2 us -> 23.8 us  [cell_sums_of(): pl.pallas_call(sums_kernel, out_shape=jax.ShapeDtypeStruct((10, levels, e...]
where the time goes in v4:
time: 104 us; the launch traced here: 103 us
  Pallas kernels  54.4 us (52%)
  local copies, waits for them, and re-layouts  25.8 us (25%)
  blocking collectives  17.5 us (17%)
  other arithmetic  3.31 us (3%)
  between operations  2.02 us (2%)
    pallas_call x3, Pallas kernels, exchange(): pl.pallas_call(functools.partial(halo_kernel, axes, sizes), out_shape=[ja...  30.6 us
    pallas_call x1, Pallas kernels, cell_sums_of(): pl.pallas_call(sums_kernel, out_shape=jax.ShapeDtypeStruct((10, levels, e...  23.8 us
    unnamed x58, local copies, waits for them, and re-layouts  8.88 us
    all_gather x1, blocking collectives, shards(): all_porosity = lax.all_gather(porosity, 'gz', axis=0, tiled=True)  5.87 us
    all_gather x1, blocking collectives, shards(): all_permeability = lax.all_gather(permeability, 'gz', axis=0, tiled=True)  5.85 us
    all_gather x1, blocking collectives, shards(): all_right = lax.all_gather(right_side, 'gz', axis=0, tiled=True)  5.79 us
    squeeze x5, local copies, waits for them, and re-layouts, exchange(): sends.append(lax.index_in_dim(cells, size - 1, axis=dim, keepdims=False))  3.58 us
    concatenate x14, local copies, waits for them, and re-layouts, along(): jnp.concatenate([lower, lax.slice_in_dim(cells, 0, size - 1, axis=dim)],...  3.2 us

profile of v4, /device:TPU:102, one launch (start us, length us, event | category | flops | bytes accessed | tf_op | source)
XLA Modules:
  0.0 103.1 jit_solution(18193252535698358901)
XLA Ops:
  1.3 23.8 %shard_map.113 = f32[10,16,8,128]{3,2,1,0:T(8,128)} custom-call(s32[1,1]{1,0:T(1,128)} %bitcast.163.count_ref, f32[6,24576]{1,0:T(8,128)} %st_ref.1, f32[1,24576]{1,0:T(1,128)} %bitcast.209, f32[1,24576]{1,0:T(1,128)} %bitcast.210, f32[3,24576]{1,0:T(4,128)} %vel_ref.1, f32[1,24576]{1,0:T(1,128)} %bitcast.211, s32[1,24576]{1,0:T(1,128)} %bitcast.212, ...), custom_call_target="tpu_custom_call" | custom-call | flops 16106127360 | bytes 1933312 | tf_op jit(solution)/shard_map/pallas_call | solution.py:88
  25.1 1.3 %fusion.35 = (f32[6,16,8,1]{3,2,1,0:T(8,128)S(1)}, f32[6,16,8,1]{3,2,1,0:T(8,128)S(1)}) fusion(f32[10,16,8,128]{3,2,1,0:T(8,128)} %shard_map.113), kind=kLoop, calls=%fused_computation.127 | loop fusion | bytes 12288 | tf_op jit(solution)/shard_map/slice | solution.py:282
  26.4 1.2 %copy.219 = f32[6,16,8,1]{2,1,0,3:T(8,128)} copy(f32[6,16,8,1]{3,2,1,0:T(8,128)S(1)} %get-tuple-element.83) | data formatting | bytes 6144
  27.6 1.2 %copy.220 = f32[6,16,8,1]{2,1,0,3:T(8,128)} copy(f32[6,16,8,1]{3,2,1,0:T(8,128)S(1)} %get-tuple-element.82) | data formatting | bytes 6144
  28.9 0.7 fusion.36
  29.6 0.6 slice_bitcast_fusion.12
  30.2 11.4 %shard_map.114 = (f32[6,16,128]{2,1,0:T(8,128)}, f32[6,16,128]{2,1,0:T(8,128)}, f32[6,16,8]{2,1,0:T(8,128)}, f32[6,16,8]{2,1,0:T(8,128)}, f32[6,8,128]{2,1,0:T(8,128)}, /*index=5*/f32[6,8,128]{2,1,0:T(8,128)}) custom-call(f32[6,16,128]{2,1,0:T(8,128)} %bitcast.190, f32[6,16,128]{2,1,0:T(8,128)} %bitcast.189, f32[6,16,8]{2,1,0:T(8,128)} %bitcast.187, ...), custom_call_target="tpu_custom_call" | custom-call | tf_op jit(solution)/shard_map/pallas_call | solution.py:286
  41.7 0.7 fusion.64
  42.5 0.7 slice_bitcast_fusion.28
  43.2 0.2 copy.141
  43.4 0.2 copy.144
  43.6 0.4 copy-done.4
  44.0 0.2 copy-done.3
  44.5 0.1 fusion.11
  44.7 0.2 copy.153
  44.8 0.2 copy.156
  45.1 0.1 fusion.16
  45.3 0.2 copy.164
  45.4 0.2 copy.167
  45.7 0.1 fusion.21
  45.9 0.1 fusion.61
  46.0 1.0 copy.203
  47.0 1.0 copy.204
  47.9 0.6 slice_bitcast_fusion.10
  48.5 0.6 fusion.60
  49.2 9.7 %shard_map.115 = (f32[3,16,128]{2,1,0:T(8,128)}, f32[3,16,128]{2,1,0:T(8,128)}, f32[3,16,8]{2,1,0:T(8,128)}, f32[3,16,8]{2,1,0:T(8,128)}, f32[3,8,128]{2,1,0:T(8,128)}, /*index=5*/f32[3,8,128]{2,1,0:T(8,128)}) custom-call(f32[3,16,128]{2,1,0:T(8,128)} %get-tuple-element.143.refs_0_, f32[3,16,128]{2,1,0:T(8,128)} %get-tuple-element.142.refs_1_, ...), custom_call_target="tpu_custom_call" | custom-call | tf_op jit(solution)/shard_map/pallas_call | solution.py:286
  58.9 0.7 slice_bitcast_fusion.17
  59.6 0.2 copy.174
  59.8 0.7 slice_bitcast_fusion.16
  60.5 0.2 copy.176
  60.7 0.7 slice_bitcast_fusion.18
  61.4 0.7 slice_bitcast_fusion.19
  62.1 0.7 slice.526
  62.7 0.7 slice.527
  63.5 0.8 copy-done.1
  64.4 0.1 fusion.25
  64.5 5.8 %all_gather.9 = f32[64,8,128]{2,0,1:T(8,128)S(1)} all-gather(f32[16,8,128]{2,0,1:T(8,128)S(1)} %fusion.25), channel_id=1, replica_groups=mesh['gx'=16,'gy'=8,'gz'=4] {'gz'}, dimensions={0}, use_global_device_ids=true | all-gather | bytes 327680 | tf_op jit(solution)/shard_map/all_gather | solution.py:372
  70.3 0.2 copy.180
  70.6 0.2 copy.181
  70.8 0.8 copy-done.2
  71.6 5.8 %all_gather.10 = f32[64,8,128]{2,1,0:T(8,128)S(1)} all-gather(f32[16,8,128]{2,1,0:T(8,128)S(1)} %copy-done.2), channel_id=1, replica_groups=mesh['gx'=16,'gy'=8,'gz'=4] {'gz'}, dimensions={0}, use_global_device_ids=true | all-gather | bytes 327680 | tf_op jit(solution)/shard_map/all_gather | solution.py:342
  77.5 5.9 %all_gather.11 = f32[64,8,128]{2,1,0:T(8,128)S(1)} all-gather(f32[16,8,128]{2,1,0:T(8,128)S(1)} %copy-done.1), channel_id=1, replica_groups=mesh['gx'=16,'gy'=8,'gz'=4] {'gz'}, dimensions={0}, use_global_device_ids=true | all-gather | bytes 327680 | tf_op jit(solution)/shard_map/all_gather | solution.py:341
  83.3 0.2 fusion.29
  84.0 0.4 fusion
  84.6 0.4 multiply_add_fusion.7
  85.1 0.2 multiply_add_fusion.6
  85.4 0.3 multiply_add_fusion.5
  85.8 0.2 multiply_add_fusion.4
  86.1 0.3 multiply_add_fusion.3
  86.5 0.1 multiply_add_fusion.2
  86.7 0.3 multiply_add_fusion.1
  87.0 0.2 pad_multiply_fusion
  87.3 0.1 copy_bitcast_fusion
  87.6 0.8 copy.209
  88.3 0.8 copy.210
  89.1 0.6 slice_bitcast_fusion.14
  89.7 9.4 %shard_map.116 = (f32[16,128]{1,0:T(8,128)}, f32[16,128]{1,0:T(8,128)}, f32[16,8]{1,0:T(8,128)}, f32[16,8]{1,0:T(8,128)}) custom-call(f32[16,128]{1,0:T(8,128)} %get-tuple-element.153.refs_0_, f32[16,128]{1,0:T(8,128)} %get-tuple-element.152.refs_1_, f32[16,8]{1,0:T(8,128)} %bitcast.195, f32[16,8]{1,0:T(8,128)} %bitcast.196), custom_call_target="tpu_custom_call" | custom-call | tf_op jit(solution)/shard_map/pallas_call | solution.py:286
  99.2 0.7 copy-done.8
  99.9 0.7 copy-done.7
  100.5 0.2 copy.186
  100.7 0.5 copy-done.6
  101.2 0.2 copy.188
  101.7 0.7 copy.189
  102.4 0.7 copy.190
  (90 shorter events, 2.4 us)
Async XLA Ops:
  26.4 2.5 %copy-start = (f32[10,16,8,128]{3,2,1,0:T(8,128)S(1)}, f32[10,16,8,128]{3,2,1,0:T(8,128)}, u32[]{:S(2)}) copy-start(f32[10,16,8,128]{3,2,1,0:T(8,128)} %shard_map.113) | copy-start | bytes 1966084
  41.7 0.8 copy-start.5
  43.2 0.8 copy-start.4
  43.4 0.8 copy-start.3
  63.5 0.8 copy-start.1
  70.7 0.8 copy-start.2
  99.1 0.7 copy-start.8
  99.1 0.7 copy-start.9
  99.8 0.7 copy-start.7
  100.5 0.7 copy-start.6

commit v5 on v4

--- a/solution.py
+++ b/solution.py
@@ -223,26 +223,41 @@
 MESH_AXES = ("gx", "gy", "gz")
 
 
-def halo_kernel(sides, sizes, *refs):
+def halo_kernel(sides, sizes, gathered, group, *refs):
     count = len(sides)
     sends = refs[:2 * count]
-    recvs = refs[2 * count:4 * count]
-    send_sem, recv_sem = refs[4 * count:]
+    gins = refs[2 * count:2 * count + gathered]
+    recvs = refs[2 * count + gathered:4 * count + gathered]
+    gouts = refs[4 * count + gathered:4 * count + 2 * gathered]
+    send_sem, recv_sem, gsend_sem, grecv_sem = refs[4 * count + 2 * gathered:]
     me = {a: lax.axis_index(a) for a in MESH_AXES}
 
     def peer(axis, delta):
         return tuple(me[a] + delta if a == axis else me[a] for a in MESH_AXES)
+
+    def across(level):
+        return tuple(level if a == "gz" else me[a] for a in MESH_AXES)
 
     links = []
     for i, axis in enumerate(sides):
         links.append((axis, -1, me[axis] > 0, 2 * i, 2 * i + 1))
         links.append((axis, 1, me[axis] < sizes[i] - 1, 2 * i + 1, 2 * i))
     barrier = pltpu.get_barrier_semaphore()
+    peers = 0
     for axis, delta, present, _, _ in links:
+        if gathered and axis == "gz":
+            continue
+        peers = peers + present.astype(jnp.int32)
+
         @pl.when(present)
         def _():
             pl.semaphore_signal(barrier, 1, device_id=peer(axis, delta), device_id_type=pl.DeviceIdType.MESH)
-    peers = sum(present.astype(jnp.int32) for _, _, present, _, _ in links)
+    if gathered:
+        for d in range(1, group):
+            pl.semaphore_signal(
+                barrier, 1, device_id=across(lax.rem(me["gz"] + d, group)), device_id_type=pl.DeviceIdType.MESH
+            )
+        peers = peers + (group - 1)
     pl.semaphore_wait(barrier, peers)
     copies = []
     for axis, delta, present, src, dst in links:
@@ -255,6 +270,19 @@
         @pl.when(present)
         def _():
             copy.start()
+    gcopies = []
+    for j in range(gathered):
+        for d in range(1, group):
+            slot = j * (group - 1) + d - 1
+            copy = pltpu.make_async_remote_copy(
+                src_ref=gins[j], dst_ref=gouts[j].at[me["gz"]], send_sem=gsend_sem.at[slot],
+                recv_sem=grecv_sem.at[slot], device_id=across(lax.rem(me["gz"] + d, group)),
+                device_id_type=pl.DeviceIdType.MESH,
+            )
+            copy.start()
+            gcopies.append(copy)
+    for j in range(gathered):
+        gouts[j][me["gz"]] = gins[j][...]
     for axis, delta, present, src, dst in links:
         incoming = pltpu.make_async_remote_copy(
             src_ref=sends[dst], dst_ref=recvs[src], send_sem=send_sem.at[dst], recv_sem=recv_sem.at[src],
@@ -268,13 +296,24 @@
         @pl.when(jnp.logical_not(present))
         def _():
             recvs[src][...] = jnp.zeros(recvs[src].shape, recvs[src].dtype)
+    for j in range(gathered):
+        for d in range(1, group):
+            slot = j * (group - 1) + d - 1
+            origin = lax.rem(me["gz"] + group - d, group)
+            incoming = pltpu.make_async_remote_copy(
+                src_ref=gins[j], dst_ref=gouts[j].at[origin], send_sem=gsend_sem.at[slot],
+                recv_sem=grecv_sem.at[slot], device_id=across(origin), device_id_type=pl.DeviceIdType.MESH,
+            )
+            incoming.wait_recv()
     for present, copy in copies:
         @pl.when(present)
         def _():
             copy.wait_send()
-
-
-def exchange(cells, sides, collective):
+    for copy in gcopies:
+        copy.wait_send()
+
+
+def exchange(cells, sides, collective, gathers=()):
     sends = []
     for axis, dim in sides:
         size = cells.shape[dim]
@@ -282,19 +321,28 @@
         sends.append(lax.index_in_dim(cells, size - 1, axis=dim, keepdims=False))
     axes = tuple(axis for axis, _ in sides)
     sizes = tuple(lax.axis_size(axis) for axis in axes)
+    group = lax.axis_size("gz")
     vmem = pl.BlockSpec(memory_space=pltpu.VMEM)
-    recvs = pl.pallas_call(
-        functools.partial(halo_kernel, axes, sizes),
-        out_shape=[jax.ShapeDtypeStruct(s.shape, s.dtype) for s in sends],
-        in_specs=[vmem] * len(sends),
-        out_specs=[vmem] * len(sends),
-        scratch_shapes=[pltpu.SemaphoreType.DMA((len(sends),)), pltpu.SemaphoreType.DMA((len(sends),))],
+    slots = max(1, len(gathers) * (group - 1))
+    outs = pl.pallas_call(
+        functools.partial(halo_kernel, axes, sizes, len(gathers), group),
+        out_shape=[jax.ShapeDtypeStruct(s.shape, s.dtype) for s in sends]
+        + [jax.ShapeDtypeStruct((group,) + g.shape, g.dtype) for g in gathers],
+        in_specs=[vmem] * (len(sends) + len(gathers)),
+        out_specs=[vmem] * (len(sends) + len(gathers)),
+        scratch_shapes=[
+            pltpu.SemaphoreType.DMA((max(1, len(sends)),)), pltpu.SemaphoreType.DMA((max(1, len(sends)),)),
+            pltpu.SemaphoreType.DMA((slots,)), pltpu.SemaphoreType.DMA((slots,)),
+        ],
         compiler_params=pltpu.CompilerParams(collective_id=collective, has_side_effects=True),
-    )(*sends)
-    return {
+    )(*sends, *gathers)
+    recvs = outs[:len(sends)]
+    faces = {
         dim: (jnp.expand_dims(recvs[2 * i], dim), jnp.expand_dims(recvs[2 * i + 1], dim))
         for i, (axis, dim) in enumerate(sides)
     }
+    stacked = [g.reshape((group * g.shape[1],) + g.shape[2:]) for g in outs[len(sends):]]
+    return faces, stacked
 
 
 def face_from(part, axis, from_lower):
@@ -338,16 +386,14 @@
     permeability,
 ):
     levels, extent, breadth = porosity.shape
-    all_porosity = lax.all_gather(porosity, "gz", axis=0, tiled=True)
-    all_permeability = lax.all_gather(permeability, "gz", axis=0, tiled=True)
-    height = all_porosity.shape[0]
     cell_sums = cell_sums_of(
         stress_trial, mean_stress, consolidation, point_velocity, point_weight, point_cell,
         yield_flag, point_count, levels, extent, breadth,
     )
     sides = (("gx", 2), ("gy", 3), ("gz", 1))
     stress_sums = cell_sums[:6]
-    sf = exchange(stress_sums, sides, 0)
+    sf, (all_porosity, all_permeability) = exchange(stress_sums, sides, 0, (porosity, permeability))
+    height = all_porosity.shape[0]
     d_x = lambda c: along(stress_sums[c:c + 1], {2: (sf[2][0][c:c + 1], sf[2][1][c:c + 1])}, 2)[0]
     d_y = lambda c: along(stress_sums[c:c + 1], {3: (sf[3][0][c:c + 1], sf[3][1][c:c + 1])}, 3)[0]
     d_z = lambda c: along(stress_sums[c:c + 1], {1: (sf[1][0][c:c + 1], sf[1][1][c:c + 1])}, 1)[0]
@@ -362,14 +408,14 @@
             (cell_sums[8] + time_step * force_z) / floored,
         ]
     )
-    vf = exchange(velocity, sides, 1)
+    vf, _ = exchange(velocity, sides, 1)
     dilation = (
         along(velocity[0:1], {2: (vf[2][0][0:1], vf[2][1][0:1])}, 2)[0]
         + along(velocity[1:2], {3: (vf[3][0][1:2], vf[3][1][1:2])}, 3)[0]
         + along(velocity[2:3], {1: (vf[1][0][2:3], vf[1][1][2:3])}, 1)[0]
     )
     right_side = -source_rate * (1.0 - porosity) * dilation
-    all_right = lax.all_gather(right_side, "gz", axis=0, tiled=True)
+    _, (all_right,) = exchange(right_side, (), 3, (right_side,))
     zero_level = jnp.zeros((1, extent, breadth), jnp.float32)
     level_above = jnp.concatenate([all_permeability[1:], zero_level], axis=0)
     level_below = jnp.concatenate([zero_level, all_permeability[:-1]], axis=0)
@@ -390,7 +436,7 @@
         jnp.concatenate([zero_level, solved, zero_level], axis=0), first, levels + 2, axis=0
     )
     pressure = around[1:-1]
-    pf = exchange(pressure, (("gx", 1), ("gy", 2)), 2)
+    pf, _ = exchange(pressure, (("gx", 1), ("gy", 2)), 2)
     gradient = jnp.stack(
         [
             along(pressure, pf, 1),

time: 104 us -> 100 us (0.962)
  the two profiles are of different devices: /device:TPU:102 before, /device:TPU:121 now
where the time goes in v5:
time: 100 us; the launch traced here: 99.2 us
  Pallas kernels  64.9 us (65%)
  local copies, waits for them, and re-layouts  28.9 us (29%)
  other arithmetic  3.37 us (3%)
  between operations  2 us (2%)
    pallas_call x4, Pallas kernels, exchange(): pl.pallas_call(functools.partial(halo_kernel, axes, sizes, len(gathers),...  41.1 us
    pallas_call x1, Pallas kernels, cell_sums_of(): pl.pallas_call(sums_kernel, out_shape=jax.ShapeDtypeStruct((10, levels, e...  23.8 us
    unnamed x61, local copies, waits for them, and re-layouts  12.3 us
    squeeze x5, local copies, waits for them, and re-layouts, exchange(): sends.append(lax.index_in_dim(cells, size - 1, axis=dim, keepdims=False))  3.57 us
    concatenate x14, local copies, waits for them, and re-layouts, along(): jnp.concatenate([lower, lax.slice_in_dim(cells, 0, size - 1, axis=dim)],...  3.26 us
    slice x5, local copies, waits for them, and re-layouts, exchange(): sends.append(lax.index_in_dim(cells, size - 1, axis=dim, keepdims=False))  2.8 us
    concatenate x7, local copies, waits for them, and re-layouts, along(): jnp.concatenate([lax.slice_in_dim(cells, 1, size, axis=dim), upper], axis...  2.28 us

profile of v5, /device:TPU:121, one launch (start us, length us, event | category | flops | bytes accessed | tf_op | source)
XLA Modules:
  0.0 99.2 jit_solution(474705514602034588)
XLA Ops:
  1.3 23.8 %shard_map.113 = f32[10,16,8,128]{3,2,1,0:T(8,128)} custom-call(s32[1,1]{1,0:T(1,128)} %bitcast.165.count_ref, f32[6,24576]{1,0:T(8,128)} %st_ref.1, f32[1,24576]{1,0:T(1,128)} %bitcast.211, f32[1,24576]{1,0:T(1,128)} %bitcast.212, f32[3,24576]{1,0:T(4,128)} %vel_ref.1, f32[1,24576]{1,0:T(1,128)} %bitcast.213, s32[1,24576]{1,0:T(1,128)} %bitcast.214, ...), custom_call_target="tpu_custom_call" | custom-call | flops 16106127360 | bytes 1933312 | tf_op jit(solution)/shard_map/pallas_call | solution.py:88
  25.1 1.3 %fusion.34 = (f32[6,16,8,1]{3,2,1,0:T(8,128)S(1)}, f32[6,16,8,1]{3,2,1,0:T(8,128)S(1)}) fusion(f32[10,16,8,128]{3,2,1,0:T(8,128)} %shard_map.113), kind=kLoop, calls=%fused_computation.128 | loop fusion | bytes 12288 | tf_op jit(solution)/shard_map/slice | solution.py:321
  26.4 1.2 %copy.157 = f32[6,16,8,1]{2,1,0,3:T(8,128)} copy(f32[6,16,8,1]{3,2,1,0:T(8,128)S(1)} %get-tuple-element.85) | data formatting | bytes 6144
  27.7 1.2 %copy.158 = f32[6,16,8,1]{2,1,0,3:T(8,128)} copy(f32[6,16,8,1]{3,2,1,0:T(8,128)S(1)} %get-tuple-element.84) | data formatting | bytes 6144
  28.9 0.7 fusion.35
  29.6 0.6 slice_bitcast_fusion.12
  30.2 14.8 %shard_map.114 = (f32[6,16,128]{2,1,0:T(8,128)}, f32[6,16,128]{2,1,0:T(8,128)}, f32[6,16,8]{2,1,0:T(8,128)}, f32[6,16,8]{2,1,0:T(8,128)}, f32[6,8,128]{2,1,0:T(8...) custom-call(f32[6,16,128]{2,1,0:T(8,128)} %bitcast.192, ...), custom_call_target="tpu_custom_call" | custom-call | tf_op jit(solution)/shard_map/pallas_call | solution.py:327
  45.0 0.8 slice_bitcast_fusion.28
  45.8 0.2 copy.81
  46.0 0.2 copy.84
  46.1 0.4 copy-done.6
  46.6 0.2 copy-done.5
  46.8 0.7 copy-done.11
  47.9 0.1 fusion.10
  48.0 0.2 copy.93
  48.2 0.2 copy.96
  48.5 0.1 fusion.15
  48.6 0.2 copy.104
  48.8 0.2 copy.107
  49.1 0.1 fusion.20
  49.2 0.1 fusion.60
  49.3 1.0 copy.141
  50.3 1.0 copy.142
  51.2 0.6 slice_bitcast_fusion.10
  51.9 0.6 fusion.59
  52.5 9.5 %shard_map.115 = (f32[3,16,128]{2,1,0:T(8,128)}, f32[3,16,128]{2,1,0:T(8,128)}, f32[3,16,8]{2,1,0:T(8,128)}, f32[3,16,8]{2,1,0:T(8,128)}, f32[3,8,128]{2,1,0:T(8,128)}, /*index=5*/f32[3,8,128]{2,1,0:T(8,128)}) custom-call(f32[3,16,128]{2,1,0:T(8,128)} %get-tuple-element.145.refs_0_, f32[3,16,128]{2,1,0:T(8,128)} %get-tuple-element.144.refs_1_, ...), custom_call_target="tpu_custom_call" | custom-call | tf_op jit(solution)/shard_map/pallas_call | solution.py:327
  62.0 0.7 slice_bitcast_fusion.17
  62.7 0.2 copy.114
  62.8 0.7 slice_bitcast_fusion.16
  63.5 0.2 copy.116
  63.7 0.7 slice_bitcast_fusion.18
  64.4 0.7 slice_bitcast_fusion.19
  65.1 0.7 slice.520
  65.8 0.7 slice.521
  66.6 0.8 copy-done.4
  67.4 0.1 fusion.24
  67.5 0.7 copy.119.refs_0_
  68.2 8.3 %shard_map.116 = f32[4,16,8,128]{3,2,1,0:T(8,128)} custom-call(f32[16,8,128]{2,1,0:T(8,128)} %copy.119.refs_0_), custom_call_target="tpu_custom_call" | custom-call | tf_op jit(solution)/shard_map/pallas_call | solution.py:327
  76.5 1.0 %copy.228 = f32[8,8,8,128]{3,1,2,0:T(8,128)S(1)} copy(f32[8,8,8,128]{3,2,1,0:T(8,128)} %bitcast.175) | data formatting | bytes 524288
  77.5 0.9 copy-done.2
  78.5 0.9 copy-done.3
  79.4 0.2 fusion.28
  80.1 0.9 copy-done.1
  81.0 0.4 fusion
  81.6 0.4 multiply_add_fusion.7
  82.1 0.2 multiply_add_fusion.6
  82.3 0.3 multiply_add_fusion.5
  82.8 0.2 multiply_add_fusion.4
  83.0 0.3 multiply_add_fusion.3
  83.5 0.1 multiply_add_fusion.2
  83.7 0.3 multiply_add_fusion.1
  84.0 0.2 pad_multiply_fusion
  84.3 0.1 copy_bitcast_fusion.1
  84.6 0.8 copy.147
  85.3 0.8 copy.148
  86.1 0.6 slice_bitcast_fusion.14
  86.7 8.6 %shard_map.117 = (f32[16,128]{1,0:T(8,128)}, f32[16,128]{1,0:T(8,128)}, f32[16,8]{1,0:T(8,128)}, f32[16,8]{1,0:T(8,128)}) custom-call(f32[16,128]{1,0:T(8,128)} %get-tuple-element.155.refs_0_, f32[16,128]{1,0:T(8,128)} %get-tuple-element.154.refs_1_, f32[16,8]{1,0:T(8,128)} %bitcast.197, f32[16,8]{1,0:T(8,128)} %bitcast.198), custom_call_target="tpu_custom_call" | custom-call | tf_op jit(solution)/shard_map/pallas_call | solution.py:327
  95.3 0.7 copy-done.9
  96.0 0.7 copy-done.8
  96.7 0.2 copy.124
  96.9 0.5 copy-done.7
  97.4 0.2 copy.126
  97.8 0.7 copy.127
  98.6 0.7 copy.128
  (91 shorter events, 2.2 us)
Async XLA Ops:
  26.4 2.5 %copy-start = (f32[10,16,8,128]{3,2,1,0:T(8,128)S(1)}, f32[10,16,8,128]{3,2,1,0:T(8,128)}, u32[]{:S(2)}) copy-start(f32[10,16,8,128]{3,2,1,0:T(8,128)} %shard_map.113) | copy-start | bytes 1966084
  45.8 0.8 copy-start.6
  46.0 0.8 copy-start.5
  46.8 0.7 copy-start.11
  46.8 0.8 copy-start.12
  66.6 0.8 copy-start.4
  77.5 1.0 copy-start.2
  78.4 0.9 copy-start.3
  80.0 1.0 copy-start.1
  95.3 0.7 copy-start.9
  95.3 0.7 copy-start.10
  96.0 0.7 copy-start.8
  96.7 0.7 copy-start.7

commit v6 on v5

--- a/solution.py
+++ b/solution.py
@@ -345,6 +345,106 @@
     return faces, stacked
 
 
+def column_kernel(sizes, group, v_ref, xlo_s, xhi_s, ylo_s, yhi_s, v_out, xlo_o, xhi_o, ylo_o, yhi_o, send_sem, recv_sem):
+    i, j, k = (lax.axis_index(a) for a in MESH_AXES)
+    nx, ny = sizes
+    mesh_id = pl.DeviceIdType.MESH
+    sides = (
+        (i > 0, (-1, 0), xlo_s, xhi_o, xlo_o, 1),
+        (i < nx - 1, (1, 0), xhi_s, xlo_o, xhi_o, 2),
+        (j > 0, (0, -1), ylo_s, yhi_o, ylo_o, 3),
+        (j < ny - 1, (0, 1), yhi_s, ylo_o, yhi_o, 4),
+    )
+    barrier = pltpu.get_barrier_semaphore()
+    for d in range(1, group):
+        pl.semaphore_signal(barrier, 1, device_id=(i, j, lax.rem(k + d, group)), device_id_type=mesh_id)
+    peers = group - 1
+    for present, (di, dj), _, _, _, _ in sides:
+        peers = peers + group * present.astype(jnp.int32)
+        for kk in range(group):
+            @pl.when(present)
+            def _():
+                pl.semaphore_signal(barrier, 1, device_id=(i + di, j + dj, kk), device_id_type=mesh_id)
+    pl.semaphore_wait(barrier, peers)
+    block_copies = []
+    for d in range(1, group):
+        copy = pltpu.make_async_remote_copy(
+            src_ref=v_ref, dst_ref=v_out.at[:, k], send_sem=send_sem.at[d], recv_sem=recv_sem.at[d],
+            device_id=(i, j, lax.rem(k + d, group)), device_id_type=mesh_id,
+        )
+        copy.start()
+        block_copies.append(copy)
+    face_copies = []
+    for present, (di, dj), face, far_out, _, base in sides:
+        for kk in range(group):
+            copy = pltpu.make_async_remote_copy(
+                src_ref=face, dst_ref=far_out.at[:, k], send_sem=send_sem.at[base * group + kk],
+                recv_sem=recv_sem.at[base * group + k], device_id=(i + di, j + dj, kk), device_id_type=mesh_id,
+            )
+            face_copies.append((present, copy))
+
+            @pl.when(present)
+            def _():
+                copy.start()
+    v_out[:, k] = v_ref[...]
+    for d in range(1, group):
+        origin = lax.rem(k + group - d, group)
+        incoming = pltpu.make_async_remote_copy(
+            src_ref=v_ref, dst_ref=v_out.at[:, origin], send_sem=send_sem.at[d], recv_sem=recv_sem.at[d],
+            device_id=(i, j, origin), device_id_type=mesh_id,
+        )
+        incoming.wait_recv()
+    for index, (present, (di, dj), face, _, near_out, base) in enumerate(sides):
+        partner = sides[index ^ 1]
+        for kk in range(group):
+            incoming = pltpu.make_async_remote_copy(
+                src_ref=partner[2], dst_ref=near_out.at[:, kk], send_sem=send_sem.at[partner[5] * group + kk],
+                recv_sem=recv_sem.at[partner[5] * group + kk], device_id=(i + di, j + dj, kk),
+                device_id_type=mesh_id,
+            )
+
+            @pl.when(present)
+            def _():
+                incoming.wait_recv()
+
+        @pl.when(jnp.logical_not(present))
+        def _():
+            near_out[...] = jnp.zeros(near_out.shape, near_out.dtype)
+    for copy in block_copies:
+        copy.wait_send()
+    for present, copy in face_copies:
+        @pl.when(present)
+        def _():
+            copy.wait_send()
+
+
+def column_exchange(cells, collective):
+    chans, levels, extent, breadth = cells.shape
+    group = lax.axis_size("gz")
+    sizes = (lax.axis_size("gx"), lax.axis_size("gy"))
+    sends = [
+        cells[:, :, 0, :], cells[:, :, extent - 1, :], cells[:, :, :, 0], cells[:, :, :, breadth - 1],
+    ]
+    vmem = pl.BlockSpec(memory_space=pltpu.VMEM)
+    shapes = [(chans, group, levels, extent, breadth)] + [(chans, group) + s.shape[1:] for s in sends]
+    outs = pl.pallas_call(
+        functools.partial(column_kernel, sizes, group),
+        out_shape=[jax.ShapeDtypeStruct(s, cells.dtype) for s in shapes],
+        in_specs=[vmem] * 5,
+        out_specs=[vmem] * 5,
+        scratch_shapes=[pltpu.SemaphoreType.DMA((5 * group,)), pltpu.SemaphoreType.DMA((5 * group,))],
+        compiler_params=pltpu.CompilerParams(collective_id=collective, has_side_effects=True),
+    )(cells, *sends)
+    height = group * levels
+    whole = outs[0].reshape(chans, height, extent, breadth)
+    xlo, xhi, ylo, yhi = (o.reshape((chans, height) + o.shape[3:]) for o in outs[1:])
+    faces = {
+        2: (jnp.expand_dims(xlo, 2), jnp.expand_dims(xhi, 2)),
+        3: (jnp.expand_dims(ylo, 3), jnp.expand_dims(yhi, 3)),
+    }
+    return whole, faces
+
+
 def face_from(part, axis, from_lower):
     count = lax.axis_size(axis)
     if from_lower:
@@ -408,14 +508,14 @@
             (cell_sums[8] + time_step * force_z) / floored,
         ]
     )
-    vf, _ = exchange(velocity, sides, 1)
+    column_velocity, vf = column_exchange(velocity, 1)
+    lid = jnp.zeros((1,) + column_velocity.shape[2:], jnp.float32)
     dilation = (
-        along(velocity[0:1], {2: (vf[2][0][0:1], vf[2][1][0:1])}, 2)[0]
-        + along(velocity[1:2], {3: (vf[3][0][1:2], vf[3][1][1:2])}, 3)[0]
-        + along(velocity[2:3], {1: (vf[1][0][2:3], vf[1][1][2:3])}, 1)[0]
-    )
-    right_side = -source_rate * (1.0 - porosity) * dilation
-    _, (all_right,) = exchange(right_side, (), 3, (right_side,))
+        along(column_velocity[0:1], {2: (vf[2][0][0:1], vf[2][1][0:1])}, 2)[0]
+        + along(column_velocity[1:2], {3: (vf[3][0][1:2], vf[3][1][1:2])}, 3)[0]
+        + along(column_velocity[2], {0: (lid, lid)}, 0)
+    )
+    all_right = -source_rate * (1.0 - all_porosity) * dilation
     zero_level = jnp.zeros((1, extent, breadth), jnp.float32)
     level_above = jnp.concatenate([all_permeability[1:], zero_level], axis=0)
     level_below = jnp.concatenate([zero_level, all_permeability[:-1]], axis=0)

time: 100 us -> 102 us (1.020)
  Pallas kernels: 64.9 us -> 69.6 us
  local copies, waits for them, and re-layouts: 28.9 us -> 25.7 us
    pallas_call x0 -> x1, Pallas kernels: none -> 20.8 us  [column_exchange(): pl.pallas_call(functools.partial(column_kernel, sizes, group), out_shape=...]
    pallas_call x4 -> x2, Pallas kernels: 41.1 us -> 24.9 us  [exchange(): pl.pallas_call(functools.partial(halo_kernel, axes, sizes, len(gathers),...]
    unnamed x61 -> x60, local copies, waits for them, and re-layouts: 12.3 us -> 8.83 us
    slice x2 -> x7, local copies, waits for them, and re-layouts: 1.36 us -> 4.39 us  [the longest x1 1.16 us: shards(): column_velocity[2]]
    squeeze x0 -> x3, local copies, waits for them, and re-layouts: none -> 2.55 us  [the longest x1 0.97 us: column_exchange(): cells[:, :, :, 0]]
    squeeze x5 -> x3, local copies, waits for them, and re-layouts: 3.57 us -> 2 us  [exchange(): sends.append(lax.index_in_dim(cells, size - 1, axis=dim, keepdims=False))]
    concatenate x7 -> x5, local copies, waits for them, and re-layouts: 2.28 us -> 1.15 us  [along(): jnp.concatenate([lax.slice_in_dim(cells, 1, size, axis=dim), upper], axis...]
    concatenate x14 -> x11, local copies, waits for them, and re-layouts: 3.26 us -> 2.2 us  [along(): jnp.concatenate([lower, lax.slice_in_dim(cells, 0, size - 1, axis=dim)],...]
where the time goes in v6:
time: 102 us; the launch traced here: 101 us
  Pallas kernels  69.6 us (68%)
  local copies, waits for them, and re-layouts  25.7 us (25%)
  other arithmetic  3.59 us (4%)
  between operations  2.03 us (2%)
    pallas_call x2, Pallas kernels, exchange(): pl.pallas_call(functools.partial(halo_kernel, axes, sizes, len(gathers),...  24.9 us
    pallas_call x1, Pallas kernels, cell_sums_of(): pl.pallas_call(sums_kernel, out_shape=jax.ShapeDtypeStruct((10, levels, e...  23.8 us
    pallas_call x1, Pallas kernels, column_exchange(): pl.pallas_call(functools.partial(column_kernel, sizes, group), out_shape=...  20.8 us
    unnamed x60, local copies, waits for them, and re-layouts  8.83 us
    concatenate x11, local copies, waits for them, and re-layouts, along(): jnp.concatenate([lower, lax.slice_in_dim(cells, 0, size - 1, axis=dim)],...  2.2 us
    slice x3, local copies, waits for them, and re-layouts, exchange(): sends.append(lax.index_in_dim(cells, size - 1, axis=dim, keepdims=False))  2.06 us

profile of v6, /device:TPU:121, one launch (start us, length us, event | category | flops | bytes accessed | tf_op | source)
XLA Modules:
  0.0 100.9 jit_solution(14988622992687984971)
XLA Ops:
  1.3 23.8 %shard_map.113 = f32[10,16,8,128]{3,2,1,0:T(8,128)} custom-call(s32[1,1]{1,0:T(1,128)} %bitcast.166.count_ref, f32[6,24576]{1,0:T(8,128)} %st_ref.1, f32[1,24576]{1,0:T(1,128)} %bitcast.217, f32[1,24576]{1,0:T(1,128)} %bitcast.218, f32[3,24576]{1,0:T(4,128)} %vel_ref.1, f32[1,24576]{1,0:T(1,128)} %bitcast.219, s32[1,24576]{1,0:T(1,128)} %bitcast.220, ...), custom_call_target="tpu_custom_call" | custom-call | flops 16106127360 | bytes 1933312 | tf_op jit(solution)/shard_map/pallas_call | solution.py:88
  25.1 1.3 %fusion.35 = (f32[6,16,8,1]{3,2,1,0:T(8,128)S(1)}, f32[6,16,8,1]{3,2,1,0:T(8,128)S(1)}) fusion(f32[10,16,8,128]{3,2,1,0:T(8,128)} %shard_map.113), kind=kLoop, calls=%fused_computation.121 | loop fusion | bytes 12288 | tf_op jit(solution)/shard_map/slice | solution.py:321
  26.4 1.2 %copy.147 = f32[6,16,8,1]{2,1,0,3:T(8,128)} copy(f32[6,16,8,1]{3,2,1,0:T(8,128)S(1)} %get-tuple-element.86) | data formatting | bytes 6144
  27.6 1.2 %copy.148 = f32[6,16,8,1]{2,1,0,3:T(8,128)} copy(f32[6,16,8,1]{3,2,1,0:T(8,128)S(1)} %get-tuple-element.85) | data formatting | bytes 6144
  28.9 0.7 fusion.36
  29.6 0.6 slice_bitcast_fusion.10
  30.2 14.8 %shard_map.114 = (f32[6,16,128]{2,1,0:T(8,128)}, f32[6,16,128]{2,1,0:T(8,128)}, f32[6,16,8]{2,1,0:T(8,128)}, f32[6,16,8]{2,1,0:T(8,128)}, f32[6,8,128]{2,1,0:T(8...) custom-call(f32[6,16,128]{2,1,0:T(8,128)} %bitcast.198, ...), custom_call_target="tpu_custom_call" | custom-call | tf_op jit(solution)/shard_map/pallas_call | solution.py:327
  45.0 0.8 slice_bitcast_fusion.22
  45.8 0.2 copy.78
  46.0 0.2 copy.81
  46.1 0.4 copy-done.4
  46.6 0.2 copy-done.3
  46.8 0.7 copy-done.9
  47.5 0.1 fusion.33
  47.9 0.1 fusion.15
  48.0 0.2 copy.90
  48.2 0.2 copy.93
  48.5 0.1 fusion.20
  48.6 0.2 copy.101
  48.8 0.2 copy.104
  49.1 0.1 fusion.25
  49.2 0.1 fusion.61
  49.3 1.0 copy.135
  50.3 1.0 copy.136
  51.3 0.7 copy.107.v_ref
  52.0 0.6 slice_bitcast_fusion.8
  52.6 20.8 %shard_map.115 = (f32[3,4,16,8,128]{4,3,2,1,0:T(8,128)}, f32[3,4,16,128]{3,2,1,0:T(8,128)}, f32[3,4,16,128]{3,2,1,0:T(8,128)}, f32[3,4,16,8]{3,2,1,0:T(8,128)}, f32[3,4,16,8]{3,2,1,0:T(8,128)}) custom-call(f32[3,16,8,128]{3,2,1,0:T(8,128)} %copy.107.v_ref, f32[3,16,128]{2,1,0:T(8,128)} %get-tuple-element.152.xlo_s, f32[3,16,128]{2,1,0:T(8,128)} %get-tuple-element.151.xhi_s, ...), custom_call_target="tpu_custom_call" | custom-call | tf_op jit(solution)/shard_map/pallas_call | solution.py:430
  73.5 1.2 %fusion.30 = (f32[1,4,16,8,128]{4,3,2,1,0:T(8,128)S(1)}, f32[1,4,16,8,128]{4,3,2,1,0:T(8,128)S(1)}, f32[1,4,16,8,128]{4,3,2,1,0:T(8,128)S(1)}) fusion(f32[3,4,16,8,128]{4,3,2,1,0:T(8,128)} %get-tuple-element.26), kind=kLoop, calls=%fused_computation.116 | loop fusion | bytes 1572864 | tf_op jit(solution)/shard_map/slice | solution.py:516
  74.6 0.1 slice_bitcast_fusion
  74.9 0.8 slice.526
  75.6 0.4 copy.112
  76.1 0.8 slice.527
  76.9 0.4 copy.113
  77.3 0.8 slice.520
  78.1 0.8 slice.521
  78.9 0.3 fusion.5
  79.4 0.9 copy-done.1
  80.4 0.2 fusion.28
  80.6 0.1 fusion.53
  81.0 0.4 fusion
  81.7 0.4 multiply_add_fusion.7
  82.2 0.2 multiply_add_fusion.6
  82.4 0.3 multiply_add_fusion.5
  82.9 0.2 multiply_add_fusion.4
  83.1 0.3 multiply_add_fusion.3
  83.5 0.1 multiply_add_fusion.2
  83.7 0.3 multiply_add_fusion.1
  84.1 0.2 pad_multiply_fusion
  84.3 0.1 copy_bitcast_fusion
  84.5 0.1 fusion.8
  84.6 0.1 fusion.63
  84.7 0.8 copy.137
  85.4 0.8 copy.138
  86.2 0.6 slice_bitcast_fusion.12
  86.8 10.2 %shard_map.116 = (f32[16,128]{1,0:T(8,128)}, f32[16,128]{1,0:T(8,128)}, f32[16,8]{1,0:T(8,128)}, f32[16,8]{1,0:T(8,128)}) custom-call(f32[16,128]{1,0:T(8,128)} %get-tuple-element.162.refs_0_, f32[16,128]{1,0:T(8,128)} %get-tuple-element.161.refs_1_, f32[16,8]{1,0:T(8,128)} %bitcast.205, f32[16,8]{1,0:T(8,128)} %bitcast.206), custom_call_target="tpu_custom_call" | custom-call | tf_op jit(solution)/shard_map/pallas_call | solution.py:327
  97.0 0.7 copy-done.7
  97.7 0.7 copy-done.6
  98.4 0.2 copy.118
  98.6 0.5 copy-done.5
  99.1 0.2 copy.120
  99.2 0.1 slice_bitcast_fusion.4
  99.3 0.1 fusion.27
  99.5 0.7 copy.121
  100.2 0.7 copy.122
  (87 shorter events, 1.9 us)
Async XLA Ops:
  26.4 2.5 %copy-start = (f32[10,16,8,128]{3,2,1,0:T(8,128)S(1)}, f32[10,16,8,128]{3,2,1,0:T(8,128)}, u32[]{:S(2)}) copy-start(f32[10,16,8,128]{3,2,1,0:T(8,128)} %shard_map.113) | copy-start | bytes 1966084
  45.8 0.8 copy-start.4
  46.0 0.8 copy-start.3
  46.8 0.7 copy-start.9
  46.8 0.8 copy-start.10
  76.1 2.8 %copy-start.2 = (f32[4,16,8,128]{3,2,1,0:T(8,128)S(1)}, f32[4,16,8,128]{3,2,1,0:T(8,128)}, u32[]{:S(2)}) copy-start(f32[4,16,8,128]{3,2,1,0:T(8,128)} %get-tuple-element.25) | copy-start | bytes 786436
  79.4 1.0 copy-start.1
  97.0 0.7 copy-start.7
  97.0 0.7 copy-start.8
  97.7 0.7 copy-start.6
  98.4 0.7 copy-start.5

commit v7 on v5

--- a/solution.py
+++ b/solution.py
@@ -29,7 +29,7 @@
     return [hi, lo]
 
 
-def sums_kernel(count_ref, st_ref, ms_ref, cons_ref, vel_ref, w_ref, cell_ref, yf_ref, out_ref, acc_ref):
+def sums_kernel(count_ref, st_ref, ms_ref, cons_ref, vel_ref, w_ref, cell_ref, yf_ref, out_ref, xlo_ref, xhi_ref, ylo_ref, yhi_ref, zlo_ref, zhi_ref, acc_ref):
     count = count_ref[0, 0]
     acc_ref[...] = jnp.zeros_like(acc_ref)
     chunks = st_ref.shape[1] // CHUNK
@@ -79,6 +79,16 @@
             for s in range(1, SPLITS):
                 total = total + acc_ref[pl.ds((comp * SPLITS + s) * M_ROWS + (level >> 2) * 8, 8), lanes]
             out_ref[comp, level] = total
+            if comp < 6:
+                xlo_ref[comp, pl.ds(level, 1), :] = total[0:1, :]
+                xhi_ref[comp, pl.ds(level, 1), :] = total[7:8, :]
+                turned = total.T
+                ylo_ref[comp, pl.ds(level, 1), :] = turned[0:1, :]
+                yhi_ref[comp, pl.ds(level, 1), :] = turned[127:128, :]
+                if level == 0:
+                    zlo_ref[comp] = total
+                if level == 15:
+                    zhi_ref[comp] = total
 
 
 def cell_sums_of(stress_trial, mean_stress, consolidation, point_velocity, point_weight, point_cell, yield_flag, point_count, levels, extent, breadth):
@@ -87,9 +97,13 @@
     vmem = pl.BlockSpec(memory_space=pltpu.VMEM)
     return pl.pallas_call(
         sums_kernel,
-        out_shape=jax.ShapeDtypeStruct((10, levels, extent, breadth), jnp.float32),
+        out_shape=[
+            jax.ShapeDtypeStruct(s, jnp.float32)
+            for s in [(10, levels, extent, breadth)] + [(6, levels, breadth)] * 2 + [(6, levels, extent)] * 2
+            + [(6, extent, breadth)] * 2
+        ],
         in_specs=[pl.BlockSpec(memory_space=pltpu.SMEM)] + [vmem] * 7,
-        out_specs=vmem,
+        out_specs=[vmem] * 7,
         scratch_shapes=[pltpu.VMEM((10 * SPLITS * M_ROWS, N_COLS), jnp.float32)],
         cost_estimate=pl.CostEstimate(
             flops=2 * 10 * SPLITS * M_ROWS * N_COLS * n, bytes_accessed=13 * 4 * n + 10 * 4 * levels * extent * breadth,
@@ -313,12 +327,14 @@
         copy.wait_send()
 
 
-def exchange(cells, sides, collective, gathers=()):
+def exchange(cells, sides, collective, gathers=(), given=None):
     sends = []
     for axis, dim in sides:
         size = cells.shape[dim]
         sends.append(lax.index_in_dim(cells, 0, axis=dim, keepdims=False))
         sends.append(lax.index_in_dim(cells, size - 1, axis=dim, keepdims=False))
+    if given is not None:
+        sends = list(given)
     axes = tuple(axis for axis, _ in sides)
     sizes = tuple(lax.axis_size(axis) for axis in axes)
     group = lax.axis_size("gz")
@@ -386,13 +402,15 @@
     permeability,
 ):
     levels, extent, breadth = porosity.shape
-    cell_sums = cell_sums_of(
+    cell_sums, *stress_faces = cell_sums_of(
         stress_trial, mean_stress, consolidation, point_velocity, point_weight, point_cell,
         yield_flag, point_count, levels, extent, breadth,
     )
     sides = (("gx", 2), ("gy", 3), ("gz", 1))
     stress_sums = cell_sums[:6]
-    sf, (all_porosity, all_permeability) = exchange(stress_sums, sides, 0, (porosity, permeability))
+    sf, (all_porosity, all_permeability) = exchange(
+        stress_sums, sides, 0, (porosity, permeability), given=stress_faces
+    )
     height = all_porosity.shape[0]
     d_x = lambda c: along(stress_sums[c:c + 1], {2: (sf[2][0][c:c + 1], sf[2][1][c:c + 1])}, 2)[0]
     d_y = lambda c: along(stress_sums[c:c + 1], {3: (sf[3][0][c:c + 1], sf[3][1][c:c + 1])}, 3)[0]

time: 100 us -> 96.2 us (0.962)
  local copies, waits for them, and re-layouts: 28.9 us -> 23.2 us
  Pallas kernels: 64.9 us -> 66.7 us
    unnamed x61 -> x37, local copies, waits for them, and re-layouts: 12.3 us -> 8.26 us
    slice x5 -> x3, local copies, waits for them, and re-layouts: 2.8 us -> 0.81 us  [exchange(): sends.append(lax.index_in_dim(cells, size - 1, axis=dim, keepdims=False))]
    pallas_call x1, Pallas kernels: 23.8 us -> 25.4 us  [cell_sums_of(): pl.pallas_call(sums_kernel, out_shape=[jax.ShapeDtypeStruct(s, jnp.float3...]
    squeeze x5 -> x4, local copies, waits for them, and re-layouts: 3.57 us -> 2.95 us  [exchange(): sends.append(lax.index_in_dim(cells, size - 1, axis=dim, keepdims=False))]
where the time goes in v7:
time: 96.2 us; the launch traced here: 95.1 us
  Pallas kernels  66.7 us (69%)
  local copies, waits for them, and re-layouts  23.2 us (24%)
  other arithmetic  3.39 us (4%)
  between operations  1.84 us (2%)
    pallas_call x4, Pallas kernels, exchange(): pl.pallas_call(functools.partial(halo_kernel, axes, sizes, len(gathers),...  41.3 us
    pallas_call x1, Pallas kernels, cell_sums_of(): pl.pallas_call(sums_kernel, out_shape=[jax.ShapeDtypeStruct(s, jnp.float3...  25.4 us
    unnamed x37, local copies, waits for them, and re-layouts  8.26 us
    concatenate x14, local copies, waits for them, and re-layouts, along(): jnp.concatenate([lower, lax.slice_in_dim(cells, 0, size - 1, axis=dim)],...  4.06 us
    squeeze x4, local copies, waits for them, and re-layouts, exchange(): sends.append(lax.index_in_dim(cells, size - 1, axis=dim, keepdims=False))  2.95 us
    concatenate x7, local copies, waits for them, and re-layouts, along(): jnp.concatenate([lax.slice_in_dim(cells, 1, size, axis=dim), upper], axis...  2.28 us

profile of v7, /device:TPU:121, one launch (start us, length us, event | category | flops | bytes accessed | tf_op | source)
XLA Modules:
  0.0 95.1 jit_solution(2987425704113811572)
XLA Ops:
  1.3 25.4 %shard_map.113 = (f32[10,16,8,128]{3,2,1,0:T(8,128)}, f32[6,16,128]{2,1,0:T(8,128)}, f32[6,16,128]{2,1,0:T(8,128)}, f32[6,16,8]{2,1,0:T(8,128)}, f32[6,16,8]{2,1...) custom-call(s32[1,1]{1,0:T(1,128)} %bitcast.149.count_ref, f32[6,24576]{1,0:T(8,128)} %st_ref.1, ...), custom_call_target="tpu_custom_call" | custom-call | flops 16106127360 | bytes 1933312 | tf_op jit(solution)/shard_map/pallas_call | solution.py:98
  26.7 14.9 %shard_map.114 = (f32[6,16,128]{2,1,0:T(8,128)}, f32[6,16,128]{2,1,0:T(8,128)}, f32[6,16,8]{2,1,0:T(8,128)}, f32[6,16,8]{2,1,0:T(8,128)}, f32[6,8,128]{2,1,0:T(8...) custom-call(f32[6,16,128]{2,1,0:T(8,128)} %get-tuple-element.28.refs_0_, ...), custom_call_target="tpu_custom_call" | custom-call | tf_op jit(solution)/shard_map/pallas_call | solution.py:343
  41.6 0.8 slice_bitcast_fusion.26
  42.4 0.2 copy.69
  42.6 0.2 copy.72
  42.8 0.8 slice_bitcast_fusion.28
  43.6 0.1 copy.64
  43.8 0.1 fusion.28
  43.9 0.1 fusion.8
  44.0 0.2 copy.81
  44.2 0.2 copy.84
  44.4 0.1 fusion.7
  44.5 0.2 copy.92
  44.7 0.2 copy.95
  44.9 0.1 fusion.6
  45.0 0.1 fusion.54
  45.1 1.0 %copy.129 = f32[3,16,8,1]{2,1,0,3:T(8,128)} copy(f32[3,16,8,1]{3,1,2,0:T(8,128)S(1)} %get-tuple-element.147) | data formatting | bytes 3072 | tf_op jit(solution)/shard_map/squeeze | solution.py:334
  46.1 1.0 %copy.130 = f32[3,16,8,1]{2,1,0,3:T(8,128)} copy(f32[3,16,8,1]{3,1,2,0:T(8,128)S(1)} %get-tuple-element.146) | data formatting | bytes 3072 | tf_op jit(solution)/shard_map/squeeze | solution.py:335
  47.1 0.6 slice_bitcast_fusion.10
  47.7 0.6 fusion.53
  48.3 9.5 %shard_map.115 = (f32[3,16,128]{2,1,0:T(8,128)}, f32[3,16,128]{2,1,0:T(8,128)}, f32[3,16,8]{2,1,0:T(8,128)}, f32[3,16,8]{2,1,0:T(8,128)}, f32[3,8,128]{2,1,0:T(8,128)}, /*index=5*/f32[3,8,128]{2,1,0:T(8,128)}) custom-call(f32[3,16,128]{2,1,0:T(8,128)} %get-tuple-element.149.refs_0_, f32[3,16,128]{2,1,0:T(8,128)} %get-tuple-element.148.refs_1_, ...), custom_call_target="tpu_custom_call" | custom-call | tf_op jit(solution)/shard_map/pallas_call | solution.py:343
  57.8 0.7 slice_bitcast_fusion.15
  58.5 0.2 copy.102
  58.7 0.7 slice_bitcast_fusion.14
  59.4 0.2 copy.104
  59.6 0.7 slice_bitcast_fusion.16
  60.3 0.7 slice_bitcast_fusion.17
  61.0 0.7 slice.490
  61.6 0.7 slice.491
  62.3 0.1 slice_bitcast_fusion.4
  62.4 0.8 copy-done.4
  63.3 0.1 fusion.21
  63.4 0.7 copy.107.refs_0_
  64.0 8.3 %shard_map.116 = f32[4,16,8,128]{3,2,1,0:T(8,128)} custom-call(f32[16,8,128]{2,1,0:T(8,128)} %copy.107.refs_0_), custom_call_target="tpu_custom_call" | custom-call | tf_op jit(solution)/shard_map/pallas_call | solution.py:343
  72.3 1.0 %copy.178 = f32[8,8,8,128]{3,1,2,0:T(8,128)S(1)} copy(f32[8,8,8,128]{3,2,1,0:T(8,128)} %bitcast.159) | data formatting | bytes 524288
  73.4 0.9 copy-done.1
  74.3 0.9 copy-done.3
  75.3 0.2 fusion.25
  75.5 0.1 fusion.46
  75.9 0.9 copy-done
  76.8 0.4 fusion
  77.5 0.4 multiply_add_fusion.7
  78.0 0.2 multiply_add_fusion.6
  78.2 0.3 multiply_add_fusion.5
  78.7 0.2 multiply_add_fusion.4
  78.9 0.3 multiply_add_fusion.3
  79.3 0.1 multiply_add_fusion.2
  79.5 0.3 multiply_add_fusion.1
  79.9 0.2 pad_multiply_fusion
  80.1 0.1 copy_bitcast_fusion.1
  80.4 0.1 fusion.56
  80.4 0.8 copy.135
  81.2 0.8 copy.136
  82.0 0.6 slice_bitcast_fusion.12
  82.6 8.6 %shard_map.117 = (f32[16,128]{1,0:T(8,128)}, f32[16,128]{1,0:T(8,128)}, f32[16,8]{1,0:T(8,128)}, f32[16,8]{1,0:T(8,128)}) custom-call(f32[16,128]{1,0:T(8,128)} %get-tuple-element.159.refs_0_, f32[16,128]{1,0:T(8,128)} %get-tuple-element.158.refs_1_, f32[16,8]{1,0:T(8,128)} %bitcast.177, f32[16,8]{1,0:T(8,128)} %bitcast.178), custom_call_target="tpu_custom_call" | custom-call | tf_op jit(solution)/shard_map/pallas_call | solution.py:343
  91.2 0.7 copy-done.7
  91.9 0.7 copy-done.6
  92.6 0.2 copy.112
  92.7 0.5 copy-done.5
  93.2 0.2 copy.114
  93.4 0.1 slice_bitcast_fusion
  93.5 0.1 fusion.23
  93.7 0.7 copy.115
  94.4 0.7 copy.116
  (64 shorter events, 1.5 us)
Async XLA Ops:
  26.7 16.9 %copy-start.2 = (f32[10,16,8,128]{3,2,1,0:T(8,128)S(1)}, f32[10,16,8,128]{3,2,1,0:T(8,128)}, u32[]{:S(2)}) copy-start(f32[10,16,8,128]{3,2,1,0:T(8,128)} %get-tuple-element.27) | copy-start | bytes 1966084
  42.7 0.8 copy-start.9
  42.7 0.8 copy-start.10
  62.4 0.8 copy-start.4
  73.3 1.0 %copy-start.1 = (f32[4,16,8,128]{3,2,1,0:T(8,128)S(1)}, f32[4,16,8,128]{3,2,1,0:T(8,128)}, u32[]{:S(2)}) copy-start(f32[4,16,8,128]{3,2,1,0:T(8,128)} %get-tuple-element.46) | copy-start | bytes 786436
  74.3 0.9 copy-start.3
  75.9 1.0 %copy-start = (f32[4,16,8,128]{3,2,1,0:T(8,128)S(1)}, f32[4,16,8,128]{3,2,1,0:T(8,128)}, u32[]{:S(2)}) copy-start(f32[4,16,8,128]{3,2,1,0:T(8,128)} %shard_map.116) | copy-start | bytes 786436
  91.1 0.7 copy-start.7
  91.2 0.7 copy-start.8
  91.9 0.7 copy-start.6
  92.6 0.7 copy-start.5

commit v8 on v7

--- a/solution.py
+++ b/solution.py
@@ -361,6 +361,36 @@
     return faces, stacked
 
 
+def faces_kernel(with_z, cells_ref, *out_refs):
+    chans, levels, extent, breadth = cells_ref.shape
+    xlo, xhi, ylo, yhi = out_refs[:4]
+    for c in range(chans):
+        for level in range(levels):
+            tile = cells_ref[c, level]
+            xlo[c, pl.ds(level, 1), :] = tile[0:1, :]
+            xhi[c, pl.ds(level, 1), :] = tile[extent - 1:extent, :]
+            turned = tile.T
+            ylo[c, pl.ds(level, 1), :] = turned[0:1, :]
+            yhi[c, pl.ds(level, 1), :] = turned[breadth - 1:breadth, :]
+        if with_z:
+            out_refs[4][c] = cells_ref[c, 0]
+            out_refs[5][c] = cells_ref[c, levels - 1]
+
+
+def faces_by_kernel(cells, with_z):
+    chans, levels, extent, breadth = cells.shape
+    shapes = [(chans, levels, breadth)] * 2 + [(chans, levels, extent)] * 2
+    if with_z:
+        shapes += [(chans, extent, breadth)] * 2
+    vmem = pl.BlockSpec(memory_space=pltpu.VMEM)
+    return pl.pallas_call(
+        functools.partial(faces_kernel, with_z),
+        out_shape=[jax.ShapeDtypeStruct(s, cells.dtype) for s in shapes],
+        in_specs=[vmem],
+        out_specs=[vmem] * len(shapes),
+    )(cells)
+
+
 def face_from(part, axis, from_lower):
     count = lax.axis_size(axis)
     if from_lower:
@@ -426,7 +456,7 @@
             (cell_sums[8] + time_step * force_z) / floored,
         ]
     )
-    vf, _ = exchange(velocity, sides, 1)
+    vf, _ = exchange(velocity, sides, 1, given=faces_by_kernel(velocity, True))
     dilation = (
         along(velocity[0:1], {2: (vf[2][0][0:1], vf[2][1][0:1])}, 2)[0]
         + along(velocity[1:2], {3: (vf[3][0][1:2], vf[3][1][1:2])}, 3)[0]
@@ -454,7 +484,8 @@
         jnp.concatenate([zero_level, solved, zero_level], axis=0), first, levels + 2, axis=0
     )
     pressure = around[1:-1]
-    pf, _ = exchange(pressure, (("gx", 1), ("gy", 2)), 2)
+    pressure_faces = [f[0] for f in faces_by_kernel(pressure[None], False)]
+    pf, _ = exchange(pressure, (("gx", 1), ("gy", 2)), 2, given=pressure_faces)
     gradient = jnp.stack(
         [
             along(pressure, pf, 1),

time: 96.2 us -> 95.3 us (level)
  local copies, waits for them, and re-layouts: 23.2 us -> 15.5 us
  Pallas kernels: 66.7 us -> 70.8 us
  other arithmetic: 3.39 us -> 6.01 us
    squeeze x6 -> x0, local copies, waits for them, and re-layouts: 4.69 us -> none  [the longest x4 2.95 us: exchange(): sends.append(lax.index_in_dim(cells, size - 1, axis=dim, keepdims=False))]
    pallas_call x0 -> x2, Pallas kernels: none -> 4.19 us  [faces_by_kernel(): pl.pallas_call(functools.partial(faces_kernel, with_z), out_shape=[jax.Sh...]
    concatenate x14 -> x13, local copies, waits for them, and re-layouts: 4.06 us -> 2.52 us  [along(): jnp.concatenate([lower, lax.slice_in_dim(cells, 0, size - 1, axis=dim)],...]
    slice x4 -> x3, local copies, waits for them, and re-layouts: 0.82 us -> 2.19 us  [the longest x1 0.8 us: shards(): sf[2][0][c:c + 1]]
    unnamed x37 -> x36, local copies, waits for them, and re-layouts: 8.26 us -> 6.91 us
    concatenate x7 -> x6, local copies, waits for them, and re-layouts: 2.28 us -> 1.54 us  [along(): jnp.concatenate([lax.slice_in_dim(cells, 1, size, axis=dim), upper], axis...]
where the time goes in v8:
time: 95.3 us; the launch traced here: 94.1 us
  Pallas kernels  70.8 us (74%)
  local copies, waits for them, and re-layouts  15.5 us (16%)
  other arithmetic  6.01 us (6%)
  between operations  1.8 us (2%)
    pallas_call x4, Pallas kernels, exchange(): pl.pallas_call(functools.partial(halo_kernel, axes, sizes, len(gathers),...  41.2 us
    pallas_call x1, Pallas kernels, cell_sums_of(): pl.pallas_call(sums_kernel, out_shape=[jax.ShapeDtypeStruct(s, jnp.float3...  25.4 us
    unnamed x36, local copies, waits for them, and re-layouts  6.91 us
    pallas_call x2, Pallas kernels, faces_by_kernel(): pl.pallas_call(functools.partial(faces_kernel, with_z), out_shape=[jax.Sh...  4.19 us
    concatenate x13, local copies, waits for them, and re-layouts, along(): jnp.concatenate([lower, lax.slice_in_dim(cells, 0, size - 1, axis=dim)],...  2.52 us

profile of v8, /device:TPU:121, one launch (start us, length us, event | category | flops | bytes accessed | tf_op | source)
XLA Modules:
  0.0 94.1 jit_solution(5093910460008860375)
XLA Ops:
  1.3 25.4 %shard_map.113 = (f32[10,16,8,128]{3,2,1,0:T(8,128)}, f32[6,16,128]{2,1,0:T(8,128)}, f32[6,16,128]{2,1,0:T(8,128)}, f32[6,16,8]{2,1,0:T(8,128)}, f32[6,16,8]{2,1...) custom-call(s32[1,1]{1,0:T(1,128)} %bitcast.138.count_ref, f32[6,24576]{1,0:T(8,128)} %st_ref.1, ...), custom_call_target="tpu_custom_call" | custom-call | flops 16106127360 | bytes 1933312 | tf_op jit(solution)/shard_map/pallas_call | solution.py:98
  26.7 14.9 %shard_map.114 = (f32[6,16,128]{2,1,0:T(8,128)}, f32[6,16,128]{2,1,0:T(8,128)}, f32[6,16,8]{2,1,0:T(8,128)}, f32[6,16,8]{2,1,0:T(8,128)}, f32[6,8,128]{2,1,0:T(8...) custom-call(f32[6,16,128]{2,1,0:T(8,128)} %get-tuple-element.38.refs_0_, ...), custom_call_target="tpu_custom_call" | custom-call | tf_op jit(solution)/shard_map/pallas_call | solution.py:343
  41.6 0.8 slice_bitcast_fusion.16
  42.4 0.2 copy.13
  42.6 0.2 copy.15
  42.8 0.8 fusion.56
  43.5 0.0 copy-done.9
  43.6 0.0 copy-done.10
  43.6 0.0 copy-done
  43.6 0.1 fusion.30
  43.8 0.1 fusion.10
  43.9 0.2 copy.17
  44.1 0.2 copy.19
  44.3 0.1 fusion.15
  44.4 0.2 copy.21
  44.5 0.2 copy.23
  44.7 0.1 fusion.20
  44.8 0.7 pad_maximum_fusion.cells_ref
  45.5 2.4 %shard_map.115 = (f32[3,16,128]{2,1,0:T(8,128)}, f32[3,16,128]{2,1,0:T(8,128)}, f32[3,16,8]{2,1,0:T(8,128)}, f32[3,16,8]{2,1,0:T(8,128)}, f32[3,8,128]{2,1,0:T(8,128)}, /*index=5*/f32[3,8,128]{2,1,0:T(8,128)}) custom-call(f32[3,16,8,128]{3,2,1,0:T(8,128)} %pad_maximum_fusion.cells_ref), custom_call_target="tpu_custom_call" | custom-call | tf_op jit(solution)/shard_map/pallas_call | solution.py:386
  47.9 9.5 %shard_map.116 = (f32[3,16,128]{2,1,0:T(8,128)}, f32[3,16,128]{2,1,0:T(8,128)}, f32[3,16,8]{2,1,0:T(8,128)}, f32[3,16,8]{2,1,0:T(8,128)}, f32[3,8,128]{2,1,0:T(8,128)}, /*index=5*/f32[3,8,128]{2,1,0:T(8,128)}) custom-call(f32[3,16,128]{2,1,0:T(8,128)} %get-tuple-element.50.refs_0_, f32[3,16,128]{2,1,0:T(8,128)} %get-tuple-element.51.refs_1_, ...), custom_call_target="tpu_custom_call" | custom-call | tf_op jit(solution)/shard_map/pallas_call | solution.py:343
  57.4 0.7 slice_bitcast_fusion.11
  58.1 0.2 copy.25
  58.3 0.7 slice_bitcast_fusion.10
  59.0 0.2 copy.27
  59.2 0.7 slice.442
  59.9 0.7 slice.443
  60.6 0.7 slice.450
  61.3 0.7 slice.451
  61.9 0.1 slice_bitcast_fusion.4
  62.0 0.8 copy-done.4
  62.9 0.7 fusion.24.refs_0_
  63.6 8.3 %shard_map.117 = f32[4,16,8,128]{3,2,1,0:T(8,128)} custom-call(f32[16,8,128]{2,1,0:T(8,128)} %fusion.24.refs_0_), custom_call_target="tpu_custom_call" | custom-call | tf_op jit(solution)/shard_map/pallas_call | solution.py:343
  71.9 1.0 %copy.91 = f32[8,8,8,128]{3,1,2,0:T(8,128)S(1)} copy(f32[8,8,8,128]{3,2,1,0:T(8,128)} %bitcast.148) | data formatting | bytes 524288
  72.9 0.0 copy-start.2
  72.9 0.9 copy-done.2
  73.9 0.9 copy-done.3
  74.8 0.2 fusion.27
  75.0 0.1 fusion.48
  75.4 0.0 copy-start.1
  75.5 0.9 copy-done.1
  76.4 0.4 fusion
  77.0 0.4 multiply_add_fusion.7
  77.5 0.2 multiply_add_fusion.6
  77.8 0.3 multiply_add_fusion.5
  78.2 0.2 multiply_add_fusion.4
  78.5 0.3 multiply_add_fusion.3
  78.9 0.1 multiply_add_fusion.2
  79.1 0.3 multiply_add_fusion.1
  79.4 0.2 pad_multiply_fusion
  79.7 0.2 divide_bitcast_fusion
  80.0 0.6 fusion.55
  80.6 1.8 %shard_map.118 = (f32[1,16,128]{2,1,0:T(8,128)}, f32[1,16,128]{2,1,0:T(8,128)}, f32[1,16,8]{2,1,0:T(8,128)}, f32[1,16,8]{2,1,0:T(8,128)}) custom-call(f32[1,16,8,128]{3,2,1,0:T(8,128)} %bitcast.163), custom_call_target="tpu_custom_call" | custom-call | tf_op jit(solution)/shard_map/pallas_call | solution.py:386
  82.4 8.6 %shard_map.119 = (f32[16,128]{1,0:T(8,128)}, f32[16,128]{1,0:T(8,128)}, f32[16,8]{1,0:T(8,128)}, f32[16,8]{1,0:T(8,128)}) custom-call(f32[16,128]{1,0:T(8,128)} %bitcast.174, f32[16,128]{1,0:T(8,128)} %bitcast.175, f32[16,8]{1,0:T(8,128)} %bitcast.176, f32[16,8]{1,0:T(8,128)} %bitcast.177), custom_call_target="tpu_custom_call" | custom-call | tf_op jit(solution)/shard_map/pallas_call | solution.py:343
  90.9 0.0 copy-start.7
  91.0 0.0 copy-start.8
  91.0 0.7 copy-done.7
  91.6 0.0 copy-done.8
  91.7 0.7 copy-done.6
  92.4 0.2 copy.35
  92.5 0.5 copy-done.5
  93.1 0.2 copy.37
  93.2 0.1 slice_bitcast_fusion
  93.3 0.1 fusion.26
  93.4 0.7 fusion.1
  (54 shorter events, 1.4 us)
Async XLA Ops:
  26.7 16.9 %copy-start = (f32[10,16,8,128]{3,2,1,0:T(8,128)S(1)}, f32[10,16,8,128]{3,2,1,0:T(8,128)}, u32[]{:S(2)}) copy-start(f32[10,16,8,128]{3,2,1,0:T(8,128)} %get-tuple-element.37) | copy-start | bytes 1966084
  42.7 0.8 copy-start.9
  42.8 0.8 copy-start.10
  62.0 0.8 copy-start.4
  72.9 1.0 %copy-start.2 = (f32[4,16,8,128]{3,2,1,0:T(8,128)S(1)}, f32[4,16,8,128]{3,2,1,0:T(8,128)}, u32[]{:S(2)}) copy-start(f32[4,16,8,128]{3,2,1,0:T(8,128)} %get-tuple-element.62) | copy-start | bytes 786436
  73.8 0.9 %copy-start.3 = (f32[4,16,8,128]{3,2,1,0:T(8,128)S(1)}, f32[4,16,8,128]{3,2,1,0:T(8,128)}, u32[]{:S(2)}) copy-start(f32[4,16,8,128]{3,2,1,0:T(8,128)} %get-tuple-element.63) | copy-start | bytes 786436
  75.4 1.0 %copy-start.1 = (f32[4,16,8,128]{3,2,1,0:T(8,128)S(1)}, f32[4,16,8,128]{3,2,1,0:T(8,128)}, u32[]{:S(2)}) copy-start(f32[4,16,8,128]{3,2,1,0:T(8,128)} %shard_map.117) | copy-start | bytes 786436
  90.9 0.7 copy-start.7
  91.0 0.7 copy-start.8
  91.7 0.7 copy-start.6
  92.4 0.7 copy-start.5

commit v9 on v7

--- a/solution.py
+++ b/solution.py
@@ -21,6 +21,9 @@
 
 
 SPLITS = 2
+X_PARTS = (0, 3, 5)
+Y_PARTS = (3, 1, 4)
+Z_PARTS = (5, 4, 2)
 
 
 def _split(v):
@@ -79,16 +82,21 @@
             for s in range(1, SPLITS):
                 total = total + acc_ref[pl.ds((comp * SPLITS + s) * M_ROWS + (level >> 2) * 8, 8), lanes]
             out_ref[comp, level] = total
-            if comp < 6:
-                xlo_ref[comp, pl.ds(level, 1), :] = total[0:1, :]
-                xhi_ref[comp, pl.ds(level, 1), :] = total[7:8, :]
+            if comp in X_PARTS:
+                slot = X_PARTS.index(comp)
+                xlo_ref[slot, pl.ds(level, 1), :] = total[0:1, :]
+                xhi_ref[slot, pl.ds(level, 1), :] = total[7:8, :]
+            if comp in Y_PARTS:
+                slot = Y_PARTS.index(comp)
                 turned = total.T
-                ylo_ref[comp, pl.ds(level, 1), :] = turned[0:1, :]
-                yhi_ref[comp, pl.ds(level, 1), :] = turned[127:128, :]
+                ylo_ref[slot, pl.ds(level, 1), :] = turned[0:1, :]
+                yhi_ref[slot, pl.ds(level, 1), :] = turned[127:128, :]
+            if comp in Z_PARTS:
+                slot = Z_PARTS.index(comp)
                 if level == 0:
-                    zlo_ref[comp] = total
+                    zlo_ref[slot] = total
                 if level == 15:
-                    zhi_ref[comp] = total
+                    zhi_ref[slot] = total
 
 
 def cell_sums_of(stress_trial, mean_stress, consolidation, point_velocity, point_weight, point_cell, yield_flag, point_count, levels, extent, breadth):
@@ -99,8 +107,8 @@
         sums_kernel,
         out_shape=[
             jax.ShapeDtypeStruct(s, jnp.float32)
-            for s in [(10, levels, extent, breadth)] + [(6, levels, breadth)] * 2 + [(6, levels, extent)] * 2
-            + [(6, extent, breadth)] * 2
+            for s in [(10, levels, extent, breadth)] + [(3, levels, breadth)] * 2 + [(3, levels, extent)] * 2
+            + [(3, extent, breadth)] * 2
         ],
         in_specs=[pl.BlockSpec(memory_space=pltpu.SMEM)] + [vmem] * 7,
         out_specs=[vmem] * 7,
@@ -361,6 +369,39 @@
     return faces, stacked
 
 
+def faces_kernel(parts, cells_ref, *out_refs):
+    chans, levels, extent, breadth = cells_ref.shape
+    xlo, xhi, ylo, yhi = out_refs[:4]
+    for slot, c in enumerate(parts[0]):
+        for level in range(levels):
+            tile = cells_ref[c, level]
+            xlo[slot, pl.ds(level, 1), :] = tile[0:1, :]
+            xhi[slot, pl.ds(level, 1), :] = tile[extent - 1:extent, :]
+    for slot, c in enumerate(parts[1]):
+        for level in range(levels):
+            turned = cells_ref[c, level].T
+            ylo[slot, pl.ds(level, 1), :] = turned[0:1, :]
+            yhi[slot, pl.ds(level, 1), :] = turned[breadth - 1:breadth, :]
+    if len(parts) > 2:
+        for slot, c in enumerate(parts[2]):
+            out_refs[4][slot] = cells_ref[c, 0]
+            out_refs[5][slot] = cells_ref[c, levels - 1]
+
+
+def faces_by_kernel(cells, parts):
+    chans, levels, extent, breadth = cells.shape
+    shapes = [(len(parts[0]), levels, breadth)] * 2 + [(len(parts[1]), levels, extent)] * 2
+    if len(parts) > 2:
+        shapes += [(len(parts[2]), extent, breadth)] * 2
+    vmem = pl.BlockSpec(memory_space=pltpu.VMEM)
+    return pl.pallas_call(
+        functools.partial(faces_kernel, parts),
+        out_shape=[jax.ShapeDtypeStruct(s, cells.dtype) for s in shapes],
+        in_specs=[vmem],
+        out_specs=[vmem] * len(shapes),
+    )(cells)
+
+
 def face_from(part, axis, from_lower):
     count = lax.axis_size(axis)
     if from_lower:
@@ -412,9 +453,13 @@
         stress_sums, sides, 0, (porosity, permeability), given=stress_faces
     )
     height = all_porosity.shape[0]
-    d_x = lambda c: along(stress_sums[c:c + 1], {2: (sf[2][0][c:c + 1], sf[2][1][c:c + 1])}, 2)[0]
-    d_y = lambda c: along(stress_sums[c:c + 1], {3: (sf[3][0][c:c + 1], sf[3][1][c:c + 1])}, 3)[0]
-    d_z = lambda c: along(stress_sums[c:c + 1], {1: (sf[1][0][c:c + 1], sf[1][1][c:c + 1])}, 1)[0]
+    def part(dim, parts, c):
+        s = parts.index(c)
+        return {dim: (sf[dim][0][s:s + 1], sf[dim][1][s:s + 1])}
+
+    d_x = lambda c: along(stress_sums[c:c + 1], part(2, X_PARTS, c), 2)[0]
+    d_y = lambda c: along(stress_sums[c:c + 1], part(3, Y_PARTS, c), 3)[0]
+    d_z = lambda c: along(stress_sums[c:c + 1], part(1, Z_PARTS, c), 1)[0]
     floored = jnp.maximum(cell_sums[9], mass_floor)
     force_x = d_x(0) + d_y(3) + d_z(5)
     force_y = d_x(3) + d_y(1) + d_z(4)
@@ -426,11 +471,11 @@
             (cell_sums[8] + time_step * force_z) / floored,
         ]
     )
-    vf, _ = exchange(velocity, sides, 1)
+    vf, _ = exchange(velocity, sides, 1, given=faces_by_kernel(velocity, ((0,), (1,), (2,))))
     dilation = (
-        along(velocity[0:1], {2: (vf[2][0][0:1], vf[2][1][0:1])}, 2)[0]
-        + along(velocity[1:2], {3: (vf[3][0][1:2], vf[3][1][1:2])}, 3)[0]
-        + along(velocity[2:3], {1: (vf[1][0][2:3], vf[1][1][2:3])}, 1)[0]
+        along(velocity[0:1], {2: vf[2]}, 2)[0]
+        + along(velocity[1:2], {3: vf[3]}, 3)[0]
+        + along(velocity[2:3], {1: vf[1]}, 1)[0]
     )
     right_side = -source_rate * (1.0 - porosity) * dilation
     _, (all_right,) = exchange(right_side, (), 3, (right_side,))
@@ -454,7 +499,8 @@
         jnp.concatenate([zero_level, solved, zero_level], axis=0), first, levels + 2, axis=0
     )
     pressure = around[1:-1]
-    pf, _ = exchange(pressure, (("gx", 1), ("gy", 2)), 2)
+    pressure_faces = [f[0] for f in faces_by_kernel(pressure[None], ((0,), (0,)))]
+    pf, _ = exchange(pressure, (("gx", 1), ("gy", 2)), 2, given=pressure_faces)
     gradient = jnp.stack(
         [
             along(pressure, pf, 1),

time: 96.2 us -> 89.9 us (0.935)
  local copies, waits for them, and re-layouts: 23.2 us -> 12.6 us
  other arithmetic: 3.39 us -> 6.01 us
  Pallas kernels: 66.7 us -> 68.5 us
    squeeze x6 -> x0, local copies, waits for them, and re-layouts: 4.69 us -> none  [the longest x4 2.95 us: exchange(): sends.append(lax.index_in_dim(cells, size - 1, axis=dim, keepdims=False))]
    pallas_call x0 -> x2, Pallas kernels: none -> 3.64 us  [faces_by_kernel(): pl.pallas_call(functools.partial(faces_kernel, parts), out_shape=[jax.Sha...]
    concatenate x14 -> x12, local copies, waits for them, and re-layouts: 4.06 us -> 2.52 us  [along(): jnp.concatenate([lower, lax.slice_in_dim(cells, 0, size - 1, axis=dim)],...]
    unnamed x37 -> x42, local copies, waits for them, and re-layouts: 8.26 us -> 6.84 us
    slice x6 -> x1, local copies, waits for them, and re-layouts: 2.18 us -> 0.78 us  [part(): return {dim: (sf[dim][0][s:s + 1], sf[dim][1][s:s + 1])}]
    pallas_call x4, Pallas kernels: 41.3 us -> 40.2 us  [exchange(): pl.pallas_call(functools.partial(halo_kernel, axes, sizes, len(gathers),...]
    concatenate x7 -> x5, local copies, waits for them, and re-layouts: 2.28 us -> 1.54 us  [along(): jnp.concatenate([lax.slice_in_dim(cells, 1, size, axis=dim), upper], axis...]
where the time goes in v9:
time: 89.9 us; the launch traced here: 89 us
  Pallas kernels  68.5 us (76%)
  local copies, waits for them, and re-layouts  12.6 us (14%)
  other arithmetic  6.01 us (7%)
  between operations  1.84 us (2%)
    pallas_call x4, Pallas kernels, exchange(): pl.pallas_call(functools.partial(halo_kernel, axes, sizes, len(gathers),...  40.2 us
    pallas_call x1, Pallas kernels, cell_sums_of(): pl.pallas_call(sums_kernel, out_shape=[jax.ShapeDtypeStruct(s, jnp.float3...  24.6 us
    unnamed x42, local copies, waits for them, and re-layouts  6.84 us
    pallas_call x2, Pallas kernels, faces_by_kernel(): pl.pallas_call(functools.partial(faces_kernel, parts), out_shape=[jax.Sha...  3.64 us
    concatenate x12, local copies, waits for them, and re-layouts, along(): jnp.concatenate([lower, lax.slice_in_dim(cells, 0, size - 1, axis=dim)],...  2.52 us

profile of v9, /device:TPU:121, one launch (start us, length us, event | category | flops | bytes accessed | tf_op | source)
XLA Modules:
  0.0 89.0 jit_solution(8624398848498035553)
XLA Ops:
  1.3 24.6 %shard_map.113 = (f32[10,16,8,128]{3,2,1,0:T(8,128)}, f32[3,16,128]{2,1,0:T(8,128)}, f32[3,16,128]{2,1,0:T(8,128)}, f32[3,16,8]{2,1,0:T(8,128)}, f32[3,16,8]{2,1...) custom-call(s32[1,1]{1,0:T(1,128)} %bitcast.136.count_ref, f32[6,24576]{1,0:T(8,128)} %st_ref.1, ...), custom_call_target="tpu_custom_call" | custom-call | flops 16106127360 | bytes 1933312 | tf_op jit(solution)/shard_map/pallas_call | solution.py:106
  25.9 14.2 %shard_map.114 = (f32[3,16,128]{2,1,0:T(8,128)}, f32[3,16,128]{2,1,0:T(8,128)}, f32[3,16,8]{2,1,0:T(8,128)}, f32[3,16,8]{2,1,0:T(8,128)}, f32[3,8,128]{2,1,0:T(8...) custom-call(f32[3,16,128]{2,1,0:T(8,128)} %get-tuple-element.38.refs_0_, ...), custom_call_target="tpu_custom_call" | custom-call | tf_op jit(solution)/shard_map/pallas_call | solution.py:351
  40.1 0.8 slice_bitcast_fusion.14
  40.9 0.2 copy.13
  41.0 0.2 copy.15
  41.2 0.8 fusion.56
  42.0 0.7 slice_bitcast_fusion.20
  42.7 0.0 copy-done
  42.7 0.1 fusion.30
  42.9 0.1 fusion.10
  43.0 0.2 copy.17
  43.2 0.2 copy.19
  43.3 0.1 fusion.15
  43.5 0.2 copy.21
  43.6 0.2 copy.23
  43.8 0.1 fusion.20
  43.9 0.7 pad_maximum_fusion.cells_ref
  44.6 1.9 %shard_map.115 = (f32[1,16,128]{2,1,0:T(8,128)}, f32[1,16,128]{2,1,0:T(8,128)}, f32[1,16,8]{2,1,0:T(8,128)}, f32[1,16,8]{2,1,0:T(8,128)}, f32[1,8,128]{2,1,0:T(8,128)}, /*index=5*/f32[1,8,128]{2,1,0:T(8,128)}) custom-call(f32[3,16,8,128]{3,2,1,0:T(8,128)} %pad_maximum_fusion.cells_ref), custom_call_target="tpu_custom_call" | custom-call | tf_op jit(solution)/shard_map/pallas_call | solution.py:397
  46.5 9.2 %shard_map.116 = (f32[1,16,128]{2,1,0:T(8,128)}, f32[1,16,128]{2,1,0:T(8,128)}, f32[1,16,8]{2,1,0:T(8,128)}, f32[1,16,8]{2,1,0:T(8,128)}, f32[1,8,128]{2,1,0:T(8,128)}, /*index=5*/f32[1,8,128]{2,1,0:T(8,128)}) custom-call(f32[1,16,128]{2,1,0:T(8,128)} %get-tuple-element.50.refs_0_, f32[1,16,128]{2,1,0:T(8,128)} %get-tuple-element.51.refs_1_, ...), custom_call_target="tpu_custom_call" | custom-call | tf_op jit(solution)/shard_map/pallas_call | solution.py:351
  55.7 0.0 copy-start.9
  55.7 0.9 copy.25
  56.6 0.0 copy-done.9
  56.6 0.2 copy.27
  56.8 0.1 slice_bitcast_fusion.4
  56.8 0.0 copy-start.5
  56.9 0.0 copy-start.6
  56.9 0.0 copy-start.12
  56.9 0.0 copy-start.13
  56.9 0.8 copy-done.4
  57.7 0.0 copy-done.5
  57.7 0.0 copy-done.6
  57.7 0.0 copy-done.12
  57.7 0.7 fusion.24.refs_0_
  58.4 8.3 %shard_map.117 = f32[4,16,8,128]{3,2,1,0:T(8,128)} custom-call(f32[16,8,128]{2,1,0:T(8,128)} %fusion.24.refs_0_), custom_call_target="tpu_custom_call" | custom-call | tf_op jit(solution)/shard_map/pallas_call | solution.py:351
  66.7 1.0 %copy.91 = f32[8,8,8,128]{3,1,2,0:T(8,128)S(1)} copy(f32[8,8,8,128]{3,2,1,0:T(8,128)} %bitcast.146) | data formatting | bytes 524288
  67.7 0.0 copy-start.2
  67.8 0.9 %copy-done.2 = f32[4,16,8,128]{3,2,1,0:T(8,128)S(1)} copy-done((f32[4,16,8,128]{3,2,1,0:T(8,128)S(1)}, f32[4,16,8,128]{3,2,1,0:T(8,128)}, u32[]{:S(2)}) %copy-start.2) | copy-done | bytes 262168
  68.7 0.9 %copy-done.3 = f32[4,16,8,128]{3,2,1,0:T(8,128)S(1)} copy-done((f32[4,16,8,128]{3,2,1,0:T(8,128)S(1)}, f32[4,16,8,128]{3,2,1,0:T(8,128)}, u32[]{:S(2)}) %copy-start.3) | copy-done | bytes 262168
  69.7 0.2 fusion.27
  69.9 0.1 fusion.48
  70.3 0.0 copy-start.1
  70.3 0.9 copy-done.1
  71.2 0.4 fusion
  71.9 0.4 multiply_add_fusion.7
  72.4 0.2 multiply_add_fusion.6
  72.6 0.3 multiply_add_fusion.5
  73.1 0.2 multiply_add_fusion.4
  73.3 0.3 multiply_add_fusion.3
  73.7 0.1 multiply_add_fusion.2
  73.9 0.3 multiply_add_fusion.1
  74.3 0.2 pad_multiply_fusion
  74.5 0.2 divide_bitcast_fusion
  74.8 0.6 fusion.55
  75.5 1.8 %shard_map.118 = (f32[1,16,128]{2,1,0:T(8,128)}, f32[1,16,128]{2,1,0:T(8,128)}, f32[1,16,8]{2,1,0:T(8,128)}, f32[1,16,8]{2,1,0:T(8,128)}) custom-call(f32[1,16,8,128]{3,2,1,0:T(8,128)} %bitcast.161), custom_call_target="tpu_custom_call" | custom-call | tf_op jit(solution)/shard_map/pallas_call | solution.py:397
  77.2 8.6 %shard_map.119 = (f32[16,128]{1,0:T(8,128)}, f32[16,128]{1,0:T(8,128)}, f32[16,8]{1,0:T(8,128)}, f32[16,8]{1,0:T(8,128)}) custom-call(f32[16,128]{1,0:T(8,128)} %bitcast.174, f32[16,128]{1,0:T(8,128)} %bitcast.175, f32[16,8]{1,0:T(8,128)} %bitcast.176, f32[16,8]{1,0:T(8,128)} %bitcast.177), custom_call_target="tpu_custom_call" | custom-call | tf_op jit(solution)/shard_map/pallas_call | solution.py:351
  85.8 0.7 copy-done.10
  86.5 0.0 copy-done.11
  86.6 0.7 copy-done.8
  87.2 0.2 copy.35
  87.4 0.5 copy-done.7
  87.9 0.2 copy.37
  88.1 0.1 slice_bitcast_fusion
  88.2 0.1 fusion.26
  88.3 0.7 fusion.1
  (54 shorter events, 1.4 us)
Async XLA Ops:
  25.9 16.8 %copy-start = (f32[10,16,8,128]{3,2,1,0:T(8,128)S(1)}, f32[10,16,8,128]{3,2,1,0:T(8,128)}, u32[]{:S(2)}) copy-start(f32[10,16,8,128]{3,2,1,0:T(8,128)} %get-tuple-element.37) | copy-start | bytes 1966084
  55.7 0.9 copy-start.9
  56.8 0.8 copy-start.4
  56.8 0.8 copy-start.5
  56.9 0.8 copy-start.6
  56.9 0.8 copy-start.12
  56.9 0.8 copy-start.13
  67.7 1.0 %copy-start.2 = (f32[4,16,8,128]{3,2,1,0:T(8,128)S(1)}, f32[4,16,8,128]{3,2,1,0:T(8,128)}, u32[]{:S(2)}) copy-start(f32[4,16,8,128]{3,2,1,0:T(8,128)} %get-tuple-element.62) | copy-start | bytes 786436
  68.7 0.9 %copy-start.3 = (f32[4,16,8,128]{3,2,1,0:T(8,128)S(1)}, f32[4,16,8,128]{3,2,1,0:T(8,128)}, u32[]{:S(2)}) copy-start(f32[4,16,8,128]{3,2,1,0:T(8,128)} %get-tuple-element.63) | copy-start | bytes 786436
  70.3 1.0 %copy-start.1 = (f32[4,16,8,128]{3,2,1,0:T(8,128)S(1)}, f32[4,16,8,128]{3,2,1,0:T(8,128)}, u32[]{:S(2)}) copy-start(f32[4,16,8,128]{3,2,1,0:T(8,128)} %shard_map.117) | copy-start | bytes 786436
  85.8 0.7 copy-start.10
  85.8 0.7 copy-start.11
  86.5 0.7 copy-start.8
  87.2 0.7 copy-start.7

commit v10 on v9

--- a/solution.py
+++ b/solution.py
@@ -402,6 +402,30 @@
     )(cells)
 
 
+def solve_kernel(poro_ref, perm_ref, right_ref, out_ref):
+    perm = perm_ref[...]
+    lid = jnp.zeros((1,) + perm.shape[1:], jnp.float32)
+    level_above = jnp.concatenate([perm[1:], lid], axis=0)
+    level_below = jnp.concatenate([lid, perm[:-1]], axis=0)
+    up_face = harmonic(perm, level_above)
+    down_face = harmonic(level_below, perm)
+    top_face = jnp.concatenate([up_face[:-1], perm[-1:]], axis=0)
+    lower_band = -time_step * down_face
+    upper_band = -time_step * up_face
+    main_band = storage_rate * poro_ref[...] + time_step * (down_face + top_face)
+    out_ref[...] = cyclic_solve(lower_band, main_band, upper_band, right_ref[...])
+
+
+def column_solve(porosity, permeability, right_side):
+    vmem = pl.BlockSpec(memory_space=pltpu.VMEM)
+    return pl.pallas_call(
+        solve_kernel,
+        out_shape=jax.ShapeDtypeStruct(right_side.shape, jnp.float32),
+        in_specs=[vmem] * 3,
+        out_specs=vmem,
+    )(porosity, permeability, right_side)
+
+
 def face_from(part, axis, from_lower):
     count = lax.axis_size(axis)
     if from_lower:
@@ -480,20 +504,7 @@
     right_side = -source_rate * (1.0 - porosity) * dilation
     _, (all_right,) = exchange(right_side, (), 3, (right_side,))
     zero_level = jnp.zeros((1, extent, breadth), jnp.float32)
-    level_above = jnp.concatenate([all_permeability[1:], zero_level], axis=0)
-    level_below = jnp.concatenate([zero_level, all_permeability[:-1]], axis=0)
-    at_top = (jnp.arange(height, dtype=jnp.int32) == height - 1)[:, None, None]
-    up_face = harmonic(all_permeability, level_above)
-    down_face = harmonic(level_below, all_permeability)
-    top_face = jnp.where(at_top, all_permeability, up_face)
-    lower_band = -time_step * down_face
-    upper_band = -time_step * up_face
-    main_band = storage_rate * all_porosity + time_step * (down_face + top_face)
-    column = height, extent * breadth
-    solved = cyclic_solve(
-        lower_band.reshape(column), main_band.reshape(column), upper_band.reshape(column),
-        all_right.reshape(column),
-    ).reshape(height, extent, breadth)
+    solved = column_solve(all_porosity, all_permeability, all_right)
     first = lax.axis_index("gz") * levels
     around = lax.dynamic_slice_in_dim(
         jnp.concatenate([zero_level, solved, zero_level], axis=0), first, levels + 2, axis=0

time: 89.9 us -> 85.6 us (0.952)
  local copies, waits for them, and re-layouts: 12.6 us -> 7.69 us
  Pallas kernels: 68.5 us -> 71.4 us
  other arithmetic: 6.01 us -> 4.17 us
    unnamed x42 -> x22, local copies, waits for them, and re-layouts: 6.84 us -> 2.68 us
    pallas_call x0 -> x1, Pallas kernels: none -> 2.81 us  [column_solve(): pl.pallas_call(solve_kernel, out_shape=jax.ShapeDtypeStruct(right_side.sh...]
    add x8 -> x0, other arithmetic: 2.14 us -> none  [the longest x4 1.3 us: cyclic_solve(): right_side + back_weight * earlier(right_side, stride, 0.0)]
where the time goes in v10:
time: 85.6 us; the launch traced here: 84.7 us
  Pallas kernels  71.4 us (83%)
  local copies, waits for them, and re-layouts  7.69 us (9%)
  other arithmetic  4.17 us (5%)
  between operations  1.45 us (2%)
    pallas_call x4, Pallas kernels, exchange(): pl.pallas_call(functools.partial(halo_kernel, axes, sizes, len(gathers),...  40.3 us
    pallas_call x1, Pallas kernels, cell_sums_of(): pl.pallas_call(sums_kernel, out_shape=[jax.ShapeDtypeStruct(s, jnp.float3...  24.6 us
    pallas_call x2, Pallas kernels, faces_by_kernel(): pl.pallas_call(functools.partial(faces_kernel, parts), out_shape=[jax.Sha...  3.64 us
    pallas_call x1, Pallas kernels, column_solve(): pl.pallas_call(solve_kernel, out_shape=jax.ShapeDtypeStruct(right_side.sh...  2.81 us
    unnamed x22, local copies, waits for them, and re-layouts  2.68 us
    concatenate x12, local copies, waits for them, and re-layouts, along(): jnp.concatenate([lower, lax.slice_in_dim(cells, 0, size - 1, axis=dim)],...  2.52 us

profile of v10, /device:TPU:121, one launch (start us, length us, event | category | flops | bytes accessed | tf_op | source)
XLA Modules:
  0.0 84.7 jit_solution(7561508305760739062)
XLA Ops:
  1.3 24.6 %shard_map.113 = (f32[10,16,8,128]{3,2,1,0:T(8,128)}, f32[3,16,128]{2,1,0:T(8,128)}, f32[3,16,128]{2,1,0:T(8,128)}, f32[3,16,8]{2,1,0:T(8,128)}, f32[3,16,8]{2,1...) custom-call(s32[1,1]{1,0:T(1,128)} %bitcast.78.count_ref, f32[6,24576]{1,0:T(8,128)} %st_ref.1, ...), custom_call_target="tpu_custom_call" | custom-call | flops 16106127360 | bytes 1933312 | tf_op jit(solution)/shard_map/pallas_call | solution.py:106
  25.9 0.0 copy-start
  25.9 14.2 %shard_map.114 = (f32[3,16,128]{2,1,0:T(8,128)}, f32[3,16,128]{2,1,0:T(8,128)}, f32[3,16,8]{2,1,0:T(8,128)}, f32[3,16,8]{2,1,0:T(8,128)}, f32[3,8,128]{2,1,0:T(8...) custom-call(f32[3,16,128]{2,1,0:T(8,128)} %get-tuple-element.38.refs_0_, ...), custom_call_target="tpu_custom_call" | custom-call | tf_op jit(solution)/shard_map/pallas_call | solution.py:351
  40.1 0.7 slice_bitcast_fusion.20
  40.8 0.8 slice_bitcast_fusion.14
  41.6 0.2 copy.13
  41.8 0.2 copy.15
  41.9 0.8 fusion.30
  42.7 0.0 copy-done
  42.7 0.1 fusion.27
  42.9 0.1 fusion.9
  43.0 0.2 copy.17
  43.2 0.2 copy.19
  43.4 0.1 fusion.14
  43.5 0.2 copy.21
  43.7 0.2 copy.23
  43.8 0.1 fusion.19
  44.0 0.7 pad_maximum_fusion.cells_ref
  44.6 1.9 %shard_map.115 = (f32[1,16,128]{2,1,0:T(8,128)}, f32[1,16,128]{2,1,0:T(8,128)}, f32[1,16,8]{2,1,0:T(8,128)}, f32[1,16,8]{2,1,0:T(8,128)}, f32[1,8,128]{2,1,0:T(8,128)}, /*index=5*/f32[1,8,128]{2,1,0:T(8,128)}) custom-call(f32[3,16,8,128]{3,2,1,0:T(8,128)} %pad_maximum_fusion.cells_ref), custom_call_target="tpu_custom_call" | custom-call | tf_op jit(solution)/shard_map/pallas_call | solution.py:397
  46.5 9.2 %shard_map.116 = (f32[1,16,128]{2,1,0:T(8,128)}, f32[1,16,128]{2,1,0:T(8,128)}, f32[1,16,8]{2,1,0:T(8,128)}, f32[1,16,8]{2,1,0:T(8,128)}, f32[1,8,128]{2,1,0:T(8,128)}, /*index=5*/f32[1,8,128]{2,1,0:T(8,128)}) custom-call(f32[1,16,128]{2,1,0:T(8,128)} %get-tuple-element.52.refs_0_, f32[1,16,128]{2,1,0:T(8,128)} %get-tuple-element.53.refs_1_, ...), custom_call_target="tpu_custom_call" | custom-call | tf_op jit(solution)/shard_map/pallas_call | solution.py:351
  55.7 0.0 copy-start.6
  55.8 0.9 %copy.25 = f32[16,8,1]{2,1,0:T(8,128)S(1)} copy(f32[16,8,1]{1,0,2:T(8,128)} %bitcast.94) | data formatting | bytes 1024 | tf_op jit(solution)/shard_map/concatenate | solution.py:452
  56.6 0.0 copy-done.6
  56.6 0.2 copy.27
  56.8 0.1 slice_bitcast_fusion.4
  56.9 0.0 copy-start.1
  56.9 0.0 copy-start.2
  56.9 0.0 copy-start.3
  56.9 0.0 copy-start.9
  56.9 0.0 copy-start.10
  56.9 0.8 copy-done.1
  57.7 0.0 copy-done.2
  57.7 0.0 copy-done.3
  57.7 0.0 copy-done.9
  57.7 0.0 copy-done.10
  57.7 0.7 fusion.23.refs_0_
  58.5 8.3 %shard_map.117 = f32[4,16,8,128]{3,2,1,0:T(8,128)} custom-call(f32[16,8,128]{2,1,0:T(8,128)} %fusion.23.refs_0_), custom_call_target="tpu_custom_call" | custom-call | tf_op jit(solution)/shard_map/pallas_call | solution.py:351
  66.8 2.8 %shard_map.118 = f32[64,8,128]{2,1,0:T(8,128)} custom-call(f32[64,8,128]{2,1,0:T(8,128)} %bitcast.81, f32[64,8,128]{2,1,0:T(8,128)} %bitcast.82, f32[64,8,128]{2,1,0:T(8,128)} %bitcast.79), custom_call_target="tpu_custom_call" | custom-call | tf_op jit(solution)/shard_map/pallas_call | solution.py:421
  69.6 0.9 %fusion.2 = f32[18,8,128]{2,1,0:T(8,128)S(1)} fusion(s32[]{:T(128)S(6)} %select_n.3, f32[1,8,128]{2,1,0:T(8,128)S(1)} %broadcast_in_dim.4, f32[64,8,128]{2,1,0:T(8,128)} %shard_map.118), kind=kLoop, calls=%fused_computation.7 | loop fusion | flops 36864 | bytes 339972 | tf_op jit(solution)/shard_map/concatenate | solution.py:510
  70.5 0.6 fusion.29
  71.2 1.8 %shard_map.119 = (f32[1,16,128]{2,1,0:T(8,128)}, f32[1,16,128]{2,1,0:T(8,128)}, f32[1,16,8]{2,1,0:T(8,128)}, f32[1,16,8]{2,1,0:T(8,128)}) custom-call(f32[1,16,8,128]{3,2,1,0:T(8,128)} %bitcast.80), custom_call_target="tpu_custom_call" | custom-call | tf_op jit(solution)/shard_map/pallas_call | solution.py:397
  72.9 8.6 %shard_map.120 = (f32[16,128]{1,0:T(8,128)}, f32[16,128]{1,0:T(8,128)}, f32[16,8]{1,0:T(8,128)}, f32[16,8]{1,0:T(8,128)}) custom-call(f32[16,128]{1,0:T(8,128)} %bitcast.95, f32[16,128]{1,0:T(8,128)} %bitcast.96, f32[16,8]{1,0:T(8,128)} %bitcast.97, f32[16,8]{1,0:T(8,128)} %bitcast.98), custom_call_target="tpu_custom_call" | custom-call | tf_op jit(solution)/shard_map/pallas_call | solution.py:351
  81.5 0.0 copy-start.7
  81.5 0.0 copy-start.8
  81.5 0.7 copy-done.7
  82.2 0.0 copy-done.8
  82.2 0.0 copy-start.5
  82.2 0.7 copy-done.5
  82.9 0.0 copy-start.4
  82.9 0.2 copy.35
  83.1 0.5 copy-done.4
  83.6 0.2 copy.37
  83.8 0.1 slice_bitcast_fusion
  83.8 0.1 fusion.25
  84.0 0.7 fusion
  (7 shorter events, 0.1 us)
Async XLA Ops:
  25.9 16.8 %copy-start = (f32[10,16,8,128]{3,2,1,0:T(8,128)S(1)}, f32[10,16,8,128]{3,2,1,0:T(8,128)}, u32[]{:S(2)}) copy-start(f32[10,16,8,128]{3,2,1,0:T(8,128)} %get-tuple-element.37) | copy-start | bytes 1966084
  55.7 0.9 %copy-start.6 = (f32[1,16,8]{2,1,0:T(8,128)S(1)}, f32[1,16,8]{2,1,0:T(8,128)}, u32[]{:S(2)}) copy-start(f32[1,16,8]{2,1,0:T(8,128)} %get-tuple-element.61) | copy-start | bytes 1540
  56.9 0.8 %copy-start.1 = (f32[16,8,128]{2,1,0:T(8,128)S(1)}, f32[16,8,128]{2,1,0:T(8,128)}, u32[]{:S(2)}) copy-start(f32[16,8,128]{2,1,0:T(8,128)} %refs_6_.1) | copy-start | bytes 196612
  56.9 0.8 copy-start.2
  56.9 0.8 copy-start.3
  56.9 0.8 copy-start.9
  56.9 0.8 copy-start.10
  81.5 0.7 copy-start.7
  81.5 0.7 copy-start.8
  82.2 0.7 copy-start.5
  82.9 0.7 copy-start.4

commit v11 on v10

--- a/solution.py
+++ b/solution.py
@@ -402,7 +402,7 @@
     )(cells)
 
 
-def solve_kernel(poro_ref, perm_ref, right_ref, out_ref):
+def solve_kernel(levels, poro_ref, perm_ref, right_ref, out_ref, grad_ref, xlo, xhi, ylo, yhi, padded_ref):
     perm = perm_ref[...]
     lid = jnp.zeros((1,) + perm.shape[1:], jnp.float32)
     level_above = jnp.concatenate([perm[1:], lid], axis=0)
@@ -413,16 +413,33 @@
     lower_band = -time_step * down_face
     upper_band = -time_step * up_face
     main_band = storage_rate * poro_ref[...] + time_step * (down_face + top_face)
-    out_ref[...] = cyclic_solve(lower_band, main_band, upper_band, right_ref[...])
-
-
-def column_solve(porosity, permeability, right_side):
+    solved = cyclic_solve(lower_band, main_band, upper_band, right_ref[...])
+    height, extent, breadth = solved.shape
+    padded_ref[pl.ds(0, 1)] = lid
+    padded_ref[pl.ds(height + 1, 1)] = lid
+    padded_ref[pl.ds(1, height)] = solved
+    first = lax.axis_index("gz") * levels
+    out_ref[...] = padded_ref[pl.ds(first + 1, levels)]
+    grad_ref[...] = (padded_ref[pl.ds(first + 2, levels)] - padded_ref[pl.ds(first, levels)]) * 0.5
+    for level in range(levels):
+        tile = out_ref[level]
+        xlo[pl.ds(level, 1), :] = tile[0:1, :]
+        xhi[pl.ds(level, 1), :] = tile[extent - 1:extent, :]
+        turned = tile.T
+        ylo[pl.ds(level, 1), :] = turned[0:1, :]
+        yhi[pl.ds(level, 1), :] = turned[breadth - 1:breadth, :]
+
+
+def column_solve(porosity, permeability, right_side, levels):
+    height, extent, breadth = right_side.shape
     vmem = pl.BlockSpec(memory_space=pltpu.VMEM)
+    shapes = [(levels, extent, breadth)] * 2 + [(levels, breadth)] * 2 + [(levels, extent)] * 2
     return pl.pallas_call(
-        solve_kernel,
-        out_shape=jax.ShapeDtypeStruct(right_side.shape, jnp.float32),
+        functools.partial(solve_kernel, levels),
+        out_shape=[jax.ShapeDtypeStruct(s, jnp.float32) for s in shapes],
         in_specs=[vmem] * 3,
-        out_specs=vmem,
+        out_specs=[vmem] * len(shapes),
+        scratch_shapes=[pltpu.VMEM((height + 2, extent, breadth), jnp.float32)],
     )(porosity, permeability, right_side)
 
 
@@ -504,21 +521,9 @@
     right_side = -source_rate * (1.0 - porosity) * dilation
     _, (all_right,) = exchange(right_side, (), 3, (right_side,))
     zero_level = jnp.zeros((1, extent, breadth), jnp.float32)
-    solved = column_solve(all_porosity, all_permeability, all_right)
-    first = lax.axis_index("gz") * levels
-    around = lax.dynamic_slice_in_dim(
-        jnp.concatenate([zero_level, solved, zero_level], axis=0), first, levels + 2, axis=0
-    )
-    pressure = around[1:-1]
-    pressure_faces = [f[0] for f in faces_by_kernel(pressure[None], ((0,), (0,)))]
+    pressure, rise, *pressure_faces = column_solve(all_porosity, all_permeability, all_right, levels)
     pf, _ = exchange(pressure, (("gx", 1), ("gy", 2)), 2, given=pressure_faces)
-    gradient = jnp.stack(
-        [
-            along(pressure, pf, 1),
-            along(pressure, pf, 2),
-            (around[2:] - around[:-2]) * 0.5,
-        ]
-    )
+    gradient = jnp.stack([along(pressure, pf, 1), along(pressure, pf, 2), rise])
     return (velocity - time_step * gradient, pressure)
 
 

time: 85.6 us -> 84.1 us (0.982)
  Pallas kernels: 71.4 us -> 69.7 us
  local copies, waits for them, and re-layouts: 7.69 us -> 9.33 us
  other arithmetic: 4.17 us -> 2.62 us
    unnamed x22 -> x34, local copies, waits for them, and re-layouts: 2.68 us -> 4.79 us
    pallas_call x2 -> x1, Pallas kernels: 3.64 us -> 1.88 us  [faces_by_kernel(): pl.pallas_call(functools.partial(faces_kernel, parts), out_shape=[jax.Sha...]
    concatenate x12, local copies, waits for them, and re-layouts: 2.52 us -> 1.04 us  [along(): jnp.concatenate([lower, lax.slice_in_dim(cells, 0, size - 1, axis=dim)],...]
    slice x3, local copies, waits for them, and re-layouts: 0.16 us -> 1.18 us  [along(): lax.slice_in_dim(cells, 0, size - 1, axis=dim)]
    concatenate x1 -> x0, other arithmetic: 0.9 us -> none  [shards(): jnp.concatenate([zero_level, solved, zero_level], axis=0)]
where the time goes in v11:
time: 84.1 us; the launch traced here: 83.1 us
  Pallas kernels  69.7 us (83%)
  local copies, waits for them, and re-layouts  9.33 us (11%)
  other arithmetic  2.62 us (3%)
  between operations  1.46 us (2%)
    pallas_call x4, Pallas kernels, exchange(): pl.pallas_call(functools.partial(halo_kernel, axes, sizes, len(gathers),...  40.4 us
    pallas_call x1, Pallas kernels, cell_sums_of(): pl.pallas_call(sums_kernel, out_shape=[jax.ShapeDtypeStruct(s, jnp.float3...  24.6 us
    unnamed x34, local copies, waits for them, and re-layouts  4.79 us
    pallas_call x1, Pallas kernels, column_solve(): pl.pallas_call(functools.partial(solve_kernel, levels), out_shape=[jax.Sh...  2.84 us
    pallas_call x1, Pallas kernels, faces_by_kernel(): pl.pallas_call(functools.partial(faces_kernel, parts), out_shape=[jax.Sha...  1.88 us

profile of v11, /device:TPU:121, one launch (start us, length us, event | category | flops | bytes accessed | tf_op | source)
XLA Modules:
  0.0 83.1 jit_solution(480068229889500403)
XLA Ops:
  1.3 24.6 %shard_map.113 = (f32[10,16,8,128]{3,2,1,0:T(8,128)}, f32[3,16,128]{2,1,0:T(8,128)}, f32[3,16,128]{2,1,0:T(8,128)}, f32[3,16,8]{2,1,0:T(8,128)}, f32[3,16,8]{2,1...) custom-call(s32[1,1]{1,0:T(1,128)} %bitcast.72.count_ref, f32[6,24576]{1,0:T(8,128)} %st_ref.1, ...), custom_call_target="tpu_custom_call" | custom-call | flops 16106127360 | bytes 1933312 | tf_op jit(solution)/shard_map/pallas_call | solution.py:106
  25.9 0.0 copy-start
  25.9 14.2 %shard_map.114 = (f32[3,16,128]{2,1,0:T(8,128)}, f32[3,16,128]{2,1,0:T(8,128)}, f32[3,16,8]{2,1,0:T(8,128)}, f32[3,16,8]{2,1,0:T(8,128)}, f32[3,8,128]{2,1,0:T(8...) custom-call(f32[3,16,128]{2,1,0:T(8,128)} %get-tuple-element.40.refs_0_, ...), custom_call_target="tpu_custom_call" | custom-call | tf_op jit(solution)/shard_map/pallas_call | solution.py:351
  40.1 0.8 fusion.25
  40.9 0.0 copy-start.4
  40.9 0.0 copy-start.5
  40.9 1.0 %fusion.24 = (f32[1,16,7,128]{3,2,1,0:T(8,128)S(1)}, f32[1,16,7,128]{3,2,1,0:T(8,128)S(1)}, f32[1,16,7,128]{3,2,1,0:T(8,128)S(1)}, f32[1,16,7,128]{3,2,1,0:T(8,1...) fusion(f32[10,16,8,128]{3,2,1,0:T(8,128)} %get-tuple-element.39), kind=kLoop, calls=%fused_computation.63 | loop fusion | bytes 688128 | tf_op jit(solution)/shard_map/slice | solution.py:470
  41.9 0.0 copy-done.4
  41.9 0.0 copy-done.5
  42.0 0.2 copy.21
  42.1 0.0 copy-done
  42.1 0.1 fusion.23
  42.3 0.0 copy-start.6
  42.3 0.0 copy-start.7
  42.3 0.2 copy.23
  42.4 0.5 copy-done.6
  43.0 0.0 copy-done.7
  43.0 0.1 fusion.15
  43.1 0.2 copy.17
  43.3 0.2 copy.19
  43.5 0.1 fusion.10
  43.6 0.2 copy.13
  43.8 0.2 copy.15
  43.9 0.1 fusion.5
  44.0 0.7 pad_maximum_fusion.cells_ref
  44.7 1.9 %shard_map.115 = (f32[1,16,128]{2,1,0:T(8,128)}, f32[1,16,128]{2,1,0:T(8,128)}, f32[1,16,8]{2,1,0:T(8,128)}, f32[1,16,8]{2,1,0:T(8,128)}, f32[1,8,128]{2,1,0:T(8,128)}, /*index=5*/f32[1,8,128]{2,1,0:T(8,128)}) custom-call(f32[3,16,8,128]{3,2,1,0:T(8,128)} %pad_maximum_fusion.cells_ref), custom_call_target="tpu_custom_call" | custom-call | tf_op jit(solution)/shard_map/pallas_call | solution.py:397
  46.6 9.2 %shard_map.116 = (f32[1,16,128]{2,1,0:T(8,128)}, f32[1,16,128]{2,1,0:T(8,128)}, f32[1,16,8]{2,1,0:T(8,128)}, f32[1,16,8]{2,1,0:T(8,128)}, f32[1,8,128]{2,1,0:T(8,128)}, /*index=5*/f32[1,8,128]{2,1,0:T(8,128)}) custom-call(f32[1,16,128]{2,1,0:T(8,128)} %get-tuple-element.54.refs_0_, f32[1,16,128]{2,1,0:T(8,128)} %get-tuple-element.55.refs_1_, ...), custom_call_target="tpu_custom_call" | custom-call | tf_op jit(solution)/shard_map/pallas_call | solution.py:351
  55.9 0.0 copy-start.11
  55.9 0.7 copy-done.11
  56.6 0.2 copy.25
  56.7 0.0 copy-start.10
  56.7 0.1 slice_bitcast_fusion
  56.8 0.6 copy-done.10
  57.4 0.2 copy.27
  57.6 0.0 copy-start.2
  57.6 0.0 copy-start.8
  57.6 0.0 copy-start.9
  57.6 0.0 copy-start.16
  57.6 0.0 copy-start.15
  57.6 0.8 copy-done.2
  58.4 0.0 copy-done.8
  58.4 0.0 copy-done.9
  58.4 0.0 copy-done.16
  58.4 0.0 copy-done.15
  58.5 0.7 fusion.19.refs_0_
  59.2 8.3 %shard_map.117 = f32[4,16,8,128]{3,2,1,0:T(8,128)} custom-call(f32[16,8,128]{2,1,0:T(8,128)} %fusion.19.refs_0_), custom_call_target="tpu_custom_call" | custom-call | tf_op jit(solution)/shard_map/pallas_call | solution.py:351
  67.5 2.8 %shard_map.118 = (f32[16,8,128]{2,1,0:T(8,128)}, f32[16,8,128]{2,1,0:T(8,128)}, f32[16,128]{1,0:T(8,128)}, f32[16,128]{1,0:T(8,128)}, f32[16,8]{1,0:T(8,128)}, /*index=5*/f32[16,8]{1,0:T(8,128)}) custom-call(f32[64,8,128]{2,1,0:T(8,128)} %bitcast.74, f32[64,8,128]{2,1,0:T(8,128)} %bitcast.75, f32[64,8,128]{2,1,0:T(8,128)} %bitcast.73), custom_call_target="tpu_custom_call" | custom-call | tf_op jit(solution)/shard_map/pallas_call | solution.py:437
  70.3 0.0 copy-start.1
  70.3 8.7 %shard_map.119 = (f32[16,128]{1,0:T(8,128)}, f32[16,128]{1,0:T(8,128)}, f32[16,8]{1,0:T(8,128)}, f32[16,8]{1,0:T(8,128)}) custom-call(f32[16,128]{1,0:T(8,128)} %get-tuple-element.67.refs_0_, f32[16,128]{1,0:T(8,128)} %get-tuple-element.68.refs_1_, f32[16,8]{1,0:T(8,128)} %get-tuple-element.69.refs_2_, f32[16,8]{1,0:T(8,128)} %get-tuple-element.70.refs_3_), custom_call_target="tpu_custom_call" | custom-call | tf_op jit(solution)/shard_map/pallas_call | solution.py:351
  79.0 0.9 %copy.31 = f32[1,16,8,1]{3,2,1,0:T(8,128)S(1)} copy(f32[1,16,8,1]{2,1,3,0:T(8,128)} %bitcast.88) | data formatting | bytes 1024 | tf_op jit(solution)/shard_map/concatenate | solution.py:469
  79.9 0.0 copy-done.1
  79.9 0.0 copy-start.12
  79.9 0.1 slice_bitcast_fusion.4
  80.0 0.6 copy-done.12
  80.6 0.2 copy.33
  80.7 0.1 fusion.21
  80.9 0.0 copy-start.13
  80.9 0.0 copy-start.14
  80.9 0.7 copy-done.13
  81.6 0.0 copy-done.14
  81.6 0.0 copy-start.3
  81.6 0.8 copy-done.3
  82.4 0.7 fusion
  (7 shorter events, 0.1 us)
Async XLA Ops:
  25.9 16.2 %copy-start = (f32[10,16,8,128]{3,2,1,0:T(8,128)S(1)}, f32[10,16,8,128]{3,2,1,0:T(8,128)}, u32[]{:S(2)}) copy-start(f32[10,16,8,128]{3,2,1,0:T(8,128)} %get-tuple-element.39) | copy-start | bytes 1966084
  40.9 1.1 %copy-start.4 = (f32[3,16,8]{2,1,0:T(8,128)S(1)}, f32[3,16,8]{2,1,0:T(8,128)}, u32[]{:S(2)}) copy-start(f32[3,16,8]{2,1,0:T(8,128)} %get-tuple-element.49) | copy-start | bytes 4612
  40.9 1.1 %copy-start.5 = (f32[3,16,8]{2,1,0:T(8,128)S(1)}, f32[3,16,8]{2,1,0:T(8,128)}, u32[]{:S(2)}) copy-start(f32[3,16,8]{2,1,0:T(8,128)} %get-tuple-element.48) | copy-start | bytes 4612
  42.3 0.7 copy-start.6
  42.3 0.7 copy-start.7
  55.9 0.7 copy-start.11
  56.7 0.7 copy-start.10
  57.6 0.8 %copy-start.2 = (f32[16,8,128]{2,1,0:T(8,128)S(1)}, f32[16,8,128]{2,1,0:T(8,128)}, u32[]{:S(2)}) copy-start(f32[16,8,128]{2,1,0:T(8,128)} %refs_6_.1) | copy-start | bytes 196612
  57.6 0.8 %copy-start.8 = (f32[1,16,128]{2,1,0:T(8,128)S(1)}, f32[1,16,128]{2,1,0:T(8,128)}, u32[]{:S(2)}) copy-start(f32[1,16,128]{2,1,0:T(8,128)} %get-tuple-element.61) | copy-start | bytes 24580
  57.6 0.8 %copy-start.9 = (f32[1,16,128]{2,1,0:T(8,128)S(1)}, f32[1,16,128]{2,1,0:T(8,128)}, u32[]{:S(2)}) copy-start(f32[1,16,128]{2,1,0:T(8,128)} %get-tuple-element.60) | copy-start | bytes 24580
  57.6 0.8 %copy-start.16 = (f32[1,8,128]{2,1,0:T(8,128)S(1)}, f32[1,8,128]{2,1,0:T(8,128)}, u32[]{:S(2)}) copy-start(f32[1,8,128]{2,1,0:T(8,128)} %get-tuple-element.64) | copy-start | bytes 12292
  57.6 0.8 copy-start.15
  70.3 9.6 %copy-start.1 = (f32[16,8,128]{2,1,0:T(8,128)S(1)}, f32[16,8,128]{2,1,0:T(8,128)}, u32[]{:S(2)}) copy-start(f32[16,8,128]{2,1,0:T(8,128)} %get-tuple-element.38) | copy-start | bytes 196612
  79.9 0.7 copy-start.12
  80.9 0.7 copy-start.13
  80.9 0.7 copy-start.14
  81.6 0.8 %copy-start.3 = (f32[16,8,128]{2,1,0:T(8,128)S(1)}, f32[16,8,128]{2,1,0:T(8,128)}, u32[]{:S(2)}) copy-start(f32[16,8,128]{2,1,0:T(8,128)} %get-tuple-element.75) | copy-start | bytes 196612

commit v12 on v11

--- a/solution.py
+++ b/solution.py
@@ -15,7 +15,7 @@
 from jax.experimental import pallas as pl
 from jax.experimental.pallas import tpu as pltpu
 
-CHUNK = 1024
+CHUNK = 2048
 M_ROWS = 32
 N_COLS = 512
 

time: 84.1 us -> 81.5 us (0.969)
  Pallas kernels: 69.7 us -> 67.1 us
    pallas_call x1, Pallas kernels: 24.6 us -> 22 us  [cell_sums_of(): pl.pallas_call(sums_kernel, out_shape=[jax.ShapeDtypeStruct(s, jnp.float3...]
where the time goes in v12:
time: 81.5 us; the launch traced here: 80.5 us
  Pallas kernels  67.1 us (82%)
  local copies, waits for them, and re-layouts  9.33 us (11%)
  other arithmetic  2.62 us (3%)
  between operations  1.46 us (2%)
    pallas_call x4, Pallas kernels, exchange(): pl.pallas_call(functools.partial(halo_kernel, axes, sizes, len(gathers),...  40.4 us
    pallas_call x1, Pallas kernels, cell_sums_of(): pl.pallas_call(sums_kernel, out_shape=[jax.ShapeDtypeStruct(s, jnp.float3...  22 us
    unnamed x34, local copies, waits for them, and re-layouts  4.79 us
    pallas_call x1, Pallas kernels, column_solve(): pl.pallas_call(functools.partial(solve_kernel, levels), out_shape=[jax.Sh...  2.84 us
    pallas_call x1, Pallas kernels, faces_by_kernel(): pl.pallas_call(functools.partial(faces_kernel, parts), out_shape=[jax.Sha...  1.88 us

profile of v12, /device:TPU:121, one launch (start us, length us, event | category | flops | bytes accessed | tf_op | source)
XLA Modules:
  0.0 80.5 jit_solution(1187566420150891237)
XLA Ops:
  1.3 22.0 %shard_map.113 = (f32[10,16,8,128]{3,2,1,0:T(8,128)}, f32[3,16,128]{2,1,0:T(8,128)}, f32[3,16,128]{2,1,0:T(8,128)}, f32[3,16,8]{2,1,0:T(8,128)}, f32[3,16,8]{2,1...) custom-call(s32[1,1]{1,0:T(1,128)} %bitcast.72.count_ref, f32[6,24576]{1,0:T(8,128)} %st_ref.1, ...), custom_call_target="tpu_custom_call" | custom-call | flops 16106127360 | bytes 1933312 | tf_op jit(solution)/shard_map/pallas_call | solution.py:106
  23.3 0.0 copy-start
  23.3 14.2 %shard_map.114 = (f32[3,16,128]{2,1,0:T(8,128)}, f32[3,16,128]{2,1,0:T(8,128)}, f32[3,16,8]{2,1,0:T(8,128)}, f32[3,16,8]{2,1,0:T(8,128)}, f32[3,8,128]{2,1,0:T(8...) custom-call(f32[3,16,128]{2,1,0:T(8,128)} %get-tuple-element.40.refs_0_, ...), custom_call_target="tpu_custom_call" | custom-call | tf_op jit(solution)/shard_map/pallas_call | solution.py:351
  37.5 0.8 fusion.25
  38.2 0.0 copy-start.4
  38.2 0.0 copy-start.5
  38.3 1.0 %fusion.24 = (f32[1,16,7,128]{3,2,1,0:T(8,128)S(1)}, f32[1,16,7,128]{3,2,1,0:T(8,128)S(1)}, f32[1,16,7,128]{3,2,1,0:T(8,128)S(1)}, f32[1,16,7,128]{3,2,1,0:T(8,1...) fusion(f32[10,16,8,128]{3,2,1,0:T(8,128)} %get-tuple-element.39), kind=kLoop, calls=%fused_computation.63 | loop fusion | bytes 688128 | tf_op jit(solution)/shard_map/slice | solution.py:470
  39.3 0.0 copy-done.4
  39.3 0.0 copy-done.5
  39.3 0.2 copy.21
  39.5 0.0 copy-done
  39.5 0.1 fusion.23
  39.6 0.0 copy-start.6
  39.6 0.0 copy-start.7
  39.6 0.2 copy.23
  39.8 0.5 copy-done.6
  40.3 0.0 copy-done.7
  40.4 0.1 fusion.15
  40.5 0.2 copy.17
  40.7 0.2 copy.19
  40.8 0.1 fusion.10
  41.0 0.2 copy.13
  41.1 0.2 copy.15
  41.3 0.1 fusion.5
  41.4 0.7 pad_maximum_fusion.cells_ref
  42.1 1.9 %shard_map.115 = (f32[1,16,128]{2,1,0:T(8,128)}, f32[1,16,128]{2,1,0:T(8,128)}, f32[1,16,8]{2,1,0:T(8,128)}, f32[1,16,8]{2,1,0:T(8,128)}, f32[1,8,128]{2,1,0:T(8,128)}, /*index=5*/f32[1,8,128]{2,1,0:T(8,128)}) custom-call(f32[3,16,8,128]{3,2,1,0:T(8,128)} %pad_maximum_fusion.cells_ref), custom_call_target="tpu_custom_call" | custom-call | tf_op jit(solution)/shard_map/pallas_call | solution.py:397
  44.0 9.2 %shard_map.116 = (f32[1,16,128]{2,1,0:T(8,128)}, f32[1,16,128]{2,1,0:T(8,128)}, f32[1,16,8]{2,1,0:T(8,128)}, f32[1,16,8]{2,1,0:T(8,128)}, f32[1,8,128]{2,1,0:T(8,128)}, /*index=5*/f32[1,8,128]{2,1,0:T(8,128)}) custom-call(f32[1,16,128]{2,1,0:T(8,128)} %get-tuple-element.54.refs_0_, f32[1,16,128]{2,1,0:T(8,128)} %get-tuple-element.55.refs_1_, ...), custom_call_target="tpu_custom_call" | custom-call | tf_op jit(solution)/shard_map/pallas_call | solution.py:351
  53.2 0.0 copy-start.11
  53.2 0.7 copy-done.11
  53.9 0.2 copy.25
  54.1 0.0 copy-start.10
  54.1 0.1 slice_bitcast_fusion
  54.2 0.6 copy-done.10
  54.8 0.2 copy.27
  55.0 0.0 copy-start.2
  55.0 0.0 copy-start.8
  55.0 0.0 copy-start.9
  55.0 0.0 copy-start.16
  55.0 0.0 copy-start.15
  55.0 0.8 copy-done.2
  55.8 0.0 copy-done.8
  55.8 0.0 copy-done.9
  55.8 0.0 copy-done.16
  55.8 0.0 copy-done.15
  55.8 0.7 fusion.19.refs_0_
  56.6 8.3 %shard_map.117 = f32[4,16,8,128]{3,2,1,0:T(8,128)} custom-call(f32[16,8,128]{2,1,0:T(8,128)} %fusion.19.refs_0_), custom_call_target="tpu_custom_call" | custom-call | tf_op jit(solution)/shard_map/pallas_call | solution.py:351
  64.8 2.8 %shard_map.118 = (f32[16,8,128]{2,1,0:T(8,128)}, f32[16,8,128]{2,1,0:T(8,128)}, f32[16,128]{1,0:T(8,128)}, f32[16,128]{1,0:T(8,128)}, f32[16,8]{1,0:T(8,128)}, /*index=5*/f32[16,8]{1,0:T(8,128)}) custom-call(f32[64,8,128]{2,1,0:T(8,128)} %bitcast.74, f32[64,8,128]{2,1,0:T(8,128)} %bitcast.75, f32[64,8,128]{2,1,0:T(8,128)} %bitcast.73), custom_call_target="tpu_custom_call" | custom-call | tf_op jit(solution)/shard_map/pallas_call | solution.py:437
  67.7 0.0 copy-start.1
  67.7 8.7 %shard_map.119 = (f32[16,128]{1,0:T(8,128)}, f32[16,128]{1,0:T(8,128)}, f32[16,8]{1,0:T(8,128)}, f32[16,8]{1,0:T(8,128)}) custom-call(f32[16,128]{1,0:T(8,128)} %get-tuple-element.67.refs_0_, f32[16,128]{1,0:T(8,128)} %get-tuple-element.68.refs_1_, f32[16,8]{1,0:T(8,128)} %get-tuple-element.69.refs_2_, f32[16,8]{1,0:T(8,128)} %get-tuple-element.70.refs_3_), custom_call_target="tpu_custom_call" | custom-call | tf_op jit(solution)/shard_map/pallas_call | solution.py:351
  76.4 0.9 %copy.31 = f32[1,16,8,1]{3,2,1,0:T(8,128)S(1)} copy(f32[1,16,8,1]{2,1,3,0:T(8,128)} %bitcast.88) | data formatting | bytes 1024 | tf_op jit(solution)/shard_map/concatenate | solution.py:469
  77.3 0.0 copy-done.1
  77.3 0.0 copy-start.12
  77.3 0.1 slice_bitcast_fusion.4
  77.3 0.6 copy-done.12
  78.0 0.2 copy.33
  78.1 0.1 fusion.21
  78.2 0.0 copy-start.13
  78.2 0.0 copy-start.14
  78.3 0.7 copy-done.13
  78.9 0.0 copy-done.14
  78.9 0.0 copy-start.3
  79.0 0.8 copy-done.3
  79.8 0.7 fusion
  (7 shorter events, 0.1 us)
Async XLA Ops:
  23.3 16.2 %copy-start = (f32[10,16,8,128]{3,2,1,0:T(8,128)S(1)}, f32[10,16,8,128]{3,2,1,0:T(8,128)}, u32[]{:S(2)}) copy-start(f32[10,16,8,128]{3,2,1,0:T(8,128)} %get-tuple-element.39) | copy-start | bytes 1966084
  38.2 1.1 %copy-start.4 = (f32[3,16,8]{2,1,0:T(8,128)S(1)}, f32[3,16,8]{2,1,0:T(8,128)}, u32[]{:S(2)}) copy-start(f32[3,16,8]{2,1,0:T(8,128)} %get-tuple-element.49) | copy-start | bytes 4612
  38.2 1.1 %copy-start.5 = (f32[3,16,8]{2,1,0:T(8,128)S(1)}, f32[3,16,8]{2,1,0:T(8,128)}, u32[]{:S(2)}) copy-start(f32[3,16,8]{2,1,0:T(8,128)} %get-tuple-element.48) | copy-start | bytes 4612
  39.6 0.7 copy-start.6
  39.6 0.7 copy-start.7
  53.2 0.7 copy-start.11
  54.1 0.7 copy-start.10
  55.0 0.8 %copy-start.2 = (f32[16,8,128]{2,1,0:T(8,128)S(1)}, f32[16,8,128]{2,1,0:T(8,128)}, u32[]{:S(2)}) copy-start(f32[16,8,128]{2,1,0:T(8,128)} %refs_6_.1) | copy-start | bytes 196612
  55.0 0.8 %copy-start.8 = (f32[1,16,128]{2,1,0:T(8,128)S(1)}, f32[1,16,128]{2,1,0:T(8,128)}, u32[]{:S(2)}) copy-start(f32[1,16,128]{2,1,0:T(8,128)} %get-tuple-element.61) | copy-start | bytes 24580
  55.0 0.8 %copy-start.9 = (f32[1,16,128]{2,1,0:T(8,128)S(1)}, f32[1,16,128]{2,1,0:T(8,128)}, u32[]{:S(2)}) copy-start(f32[1,16,128]{2,1,0:T(8,128)} %get-tuple-element.60) | copy-start | bytes 24580
  55.0 0.8 %copy-start.16 = (f32[1,8,128]{2,1,0:T(8,128)S(1)}, f32[1,8,128]{2,1,0:T(8,128)}, u32[]{:S(2)}) copy-start(f32[1,8,128]{2,1,0:T(8,128)} %get-tuple-element.64) | copy-start | bytes 12292
  55.0 0.8 %copy-start.15 = (f32[1,8,128]{2,1,0:T(8,128)S(1)}, f32[1,8,128]{2,1,0:T(8,128)}, u32[]{:S(2)}) copy-start(f32[1,8,128]{2,1,0:T(8,128)} %get-tuple-element.65) | copy-start | bytes 12292
  67.7 9.6 %copy-start.1 = (f32[16,8,128]{2,1,0:T(8,128)S(1)}, f32[16,8,128]{2,1,0:T(8,128)}, u32[]{:S(2)}) copy-start(f32[16,8,128]{2,1,0:T(8,128)} %get-tuple-element.38) | copy-start | bytes 196612
  77.3 0.7 copy-start.12
  78.2 0.7 copy-start.13
  78.2 0.7 copy-start.14
  78.9 0.8 %copy-start.3 = (f32[16,8,128]{2,1,0:T(8,128)S(1)}, f32[16,8,128]{2,1,0:T(8,128)}, u32[]{:S(2)}) copy-start(f32[16,8,128]{2,1,0:T(8,128)} %get-tuple-element.75) | copy-start | bytes 196612

commit v13 on v12

--- a/solution.py
+++ b/solution.py
@@ -15,7 +15,7 @@
 from jax.experimental import pallas as pl
 from jax.experimental.pallas import tpu as pltpu
 
-CHUNK = 2048
+CHUNK = 4096
 M_ROWS = 32
 N_COLS = 512
 

time: 81.5 us -> 80.2 us (0.984)
  Pallas kernels: 67.1 us -> 65.8 us
    pallas_call x1, Pallas kernels: 22 us -> 20.7 us  [cell_sums_of(): pl.pallas_call(sums_kernel, out_shape=[jax.ShapeDtypeStruct(s, jnp.float3...]
where the time goes in v13:
time: 80.2 us; the launch traced here: 79.2 us
  Pallas kernels  65.8 us (82%)
  local copies, waits for them, and re-layouts  9.33 us (12%)
  other arithmetic  2.62 us (3%)
  between operations  1.46 us (2%)
    pallas_call x4, Pallas kernels, exchange(): pl.pallas_call(functools.partial(halo_kernel, axes, sizes, len(gathers),...  40.4 us
    pallas_call x1, Pallas kernels, cell_sums_of(): pl.pallas_call(sums_kernel, out_shape=[jax.ShapeDtypeStruct(s, jnp.float3...  20.7 us
    unnamed x34, local copies, waits for them, and re-layouts  4.79 us
    pallas_call x1, Pallas kernels, column_solve(): pl.pallas_call(functools.partial(solve_kernel, levels), out_shape=[jax.Sh...  2.84 us
    pallas_call x1, Pallas kernels, faces_by_kernel(): pl.pallas_call(functools.partial(faces_kernel, parts), out_shape=[jax.Sha...  1.88 us

profile of v13, /device:TPU:121, one launch (start us, length us, event | category | flops | bytes accessed | tf_op | source)
XLA Modules:
  0.0 79.2 jit_solution(17956261316678152229)
XLA Ops:
  1.3 20.7 %shard_map.113 = (f32[10,16,8,128]{3,2,1,0:T(8,128)}, f32[3,16,128]{2,1,0:T(8,128)}, f32[3,16,128]{2,1,0:T(8,128)}, f32[3,16,8]{2,1,0:T(8,128)}, f32[3,16,8]{2,1...) custom-call(s32[1,1]{1,0:T(1,128)} %bitcast.72.count_ref, f32[6,24576]{1,0:T(8,128)} %st_ref.1, ...), custom_call_target="tpu_custom_call" | custom-call | flops 16106127360 | bytes 1933312 | tf_op jit(solution)/shard_map/pallas_call | solution.py:106
  22.0 0.0 copy-start
  22.0 14.2 %shard_map.114 = (f32[3,16,128]{2,1,0:T(8,128)}, f32[3,16,128]{2,1,0:T(8,128)}, f32[3,16,8]{2,1,0:T(8,128)}, f32[3,16,8]{2,1,0:T(8,128)}, f32[3,8,128]{2,1,0:T(8...) custom-call(f32[3,16,128]{2,1,0:T(8,128)} %get-tuple-element.40.refs_0_, ...), custom_call_target="tpu_custom_call" | custom-call | tf_op jit(solution)/shard_map/pallas_call | solution.py:351
  36.1 0.8 fusion.25
  36.9 0.0 copy-start.4
  36.9 0.0 copy-start.5
  36.9 1.0 %fusion.24 = (f32[1,16,7,128]{3,2,1,0:T(8,128)S(1)}, f32[1,16,7,128]{3,2,1,0:T(8,128)S(1)}, f32[1,16,7,128]{3,2,1,0:T(8,128)S(1)}, f32[1,16,7,128]{3,2,1,0:T(8,1...) fusion(f32[10,16,8,128]{3,2,1,0:T(8,128)} %get-tuple-element.39), kind=kLoop, calls=%fused_computation.63 | loop fusion | bytes 688128 | tf_op jit(solution)/shard_map/slice | solution.py:470
  38.0 0.0 copy-done.4
  38.0 0.0 copy-done.5
  38.0 0.2 copy.21
  38.2 0.0 copy-done
  38.2 0.1 fusion.23
  38.3 0.0 copy-start.6
  38.3 0.0 copy-start.7
  38.3 0.2 copy.23
  38.5 0.5 copy-done.6
  39.0 0.0 copy-done.7
  39.1 0.1 fusion.15
  39.2 0.2 copy.17
  39.4 0.2 copy.19
  39.5 0.1 fusion.10
  39.7 0.2 copy.13
  39.8 0.2 copy.15
  40.0 0.1 fusion.5
  40.1 0.7 pad_maximum_fusion.cells_ref
  40.8 1.9 %shard_map.115 = (f32[1,16,128]{2,1,0:T(8,128)}, f32[1,16,128]{2,1,0:T(8,128)}, f32[1,16,8]{2,1,0:T(8,128)}, f32[1,16,8]{2,1,0:T(8,128)}, f32[1,8,128]{2,1,0:T(8,128)}, /*index=5*/f32[1,8,128]{2,1,0:T(8,128)}) custom-call(f32[3,16,8,128]{3,2,1,0:T(8,128)} %pad_maximum_fusion.cells_ref), custom_call_target="tpu_custom_call" | custom-call | tf_op jit(solution)/shard_map/pallas_call | solution.py:397
  42.7 9.2 %shard_map.116 = (f32[1,16,128]{2,1,0:T(8,128)}, f32[1,16,128]{2,1,0:T(8,128)}, f32[1,16,8]{2,1,0:T(8,128)}, f32[1,16,8]{2,1,0:T(8,128)}, f32[1,8,128]{2,1,0:T(8,128)}, /*index=5*/f32[1,8,128]{2,1,0:T(8,128)}) custom-call(f32[1,16,128]{2,1,0:T(8,128)} %get-tuple-element.54.refs_0_, f32[1,16,128]{2,1,0:T(8,128)} %get-tuple-element.55.refs_1_, ...), custom_call_target="tpu_custom_call" | custom-call | tf_op jit(solution)/shard_map/pallas_call | solution.py:351
  51.9 0.0 copy-start.11
  51.9 0.7 copy-done.11
  52.6 0.2 copy.25
  52.8 0.0 copy-start.10
  52.8 0.1 slice_bitcast_fusion
  52.9 0.6 copy-done.10
  53.5 0.2 copy.27
  53.7 0.0 copy-start.2
  53.7 0.0 copy-start.8
  53.7 0.0 copy-start.9
  53.7 0.0 copy-start.16
  53.7 0.0 copy-start.15
  53.7 0.8 %copy-done.2 = f32[16,8,128]{2,1,0:T(8,128)S(1)} copy-done((f32[16,8,128]{2,1,0:T(8,128)S(1)}, f32[16,8,128]{2,1,0:T(8,128)}, u32[]{:S(2)}) %copy-start.2) | copy-done | bytes 65560
  54.5 0.0 copy-done.8
  54.5 0.0 copy-done.9
  54.5 0.0 copy-done.16
  54.5 0.0 copy-done.15
  54.5 0.7 fusion.19.refs_0_
  55.3 8.3 %shard_map.117 = f32[4,16,8,128]{3,2,1,0:T(8,128)} custom-call(f32[16,8,128]{2,1,0:T(8,128)} %fusion.19.refs_0_), custom_call_target="tpu_custom_call" | custom-call | tf_op jit(solution)/shard_map/pallas_call | solution.py:351
  63.5 2.8 %shard_map.118 = (f32[16,8,128]{2,1,0:T(8,128)}, f32[16,8,128]{2,1,0:T(8,128)}, f32[16,128]{1,0:T(8,128)}, f32[16,128]{1,0:T(8,128)}, f32[16,8]{1,0:T(8,128)}, /*index=5*/f32[16,8]{1,0:T(8,128)}) custom-call(f32[64,8,128]{2,1,0:T(8,128)} %bitcast.74, f32[64,8,128]{2,1,0:T(8,128)} %bitcast.75, f32[64,8,128]{2,1,0:T(8,128)} %bitcast.73), custom_call_target="tpu_custom_call" | custom-call | tf_op jit(solution)/shard_map/pallas_call | solution.py:437
  66.4 0.0 copy-start.1
  66.4 8.7 %shard_map.119 = (f32[16,128]{1,0:T(8,128)}, f32[16,128]{1,0:T(8,128)}, f32[16,8]{1,0:T(8,128)}, f32[16,8]{1,0:T(8,128)}) custom-call(f32[16,128]{1,0:T(8,128)} %get-tuple-element.67.refs_0_, f32[16,128]{1,0:T(8,128)} %get-tuple-element.68.refs_1_, f32[16,8]{1,0:T(8,128)} %get-tuple-element.69.refs_2_, f32[16,8]{1,0:T(8,128)} %get-tuple-element.70.refs_3_), custom_call_target="tpu_custom_call" | custom-call | tf_op jit(solution)/shard_map/pallas_call | solution.py:351
  75.1 0.9 %copy.31 = f32[1,16,8,1]{3,2,1,0:T(8,128)S(1)} copy(f32[1,16,8,1]{2,1,3,0:T(8,128)} %bitcast.88) | data formatting | bytes 1024 | tf_op jit(solution)/shard_map/concatenate | solution.py:469
  75.9 0.0 copy-done.1
  75.9 0.0 copy-start.12
  75.9 0.1 slice_bitcast_fusion.4
  76.0 0.6 copy-done.12
  76.6 0.2 copy.33
  76.8 0.1 fusion.21
  76.9 0.0 copy-start.13
  76.9 0.0 copy-start.14
  77.0 0.7 copy-done.13
  77.6 0.0 copy-done.14
  77.6 0.0 copy-start.3
  77.7 0.8 %copy-done.3 = f32[16,8,128]{2,1,0:T(8,128)S(1)} copy-done((f32[16,8,128]{2,1,0:T(8,128)S(1)}, f32[16,8,128]{2,1,0:T(8,128)}, u32[]{:S(2)}) %copy-start.3) | copy-done | bytes 65560
  78.5 0.7 fusion
  (7 shorter events, 0.1 us)
Async XLA Ops:
  22.0 16.2 %copy-start = (f32[10,16,8,128]{3,2,1,0:T(8,128)S(1)}, f32[10,16,8,128]{3,2,1,0:T(8,128)}, u32[]{:S(2)}) copy-start(f32[10,16,8,128]{3,2,1,0:T(8,128)} %get-tuple-element.39) | copy-start | bytes 1966084
  36.9 1.1 %copy-start.4 = (f32[3,16,8]{2,1,0:T(8,128)S(1)}, f32[3,16,8]{2,1,0:T(8,128)}, u32[]{:S(2)}) copy-start(f32[3,16,8]{2,1,0:T(8,128)} %get-tuple-element.49) | copy-start | bytes 4612
  36.9 1.1 %copy-start.5 = (f32[3,16,8]{2,1,0:T(8,128)S(1)}, f32[3,16,8]{2,1,0:T(8,128)}, u32[]{:S(2)}) copy-start(f32[3,16,8]{2,1,0:T(8,128)} %get-tuple-element.48) | copy-start | bytes 4612
  38.3 0.7 copy-start.6
  38.3 0.7 copy-start.7
  51.9 0.7 copy-start.11
  52.8 0.7 copy-start.10
  53.7 0.8 %copy-start.2 = (f32[16,8,128]{2,1,0:T(8,128)S(1)}, f32[16,8,128]{2,1,0:T(8,128)}, u32[]{:S(2)}) copy-start(f32[16,8,128]{2,1,0:T(8,128)} %refs_6_.1) | copy-start | bytes 196612
  53.7 0.8 %copy-start.8 = (f32[1,16,128]{2,1,0:T(8,128)S(1)}, f32[1,16,128]{2,1,0:T(8,128)}, u32[]{:S(2)}) copy-start(f32[1,16,128]{2,1,0:T(8,128)} %get-tuple-element.61) | copy-start | bytes 24580
  53.7 0.8 %copy-start.9 = (f32[1,16,128]{2,1,0:T(8,128)S(1)}, f32[1,16,128]{2,1,0:T(8,128)}, u32[]{:S(2)}) copy-start(f32[1,16,128]{2,1,0:T(8,128)} %get-tuple-element.60) | copy-start | bytes 24580
  53.7 0.8 %copy-start.16 = (f32[1,8,128]{2,1,0:T(8,128)S(1)}, f32[1,8,128]{2,1,0:T(8,128)}, u32[]{:S(2)}) copy-start(f32[1,8,128]{2,1,0:T(8,128)} %get-tuple-element.64) | copy-start | bytes 12292
  53.7 0.8 %copy-start.15 = (f32[1,8,128]{2,1,0:T(8,128)S(1)}, f32[1,8,128]{2,1,0:T(8,128)}, u32[]{:S(2)}) copy-start(f32[1,8,128]{2,1,0:T(8,128)} %get-tuple-element.65) | copy-start | bytes 12292
  66.4 9.6 %copy-start.1 = (f32[16,8,128]{2,1,0:T(8,128)S(1)}, f32[16,8,128]{2,1,0:T(8,128)}, u32[]{:S(2)}) copy-start(f32[16,8,128]{2,1,0:T(8,128)} %get-tuple-element.38) | copy-start | bytes 196612
  75.9 0.7 copy-start.12
  76.9 0.7 copy-start.13
  76.9 0.7 copy-start.14
  77.6 0.8 %copy-start.3 = (f32[16,8,128]{2,1,0:T(8,128)S(1)}, f32[16,8,128]{2,1,0:T(8,128)}, u32[]{:S(2)}) copy-start(f32[16,8,128]{2,1,0:T(8,128)} %get-tuple-element.75) | copy-start | bytes 196612

commit v14 on v13

--- a/solution.py
+++ b/solution.py
@@ -15,7 +15,7 @@
 from jax.experimental import pallas as pl
 from jax.experimental.pallas import tpu as pltpu
 
-CHUNK = 4096
+CHUNK = 8192
 M_ROWS = 32
 N_COLS = 512
 

time: 80.2 us -> 79.5 us (level)
  no operation moved by 1% of the time
where the time goes in v14:
time: 79.5 us; the launch traced here: 78.5 us
  Pallas kernels  65.1 us (82%)
  local copies, waits for them, and re-layouts  9.33 us (12%)
  other arithmetic  2.62 us (3%)
  between operations  1.46 us (2%)
    pallas_call x4, Pallas kernels, exchange(): pl.pallas_call(functools.partial(halo_kernel, axes, sizes, len(gathers),...  40.4 us
    pallas_call x1, Pallas kernels, cell_sums_of(): pl.pallas_call(sums_kernel, out_shape=[jax.ShapeDtypeStruct(s, jnp.float3...  20 us
    unnamed x34, local copies, waits for them, and re-layouts  4.79 us
    pallas_call x1, Pallas kernels, column_solve(): pl.pallas_call(functools.partial(solve_kernel, levels), out_shape=[jax.Sh...  2.84 us
    pallas_call x1, Pallas kernels, faces_by_kernel(): pl.pallas_call(functools.partial(faces_kernel, parts), out_shape=[jax.Sha...  1.88 us

profile of v14, /device:TPU:121, one launch (start us, length us, event | category | flops | bytes accessed | tf_op | source)
XLA Modules:
  0.0 78.5 jit_solution(8068083437567646573)
XLA Ops:
  1.3 20.0 %shard_map.113 = (f32[10,16,8,128]{3,2,1,0:T(8,128)}, f32[3,16,128]{2,1,0:T(8,128)}, f32[3,16,128]{2,1,0:T(8,128)}, f32[3,16,8]{2,1,0:T(8,128)}, f32[3,16,8]{2,1...) custom-call(s32[1,1]{1,0:T(1,128)} %bitcast.72.count_ref, f32[6,24576]{1,0:T(8,128)} %st_ref.1, ...), custom_call_target="tpu_custom_call" | custom-call | flops 16106127360 | bytes 1933312 | tf_op jit(solution)/shard_map/pallas_call | solution.py:106
  21.3 0.0 copy-start
  21.3 14.2 %shard_map.114 = (f32[3,16,128]{2,1,0:T(8,128)}, f32[3,16,128]{2,1,0:T(8,128)}, f32[3,16,8]{2,1,0:T(8,128)}, f32[3,16,8]{2,1,0:T(8,128)}, f32[3,8,128]{2,1,0:T(8...) custom-call(f32[3,16,128]{2,1,0:T(8,128)} %get-tuple-element.40.refs_0_, ...), custom_call_target="tpu_custom_call" | custom-call | tf_op jit(solution)/shard_map/pallas_call | solution.py:351
  35.5 0.8 %fusion.25 = (f32[1,16,128]{2,1,0:T(8,128)S(1)}, f32[1,16,128]{2,1,0:T(8,128)S(1)}, f32[1,16,128]{2,1,0:T(8,128)S(1)}, f32[1,16,128]{2,1,0:T(8,128)S(1)}, f32[1,...) fusion(f32[3,16,128]{2,1,0:T(8,128)} %get-tuple-element.47, f32[3,16,128]{2,1,0:T(8,128)} %get-tuple-element.46), kind=kLoop, calls=%fused_computation.64 | loop fusion | bytes 98304 | tf_op jit(solution)/shard_map/slice | solution.py:499
  36.3 0.0 copy-start.4
  36.3 0.0 copy-start.5
  36.3 1.0 %fusion.24 = (f32[1,16,7,128]{3,2,1,0:T(8,128)S(1)}, f32[1,16,7,128]{3,2,1,0:T(8,128)S(1)}, f32[1,16,7,128]{3,2,1,0:T(8,128)S(1)}, f32[1,16,7,128]{3,2,1,0:T(8,1...) fusion(f32[10,16,8,128]{3,2,1,0:T(8,128)} %get-tuple-element.39), kind=kLoop, calls=%fused_computation.63 | loop fusion | bytes 688128 | tf_op jit(solution)/shard_map/slice | solution.py:470
  37.3 0.0 copy-done.4
  37.3 0.0 copy-done.5
  37.4 0.2 copy.21
  37.5 0.0 copy-done
  37.5 0.1 fusion.23
  37.7 0.0 copy-start.6
  37.7 0.0 copy-start.7
  37.7 0.2 copy.23
  37.8 0.5 copy-done.6
  38.4 0.0 copy-done.7
  38.4 0.1 fusion.15
  38.5 0.2 copy.17
  38.7 0.2 copy.19
  38.9 0.1 fusion.10
  39.0 0.2 copy.13
  39.2 0.2 copy.15
  39.3 0.1 fusion.5
  39.4 0.7 pad_maximum_fusion.cells_ref
  40.1 1.9 %shard_map.115 = (f32[1,16,128]{2,1,0:T(8,128)}, f32[1,16,128]{2,1,0:T(8,128)}, f32[1,16,8]{2,1,0:T(8,128)}, f32[1,16,8]{2,1,0:T(8,128)}, f32[1,8,128]{2,1,0:T(8,128)}, /*index=5*/f32[1,8,128]{2,1,0:T(8,128)}) custom-call(f32[3,16,8,128]{3,2,1,0:T(8,128)} %pad_maximum_fusion.cells_ref), custom_call_target="tpu_custom_call" | custom-call | tf_op jit(solution)/shard_map/pallas_call | solution.py:397
  42.0 9.2 %shard_map.116 = (f32[1,16,128]{2,1,0:T(8,128)}, f32[1,16,128]{2,1,0:T(8,128)}, f32[1,16,8]{2,1,0:T(8,128)}, f32[1,16,8]{2,1,0:T(8,128)}, f32[1,8,128]{2,1,0:T(8,128)}, /*index=5*/f32[1,8,128]{2,1,0:T(8,128)}) custom-call(f32[1,16,128]{2,1,0:T(8,128)} %get-tuple-element.54.refs_0_, f32[1,16,128]{2,1,0:T(8,128)} %get-tuple-element.55.refs_1_, ...), custom_call_target="tpu_custom_call" | custom-call | tf_op jit(solution)/shard_map/pallas_call | solution.py:351
  51.3 0.0 copy-start.11
  51.3 0.7 copy-done.11
  52.0 0.2 copy.25
  52.1 0.0 copy-start.10
  52.1 0.1 slice_bitcast_fusion
  52.2 0.6 copy-done.10
  52.8 0.2 copy.27
  53.0 0.0 copy-start.2
  53.0 0.0 copy-start.8
  53.0 0.0 copy-start.9
  53.0 0.0 copy-start.16
  53.0 0.0 copy-start.15
  53.0 0.8 %copy-done.2 = f32[16,8,128]{2,1,0:T(8,128)S(1)} copy-done((f32[16,8,128]{2,1,0:T(8,128)S(1)}, f32[16,8,128]{2,1,0:T(8,128)}, u32[]{:S(2)}) %copy-start.2) | copy-done | bytes 65560
  53.8 0.0 copy-done.8
  53.8 0.0 copy-done.9
  53.8 0.0 copy-done.16
  53.8 0.0 copy-done.15
  53.9 0.7 fusion.19.refs_0_
  54.6 8.3 %shard_map.117 = f32[4,16,8,128]{3,2,1,0:T(8,128)} custom-call(f32[16,8,128]{2,1,0:T(8,128)} %fusion.19.refs_0_), custom_call_target="tpu_custom_call" | custom-call | tf_op jit(solution)/shard_map/pallas_call | solution.py:351
  62.9 2.8 %shard_map.118 = (f32[16,8,128]{2,1,0:T(8,128)}, f32[16,8,128]{2,1,0:T(8,128)}, f32[16,128]{1,0:T(8,128)}, f32[16,128]{1,0:T(8,128)}, f32[16,8]{1,0:T(8,128)}, /*index=5*/f32[16,8]{1,0:T(8,128)}) custom-call(f32[64,8,128]{2,1,0:T(8,128)} %bitcast.74, f32[64,8,128]{2,1,0:T(8,128)} %bitcast.75, f32[64,8,128]{2,1,0:T(8,128)} %bitcast.73), custom_call_target="tpu_custom_call" | custom-call | tf_op jit(solution)/shard_map/pallas_call | solution.py:437
  65.7 0.0 copy-start.1
  65.7 8.7 %shard_map.119 = (f32[16,128]{1,0:T(8,128)}, f32[16,128]{1,0:T(8,128)}, f32[16,8]{1,0:T(8,128)}, f32[16,8]{1,0:T(8,128)}) custom-call(f32[16,128]{1,0:T(8,128)} %get-tuple-element.67.refs_0_, f32[16,128]{1,0:T(8,128)} %get-tuple-element.68.refs_1_, f32[16,8]{1,0:T(8,128)} %get-tuple-element.69.refs_2_, f32[16,8]{1,0:T(8,128)} %get-tuple-element.70.refs_3_), custom_call_target="tpu_custom_call" | custom-call | tf_op jit(solution)/shard_map/pallas_call | solution.py:351
  74.4 0.9 %copy.31 = f32[1,16,8,1]{3,2,1,0:T(8,128)S(1)} copy(f32[1,16,8,1]{2,1,3,0:T(8,128)} %bitcast.88) | data formatting | bytes 1024 | tf_op jit(solution)/shard_map/concatenate | solution.py:469
  75.3 0.0 copy-done.1
  75.3 0.0 copy-start.12
  75.3 0.1 slice_bitcast_fusion.4
  75.4 0.6 copy-done.12
  76.0 0.2 copy.33
  76.1 0.1 fusion.21
  76.3 0.0 copy-start.13
  76.3 0.0 copy-start.14
  76.3 0.7 copy-done.13
  77.0 0.0 copy-done.14
  77.0 0.0 copy-start.3
  77.0 0.8 %copy-done.3 = f32[16,8,128]{2,1,0:T(8,128)S(1)} copy-done((f32[16,8,128]{2,1,0:T(8,128)S(1)}, f32[16,8,128]{2,1,0:T(8,128)}, u32[]{:S(2)}) %copy-start.3) | copy-done | bytes 65560
  77.8 0.7 fusion
  (7 shorter events, 0.1 us)
Async XLA Ops:
  21.3 16.2 %copy-start = (f32[10,16,8,128]{3,2,1,0:T(8,128)S(1)}, f32[10,16,8,128]{3,2,1,0:T(8,128)}, u32[]{:S(2)}) copy-start(f32[10,16,8,128]{3,2,1,0:T(8,128)} %get-tuple-element.39) | copy-start | bytes 1966084
  36.3 1.1 %copy-start.4 = (f32[3,16,8]{2,1,0:T(8,128)S(1)}, f32[3,16,8]{2,1,0:T(8,128)}, u32[]{:S(2)}) copy-start(f32[3,16,8]{2,1,0:T(8,128)} %get-tuple-element.49) | copy-start | bytes 4612
  36.3 1.1 %copy-start.5 = (f32[3,16,8]{2,1,0:T(8,128)S(1)}, f32[3,16,8]{2,1,0:T(8,128)}, u32[]{:S(2)}) copy-start(f32[3,16,8]{2,1,0:T(8,128)} %get-tuple-element.48) | copy-start | bytes 4612
  37.7 0.7 copy-start.6
  37.7 0.7 copy-start.7
  51.3 0.7 copy-start.11
  52.1 0.7 copy-start.10
  53.0 0.8 %copy-start.2 = (f32[16,8,128]{2,1,0:T(8,128)S(1)}, f32[16,8,128]{2,1,0:T(8,128)}, u32[]{:S(2)}) copy-start(f32[16,8,128]{2,1,0:T(8,128)} %refs_6_.1) | copy-start | bytes 196612
  53.0 0.8 %copy-start.8 = (f32[1,16,128]{2,1,0:T(8,128)S(1)}, f32[1,16,128]{2,1,0:T(8,128)}, u32[]{:S(2)}) copy-start(f32[1,16,128]{2,1,0:T(8,128)} %get-tuple-element.61) | copy-start | bytes 24580
  53.0 0.8 %copy-start.9 = (f32[1,16,128]{2,1,0:T(8,128)S(1)}, f32[1,16,128]{2,1,0:T(8,128)}, u32[]{:S(2)}) copy-start(f32[1,16,128]{2,1,0:T(8,128)} %get-tuple-element.60) | copy-start | bytes 24580
  53.0 0.8 %copy-start.16 = (f32[1,8,128]{2,1,0:T(8,128)S(1)}, f32[1,8,128]{2,1,0:T(8,128)}, u32[]{:S(2)}) copy-start(f32[1,8,128]{2,1,0:T(8,128)} %get-tuple-element.64) | copy-start | bytes 12292
  53.0 0.8 %copy-start.15 = (f32[1,8,128]{2,1,0:T(8,128)S(1)}, f32[1,8,128]{2,1,0:T(8,128)}, u32[]{:S(2)}) copy-start(f32[1,8,128]{2,1,0:T(8,128)} %get-tuple-element.65) | copy-start | bytes 12292
  65.7 9.6 %copy-start.1 = (f32[16,8,128]{2,1,0:T(8,128)S(1)}, f32[16,8,128]{2,1,0:T(8,128)}, u32[]{:S(2)}) copy-start(f32[16,8,128]{2,1,0:T(8,128)} %get-tuple-element.38) | copy-start | bytes 196612
  75.3 0.7 copy-start.12
  76.3 0.7 copy-start.13
  76.3 0.7 copy-start.14
  77.0 0.8 %copy-start.3 = (f32[16,8,128]{2,1,0:T(8,128)S(1)}, f32[16,8,128]{2,1,0:T(8,128)}, u32[]{:S(2)}) copy-start(f32[16,8,128]{2,1,0:T(8,128)} %get-tuple-element.75) | copy-start | bytes 196612

commit v15 on v14

--- a/solution.py
+++ b/solution.py
@@ -15,7 +15,7 @@
 from jax.experimental import pallas as pl
 from jax.experimental.pallas import tpu as pltpu
 
-CHUNK = 8192
+CHUNK = 12288
 M_ROWS = 32
 N_COLS = 512
 

time: 79.5 us -> 79.3 us (level)
  no operation moved by 1% of the time
where the time goes in v15:
time: 79.3 us; the launch traced here: 78.3 us
  Pallas kernels  64.9 us (82%)
  local copies, waits for them, and re-layouts  9.33 us (12%)
  other arithmetic  2.62 us (3%)
  between operations  1.46 us (2%)
    pallas_call x4, Pallas kernels, exchange(): pl.pallas_call(functools.partial(halo_kernel, axes, sizes, len(gathers),...  40.4 us
    pallas_call x1, Pallas kernels, cell_sums_of(): pl.pallas_call(sums_kernel, out_shape=[jax.ShapeDtypeStruct(s, jnp.float3...  19.8 us
    unnamed x34, local copies, waits for them, and re-layouts  4.79 us
    pallas_call x1, Pallas kernels, column_solve(): pl.pallas_call(functools.partial(solve_kernel, levels), out_shape=[jax.Sh...  2.84 us
    pallas_call x1, Pallas kernels, faces_by_kernel(): pl.pallas_call(functools.partial(faces_kernel, parts), out_shape=[jax.Sha...  1.88 us

profile of v15, /device:TPU:121, one launch (start us, length us, event | category | flops | bytes accessed | tf_op | source)
XLA Modules:
  0.0 78.3 jit_solution(17707959056004753784)
XLA Ops:
  1.3 19.8 %shard_map.113 = (f32[10,16,8,128]{3,2,1,0:T(8,128)}, f32[3,16,128]{2,1,0:T(8,128)}, f32[3,16,128]{2,1,0:T(8,128)}, f32[3,16,8]{2,1,0:T(8,128)}, f32[3,16,8]{2,1...) custom-call(s32[1,1]{1,0:T(1,128)} %bitcast.72.count_ref, f32[6,24576]{1,0:T(8,128)} %st_ref.1, ...), custom_call_target="tpu_custom_call" | custom-call | flops 16106127360 | bytes 1933312 | tf_op jit(solution)/shard_map/pallas_call | solution.py:106
  21.1 0.0 copy-start
  21.1 14.2 %shard_map.114 = (f32[3,16,128]{2,1,0:T(8,128)}, f32[3,16,128]{2,1,0:T(8,128)}, f32[3,16,8]{2,1,0:T(8,128)}, f32[3,16,8]{2,1,0:T(8,128)}, f32[3,8,128]{2,1,0:T(8...) custom-call(f32[3,16,128]{2,1,0:T(8,128)} %get-tuple-element.40.refs_0_, ...), custom_call_target="tpu_custom_call" | custom-call | tf_op jit(solution)/shard_map/pallas_call | solution.py:351
  35.3 0.8 %fusion.25 = (f32[1,16,128]{2,1,0:T(8,128)S(1)}, f32[1,16,128]{2,1,0:T(8,128)S(1)}, f32[1,16,128]{2,1,0:T(8,128)S(1)}, f32[1,16,128]{2,1,0:T(8,128)S(1)}, f32[1,...) fusion(f32[3,16,128]{2,1,0:T(8,128)} %get-tuple-element.47, f32[3,16,128]{2,1,0:T(8,128)} %get-tuple-element.46), kind=kLoop, calls=%fused_computation.64 | loop fusion | bytes 98304 | tf_op jit(solution)/shard_map/slice | solution.py:499
  36.1 0.0 copy-start.4
  36.1 0.0 copy-start.5
  36.1 1.0 %fusion.24 = (f32[1,16,7,128]{3,2,1,0:T(8,128)S(1)}, f32[1,16,7,128]{3,2,1,0:T(8,128)S(1)}, f32[1,16,7,128]{3,2,1,0:T(8,128)S(1)}, f32[1,16,7,128]{3,2,1,0:T(8,1...) fusion(f32[10,16,8,128]{3,2,1,0:T(8,128)} %get-tuple-element.39), kind=kLoop, calls=%fused_computation.63 | loop fusion | bytes 688128 | tf_op jit(solution)/shard_map/slice | solution.py:470
  37.1 0.0 copy-done.4
  37.1 0.0 copy-done.5
  37.2 0.2 copy.21
  37.3 0.0 copy-done
  37.3 0.1 fusion.23
  37.4 0.0 copy-start.6
  37.5 0.0 copy-start.7
  37.5 0.2 copy.23
  37.6 0.5 copy-done.6
  38.2 0.0 copy-done.7
  38.2 0.1 fusion.15
  38.3 0.2 copy.17
  38.5 0.2 copy.19
  38.7 0.1 fusion.10
  38.8 0.2 copy.13
  38.9 0.2 copy.15
  39.1 0.1 fusion.5
  39.2 0.7 pad_maximum_fusion.cells_ref
  39.9 1.9 %shard_map.115 = (f32[1,16,128]{2,1,0:T(8,128)}, f32[1,16,128]{2,1,0:T(8,128)}, f32[1,16,8]{2,1,0:T(8,128)}, f32[1,16,8]{2,1,0:T(8,128)}, f32[1,8,128]{2,1,0:T(8,128)}, /*index=5*/f32[1,8,128]{2,1,0:T(8,128)}) custom-call(f32[3,16,8,128]{3,2,1,0:T(8,128)} %pad_maximum_fusion.cells_ref), custom_call_target="tpu_custom_call" | custom-call | tf_op jit(solution)/shard_map/pallas_call | solution.py:397
  41.8 9.2 %shard_map.116 = (f32[1,16,128]{2,1,0:T(8,128)}, f32[1,16,128]{2,1,0:T(8,128)}, f32[1,16,8]{2,1,0:T(8,128)}, f32[1,16,8]{2,1,0:T(8,128)}, f32[1,8,128]{2,1,0:T(8,128)}, /*index=5*/f32[1,8,128]{2,1,0:T(8,128)}) custom-call(f32[1,16,128]{2,1,0:T(8,128)} %get-tuple-element.54.refs_0_, f32[1,16,128]{2,1,0:T(8,128)} %get-tuple-element.55.refs_1_, ...), custom_call_target="tpu_custom_call" | custom-call | tf_op jit(solution)/shard_map/pallas_call | solution.py:351
  51.0 0.0 copy-start.11
  51.1 0.7 copy-done.11
  51.7 0.2 copy.25
  51.9 0.0 copy-start.10
  51.9 0.1 slice_bitcast_fusion
  52.0 0.6 copy-done.10
  52.6 0.2 copy.27
  52.8 0.0 copy-start.2
  52.8 0.0 copy-start.8
  52.8 0.0 copy-start.9
  52.8 0.0 copy-start.16
  52.8 0.0 copy-start.15
  52.8 0.8 %copy-done.2 = f32[16,8,128]{2,1,0:T(8,128)S(1)} copy-done((f32[16,8,128]{2,1,0:T(8,128)S(1)}, f32[16,8,128]{2,1,0:T(8,128)}, u32[]{:S(2)}) %copy-start.2) | copy-done | bytes 65560
  53.6 0.0 copy-done.8
  53.6 0.0 copy-done.9
  53.6 0.0 copy-done.16
  53.6 0.0 copy-done.15
  53.6 0.7 fusion.19.refs_0_
  54.4 8.3 %shard_map.117 = f32[4,16,8,128]{3,2,1,0:T(8,128)} custom-call(f32[16,8,128]{2,1,0:T(8,128)} %fusion.19.refs_0_), custom_call_target="tpu_custom_call" | custom-call | tf_op jit(solution)/shard_map/pallas_call | solution.py:351
  62.7 2.8 %shard_map.118 = (f32[16,8,128]{2,1,0:T(8,128)}, f32[16,8,128]{2,1,0:T(8,128)}, f32[16,128]{1,0:T(8,128)}, f32[16,128]{1,0:T(8,128)}, f32[16,8]{1,0:T(8,128)}, /*index=5*/f32[16,8]{1,0:T(8,128)}) custom-call(f32[64,8,128]{2,1,0:T(8,128)} %bitcast.74, f32[64,8,128]{2,1,0:T(8,128)} %bitcast.75, f32[64,8,128]{2,1,0:T(8,128)} %bitcast.73), custom_call_target="tpu_custom_call" | custom-call | tf_op jit(solution)/shard_map/pallas_call | solution.py:437
  65.5 0.0 copy-start.1
  65.5 8.7 %shard_map.119 = (f32[16,128]{1,0:T(8,128)}, f32[16,128]{1,0:T(8,128)}, f32[16,8]{1,0:T(8,128)}, f32[16,8]{1,0:T(8,128)}) custom-call(f32[16,128]{1,0:T(8,128)} %get-tuple-element.67.refs_0_, f32[16,128]{1,0:T(8,128)} %get-tuple-element.68.refs_1_, f32[16,8]{1,0:T(8,128)} %get-tuple-element.69.refs_2_, f32[16,8]{1,0:T(8,128)} %get-tuple-element.70.refs_3_), custom_call_target="tpu_custom_call" | custom-call | tf_op jit(solution)/shard_map/pallas_call | solution.py:351
  74.2 0.9 %copy.31 = f32[1,16,8,1]{3,2,1,0:T(8,128)S(1)} copy(f32[1,16,8,1]{2,1,3,0:T(8,128)} %bitcast.88) | data formatting | bytes 1024 | tf_op jit(solution)/shard_map/concatenate | solution.py:469
  75.1 0.0 copy-done.1
  75.1 0.0 copy-start.12
  75.1 0.1 slice_bitcast_fusion.4
  75.1 0.6 copy-done.12
  75.8 0.2 copy.33
  75.9 0.1 fusion.21
  76.0 0.0 copy-start.13
  76.0 0.0 copy-start.14
  76.1 0.7 copy-done.13
  76.7 0.0 copy-done.14
  76.8 0.0 copy-start.3
  76.8 0.8 %copy-done.3 = f32[16,8,128]{2,1,0:T(8,128)S(1)} copy-done((f32[16,8,128]{2,1,0:T(8,128)S(1)}, f32[16,8,128]{2,1,0:T(8,128)}, u32[]{:S(2)}) %copy-start.3) | copy-done | bytes 65560
  77.6 0.7 fusion
  (7 shorter events, 0.1 us)
Async XLA Ops:
  21.1 16.2 %copy-start = (f32[10,16,8,128]{3,2,1,0:T(8,128)S(1)}, f32[10,16,8,128]{3,2,1,0:T(8,128)}, u32[]{:S(2)}) copy-start(f32[10,16,8,128]{3,2,1,0:T(8,128)} %get-tuple-element.39) | copy-start | bytes 1966084
  36.1 1.1 %copy-start.4 = (f32[3,16,8]{2,1,0:T(8,128)S(1)}, f32[3,16,8]{2,1,0:T(8,128)}, u32[]{:S(2)}) copy-start(f32[3,16,8]{2,1,0:T(8,128)} %get-tuple-element.49) | copy-start | bytes 4612
  36.1 1.1 %copy-start.5 = (f32[3,16,8]{2,1,0:T(8,128)S(1)}, f32[3,16,8]{2,1,0:T(8,128)}, u32[]{:S(2)}) copy-start(f32[3,16,8]{2,1,0:T(8,128)} %get-tuple-element.48) | copy-start | bytes 4612
  37.4 0.7 copy-start.6
  37.5 0.7 copy-start.7
  51.0 0.7 copy-start.11
  51.9 0.7 copy-start.10
  52.8 0.8 %copy-start.2 = (f32[16,8,128]{2,1,0:T(8,128)S(1)}, f32[16,8,128]{2,1,0:T(8,128)}, u32[]{:S(2)}) copy-start(f32[16,8,128]{2,1,0:T(8,128)} %refs_6_.1) | copy-start | bytes 196612
  52.8 0.8 %copy-start.8 = (f32[1,16,128]{2,1,0:T(8,128)S(1)}, f32[1,16,128]{2,1,0:T(8,128)}, u32[]{:S(2)}) copy-start(f32[1,16,128]{2,1,0:T(8,128)} %get-tuple-element.61) | copy-start | bytes 24580
  52.8 0.8 %copy-start.9 = (f32[1,16,128]{2,1,0:T(8,128)S(1)}, f32[1,16,128]{2,1,0:T(8,128)}, u32[]{:S(2)}) copy-start(f32[1,16,128]{2,1,0:T(8,128)} %get-tuple-element.60) | copy-start | bytes 24580
  52.8 0.8 %copy-start.16 = (f32[1,8,128]{2,1,0:T(8,128)S(1)}, f32[1,8,128]{2,1,0:T(8,128)}, u32[]{:S(2)}) copy-start(f32[1,8,128]{2,1,0:T(8,128)} %get-tuple-element.64) | copy-start | bytes 12292
  52.8 0.8 %copy-start.15 = (f32[1,8,128]{2,1,0:T(8,128)S(1)}, f32[1,8,128]{2,1,0:T(8,128)}, u32[]{:S(2)}) copy-start(f32[1,8,128]{2,1,0:T(8,128)} %get-tuple-element.65) | copy-start | bytes 12292
  65.5 9.6 %copy-start.1 = (f32[16,8,128]{2,1,0:T(8,128)S(1)}, f32[16,8,128]{2,1,0:T(8,128)}, u32[]{:S(2)}) copy-start(f32[16,8,128]{2,1,0:T(8,128)} %get-tuple-element.38) | copy-start | bytes 196612
  75.1 0.7 copy-start.12
  76.0 0.7 copy-start.13
  76.0 0.7 copy-start.14
  76.8 0.8 %copy-start.3 = (f32[16,8,128]{2,1,0:T(8,128)S(1)}, f32[16,8,128]{2,1,0:T(8,128)}, u32[]{:S(2)}) copy-start(f32[16,8,128]{2,1,0:T(8,128)} %get-tuple-element.75) | copy-start | bytes 196612

commit v16 on v15

--- a/solution.py
+++ b/solution.py
@@ -266,20 +266,22 @@
         links.append((axis, 1, me[axis] < sizes[i] - 1, 2 * i + 1, 2 * i))
     barrier = pltpu.get_barrier_semaphore()
     peers = 0
+    k = me["gz"]
+    partner = (k // 2) * 2 + (1 - k % 2)
+    counterpart = (1 - k // 2) * 2 + k % 2
+    diagonal = (1 - k // 2) * 2 + (1 - k % 2)
     for axis, delta, present, _, _ in links:
         if gathered and axis == "gz":
-            continue
+            present = jnp.logical_and(present, k + delta == diagonal)
         peers = peers + present.astype(jnp.int32)
 
         @pl.when(present)
         def _():
             pl.semaphore_signal(barrier, 1, device_id=peer(axis, delta), device_id_type=pl.DeviceIdType.MESH)
     if gathered:
-        for d in range(1, group):
-            pl.semaphore_signal(
-                barrier, 1, device_id=across(lax.rem(me["gz"] + d, group)), device_id_type=pl.DeviceIdType.MESH
-            )
-        peers = peers + (group - 1)
+        for target in (partner, counterpart):
+            pl.semaphore_signal(barrier, 1, device_id=across(target), device_id_type=pl.DeviceIdType.MESH)
+        peers = peers + 2
     pl.semaphore_wait(barrier, peers)
     copies = []
     for axis, delta, present, src, dst in links:
@@ -294,17 +296,34 @@
             copy.start()
     gcopies = []
     for j in range(gathered):
-        for d in range(1, group):
-            slot = j * (group - 1) + d - 1
+        for n, target in enumerate((partner, counterpart)):
             copy = pltpu.make_async_remote_copy(
-                src_ref=gins[j], dst_ref=gouts[j].at[me["gz"]], send_sem=gsend_sem.at[slot],
-                recv_sem=grecv_sem.at[slot], device_id=across(lax.rem(me["gz"] + d, group)),
-                device_id_type=pl.DeviceIdType.MESH,
+                src_ref=gins[j], dst_ref=gouts[j].at[k], send_sem=gsend_sem.at[3 * j + n],
+                recv_sem=grecv_sem.at[3 * j + n], device_id=across(target), device_id_type=pl.DeviceIdType.MESH,
             )
             copy.start()
             gcopies.append(copy)
     for j in range(gathered):
-        gouts[j][me["gz"]] = gins[j][...]
+        gouts[j][k] = gins[j][...]
+    for j in range(gathered):
+        for n, origin in enumerate((partner, counterpart)):
+            incoming = pltpu.make_async_remote_copy(
+                src_ref=gins[j], dst_ref=gouts[j].at[origin], send_sem=gsend_sem.at[3 * j + n],
+                recv_sem=grecv_sem.at[3 * j + n], device_id=across(origin), device_id_type=pl.DeviceIdType.MESH,
+            )
+            incoming.wait_recv()
+        relay = pltpu.make_async_remote_copy(
+            src_ref=gouts[j].at[counterpart], dst_ref=gouts[j].at[counterpart], send_sem=gsend_sem.at[3 * j + 2],
+            recv_sem=grecv_sem.at[3 * j + 2], device_id=across(partner), device_id_type=pl.DeviceIdType.MESH,
+        )
+        relay.start()
+        gcopies.append(relay)
+    for j in range(gathered):
+        relayed = pltpu.make_async_remote_copy(
+            src_ref=gouts[j].at[diagonal], dst_ref=gouts[j].at[diagonal], send_sem=gsend_sem.at[3 * j + 2],
+            recv_sem=grecv_sem.at[3 * j + 2], device_id=across(partner), device_id_type=pl.DeviceIdType.MESH,
+        )
+        relayed.wait_recv()
     for axis, delta, present, src, dst in links:
         incoming = pltpu.make_async_remote_copy(
             src_ref=sends[dst], dst_ref=recvs[src], send_sem=send_sem.at[dst], recv_sem=recv_sem.at[src],
@@ -318,15 +337,6 @@
         @pl.when(jnp.logical_not(present))
         def _():
             recvs[src][...] = jnp.zeros(recvs[src].shape, recvs[src].dtype)
-    for j in range(gathered):
-        for d in range(1, group):
-            slot = j * (group - 1) + d - 1
-            origin = lax.rem(me["gz"] + group - d, group)
-            incoming = pltpu.make_async_remote_copy(
-                src_ref=gins[j], dst_ref=gouts[j].at[origin], send_sem=gsend_sem.at[slot],
-                recv_sem=grecv_sem.at[slot], device_id=across(origin), device_id_type=pl.DeviceIdType.MESH,
-            )
-            incoming.wait_recv()
     for present, copy in copies:
         @pl.when(present)
         def _():
@@ -347,6 +357,7 @@
     sizes = tuple(lax.axis_size(axis) for axis in axes)
     group = lax.axis_size("gz")
     vmem = pl.BlockSpec(memory_space=pltpu.VMEM)
+    assert group == 4 or not gathers
     slots = max(1, len(gathers) * (group - 1))
     outs = pl.pallas_call(
         functools.partial(halo_kernel, axes, sizes, len(gathers), group),

time: 79.3 us -> 78.3 us (0.987)
  Pallas kernels: 64.9 us -> 63.5 us
    pallas_call x4, Pallas kernels: 40.4 us -> 39 us  [exchange(): pl.pallas_call(functools.partial(halo_kernel, axes, sizes, len(gathers),...]
where the time goes in v16:
time: 78.3 us; the launch traced here: 77 us
  Pallas kernels  63.5 us (81%)
  local copies, waits for them, and re-layouts  9.33 us (12%)
  other arithmetic  2.62 us (3%)
  between operations  1.46 us (2%)
    pallas_call x4, Pallas kernels, exchange(): pl.pallas_call(functools.partial(halo_kernel, axes, sizes, len(gathers),...  39 us
    pallas_call x1, Pallas kernels, cell_sums_of(): pl.pallas_call(sums_kernel, out_shape=[jax.ShapeDtypeStruct(s, jnp.float3...  19.8 us
    unnamed x34, local copies, waits for them, and re-layouts  4.79 us
    pallas_call x1, Pallas kernels, column_solve(): pl.pallas_call(functools.partial(solve_kernel, levels), out_shape=[jax.Sh...  2.84 us
    pallas_call x1, Pallas kernels, faces_by_kernel(): pl.pallas_call(functools.partial(faces_kernel, parts), out_shape=[jax.Sha...  1.88 us

profile of v16, /device:TPU:121, one launch (start us, length us, event | category | flops | bytes accessed | tf_op | source)
XLA Modules:
  0.0 77.0 jit_solution(7557225478322519234)
XLA Ops:
  1.3 19.8 %shard_map.113 = (f32[10,16,8,128]{3,2,1,0:T(8,128)}, f32[3,16,128]{2,1,0:T(8,128)}, f32[3,16,128]{2,1,0:T(8,128)}, f32[3,16,8]{2,1,0:T(8,128)}, f32[3,16,8]{2,1...) custom-call(s32[1,1]{1,0:T(1,128)} %bitcast.72.count_ref, f32[6,24576]{1,0:T(8,128)} %st_ref.1, ...), custom_call_target="tpu_custom_call" | custom-call | flops 16106127360 | bytes 1933312 | tf_op jit(solution)/shard_map/pallas_call | solution.py:106
  21.1 0.0 copy-start
  21.1 12.8 %shard_map.114 = (f32[3,16,128]{2,1,0:T(8,128)}, f32[3,16,128]{2,1,0:T(8,128)}, f32[3,16,8]{2,1,0:T(8,128)}, f32[3,16,8]{2,1,0:T(8,128)}, f32[3,8,128]{2,1,0:T(8...) custom-call(f32[3,16,128]{2,1,0:T(8,128)} %get-tuple-element.40.refs_0_, ...), custom_call_target="tpu_custom_call" | custom-call | tf_op jit(solution)/shard_map/pallas_call | solution.py:362
  33.9 0.8 %fusion.25 = (f32[1,16,128]{2,1,0:T(8,128)S(1)}, f32[1,16,128]{2,1,0:T(8,128)S(1)}, f32[1,16,128]{2,1,0:T(8,128)S(1)}, f32[1,16,128]{2,1,0:T(8,128)S(1)}, f32[1,...) fusion(f32[3,16,128]{2,1,0:T(8,128)} %get-tuple-element.47, f32[3,16,128]{2,1,0:T(8,128)} %get-tuple-element.46), kind=kLoop, calls=%fused_computation.64 | loop fusion | bytes 98304 | tf_op jit(solution)/shard_map/slice | solution.py:510
  34.7 0.0 copy-start.4
  34.7 0.0 copy-start.5
  34.7 1.0 %fusion.24 = (f32[1,16,7,128]{3,2,1,0:T(8,128)S(1)}, f32[1,16,7,128]{3,2,1,0:T(8,128)S(1)}, f32[1,16,7,128]{3,2,1,0:T(8,128)S(1)}, f32[1,16,7,128]{3,2,1,0:T(8,1...) fusion(f32[10,16,8,128]{3,2,1,0:T(8,128)} %get-tuple-element.39), kind=kLoop, calls=%fused_computation.63 | loop fusion | bytes 688128 | tf_op jit(solution)/shard_map/slice | solution.py:481
  35.8 0.0 copy-done.4
  35.8 0.0 copy-done.5
  35.8 0.2 copy.21
  36.0 0.0 copy-done
  36.0 0.1 fusion.23
  36.1 0.0 copy-start.6
  36.1 0.0 copy-start.7
  36.1 0.2 copy.23
  36.3 0.5 copy-done.6
  36.8 0.0 copy-done.7
  36.8 0.1 fusion.15
  37.0 0.2 copy.17
  37.1 0.2 copy.19
  37.3 0.1 fusion.10
  37.4 0.2 copy.13
  37.6 0.2 copy.15
  37.7 0.1 fusion.5
  37.9 0.7 pad_maximum_fusion.cells_ref
  38.6 1.9 %shard_map.115 = (f32[1,16,128]{2,1,0:T(8,128)}, f32[1,16,128]{2,1,0:T(8,128)}, f32[1,16,8]{2,1,0:T(8,128)}, f32[1,16,8]{2,1,0:T(8,128)}, f32[1,8,128]{2,1,0:T(8,128)}, /*index=5*/f32[1,8,128]{2,1,0:T(8,128)}) custom-call(f32[3,16,8,128]{3,2,1,0:T(8,128)} %pad_maximum_fusion.cells_ref), custom_call_target="tpu_custom_call" | custom-call | tf_op jit(solution)/shard_map/pallas_call | solution.py:408
  40.4 9.2 %shard_map.116 = (f32[1,16,128]{2,1,0:T(8,128)}, f32[1,16,128]{2,1,0:T(8,128)}, f32[1,16,8]{2,1,0:T(8,128)}, f32[1,16,8]{2,1,0:T(8,128)}, f32[1,8,128]{2,1,0:T(8,128)}, /*index=5*/f32[1,8,128]{2,1,0:T(8,128)}) custom-call(f32[1,16,128]{2,1,0:T(8,128)} %get-tuple-element.54.refs_0_, f32[1,16,128]{2,1,0:T(8,128)} %get-tuple-element.55.refs_1_, ...), custom_call_target="tpu_custom_call" | custom-call | tf_op jit(solution)/shard_map/pallas_call | solution.py:362
  49.7 0.0 copy-start.11
  49.7 0.7 copy-done.11
  50.4 0.2 copy.25
  50.5 0.0 copy-start.10
  50.6 0.1 slice_bitcast_fusion
  50.6 0.6 copy-done.10
  51.2 0.2 copy.27
  51.4 0.0 copy-start.2
  51.4 0.0 copy-start.8
  51.4 0.0 copy-start.9
  51.4 0.0 copy-start.16
  51.4 0.0 copy-start.15
  51.5 0.8 %copy-done.2 = f32[16,8,128]{2,1,0:T(8,128)S(1)} copy-done((f32[16,8,128]{2,1,0:T(8,128)S(1)}, f32[16,8,128]{2,1,0:T(8,128)}, u32[]{:S(2)}) %copy-start.2) | copy-done | bytes 65560
  52.3 0.0 copy-done.8
  52.3 0.0 copy-done.9
  52.3 0.0 copy-done.16
  52.3 0.0 copy-done.15
  52.3 0.7 fusion.19.refs_0_
  53.0 8.3 %shard_map.117 = f32[4,16,8,128]{3,2,1,0:T(8,128)} custom-call(f32[16,8,128]{2,1,0:T(8,128)} %fusion.19.refs_0_), custom_call_target="tpu_custom_call" | custom-call | tf_op jit(solution)/shard_map/pallas_call | solution.py:362
  61.3 2.8 %shard_map.118 = (f32[16,8,128]{2,1,0:T(8,128)}, f32[16,8,128]{2,1,0:T(8,128)}, f32[16,128]{1,0:T(8,128)}, f32[16,128]{1,0:T(8,128)}, f32[16,8]{1,0:T(8,128)}, /*index=5*/f32[16,8]{1,0:T(8,128)}) custom-call(f32[64,8,128]{2,1,0:T(8,128)} %bitcast.74, f32[64,8,128]{2,1,0:T(8,128)} %bitcast.75, f32[64,8,128]{2,1,0:T(8,128)} %bitcast.73), custom_call_target="tpu_custom_call" | custom-call | tf_op jit(solution)/shard_map/pallas_call | solution.py:448
  64.2 0.0 copy-start.1
  64.2 8.7 %shard_map.119 = (f32[16,128]{1,0:T(8,128)}, f32[16,128]{1,0:T(8,128)}, f32[16,8]{1,0:T(8,128)}, f32[16,8]{1,0:T(8,128)}) custom-call(f32[16,128]{1,0:T(8,128)} %get-tuple-element.67.refs_0_, f32[16,128]{1,0:T(8,128)} %get-tuple-element.68.refs_1_, f32[16,8]{1,0:T(8,128)} %get-tuple-element.69.refs_2_, f32[16,8]{1,0:T(8,128)} %get-tuple-element.70.refs_3_), custom_call_target="tpu_custom_call" | custom-call | tf_op jit(solution)/shard_map/pallas_call | solution.py:362
  72.9 0.9 %copy.31 = f32[1,16,8,1]{3,2,1,0:T(8,128)S(1)} copy(f32[1,16,8,1]{2,1,3,0:T(8,128)} %bitcast.88) | data formatting | bytes 1024 | tf_op jit(solution)/shard_map/concatenate | solution.py:480
  73.7 0.0 copy-done.1
  73.7 0.0 copy-start.12
  73.7 0.1 slice_bitcast_fusion.4
  73.8 0.6 copy-done.12
  74.4 0.2 copy.33
  74.6 0.1 fusion.21
  74.7 0.0 copy-start.13
  74.7 0.0 copy-start.14
  74.7 0.7 copy-done.13
  75.4 0.0 copy-done.14
  75.4 0.0 copy-start.3
  75.5 0.8 %copy-done.3 = f32[16,8,128]{2,1,0:T(8,128)S(1)} copy-done((f32[16,8,128]{2,1,0:T(8,128)S(1)}, f32[16,8,128]{2,1,0:T(8,128)}, u32[]{:S(2)}) %copy-start.3) | copy-done | bytes 65560
  76.3 0.7 fusion
  (7 shorter events, 0.1 us)
Async XLA Ops:
  21.1 14.9 %copy-start = (f32[10,16,8,128]{3,2,1,0:T(8,128)S(1)}, f32[10,16,8,128]{3,2,1,0:T(8,128)}, u32[]{:S(2)}) copy-start(f32[10,16,8,128]{3,2,1,0:T(8,128)} %get-tuple-element.39) | copy-start | bytes 1966084
  34.7 1.1 %copy-start.4 = (f32[3,16,8]{2,1,0:T(8,128)S(1)}, f32[3,16,8]{2,1,0:T(8,128)}, u32[]{:S(2)}) copy-start(f32[3,16,8]{2,1,0:T(8,128)} %get-tuple-element.49) | copy-start | bytes 4612
  34.7 1.1 %copy-start.5 = (f32[3,16,8]{2,1,0:T(8,128)S(1)}, f32[3,16,8]{2,1,0:T(8,128)}, u32[]{:S(2)}) copy-start(f32[3,16,8]{2,1,0:T(8,128)} %get-tuple-element.48) | copy-start | bytes 4612
  36.1 0.7 copy-start.6
  36.1 0.7 copy-start.7
  49.7 0.7 copy-start.11
  50.5 0.7 copy-start.10
  51.4 0.8 %copy-start.2 = (f32[16,8,128]{2,1,0:T(8,128)S(1)}, f32[16,8,128]{2,1,0:T(8,128)}, u32[]{:S(2)}) copy-start(f32[16,8,128]{2,1,0:T(8,128)} %refs_6_.1) | copy-start | bytes 196612
  51.4 0.8 %copy-start.8 = (f32[1,16,128]{2,1,0:T(8,128)S(1)}, f32[1,16,128]{2,1,0:T(8,128)}, u32[]{:S(2)}) copy-start(f32[1,16,128]{2,1,0:T(8,128)} %get-tuple-element.61) | copy-start | bytes 24580
  51.4 0.8 %copy-start.9 = (f32[1,16,128]{2,1,0:T(8,128)S(1)}, f32[1,16,128]{2,1,0:T(8,128)}, u32[]{:S(2)}) copy-start(f32[1,16,128]{2,1,0:T(8,128)} %get-tuple-element.60) | copy-start | bytes 24580
  51.4 0.8 %copy-start.16 = (f32[1,8,128]{2,1,0:T(8,128)S(1)}, f32[1,8,128]{2,1,0:T(8,128)}, u32[]{:S(2)}) copy-start(f32[1,8,128]{2,1,0:T(8,128)} %get-tuple-element.64) | copy-start | bytes 12292
  51.4 0.8 %copy-start.15 = (f32[1,8,128]{2,1,0:T(8,128)S(1)}, f32[1,8,128]{2,1,0:T(8,128)}, u32[]{:S(2)}) copy-start(f32[1,8,128]{2,1,0:T(8,128)} %get-tuple-element.65) | copy-start | bytes 12292
  64.2 9.6 %copy-start.1 = (f32[16,8,128]{2,1,0:T(8,128)S(1)}, f32[16,8,128]{2,1,0:T(8,128)}, u32[]{:S(2)}) copy-start(f32[16,8,128]{2,1,0:T(8,128)} %get-tuple-element.38) | copy-start | bytes 196612
  73.7 0.7 copy-start.12
  74.7 0.7 copy-start.13
  74.7 0.7 copy-start.14
  75.4 0.8 %copy-start.3 = (f32[16,8,128]{2,1,0:T(8,128)S(1)}, f32[16,8,128]{2,1,0:T(8,128)}, u32[]{:S(2)}) copy-start(f32[16,8,128]{2,1,0:T(8,128)} %get-tuple-element.75) | copy-start | bytes 196612

commit v17 on v16

--- a/solution.py
+++ b/solution.py
@@ -15,7 +15,7 @@
 from jax.experimental import pallas as pl
 from jax.experimental.pallas import tpu as pltpu
 
-CHUNK = 12288
+CHUNK = 24576
 M_ROWS = 32
 N_COLS = 512
 

time: 78.3 us -> 78.4 us (level)
  no operation moved by 1% of the time
where the time goes in v17:
time: 78.4 us; the launch traced here: 77 us
  Pallas kernels  63.6 us (81%)
  local copies, waits for them, and re-layouts  9.33 us (12%)
  other arithmetic  2.62 us (3%)
  between operations  1.46 us (2%)
    pallas_call x4, Pallas kernels, exchange(): pl.pallas_call(functools.partial(halo_kernel, axes, sizes, len(gathers),...  39 us
    pallas_call x1, Pallas kernels, cell_sums_of(): pl.pallas_call(sums_kernel, out_shape=[jax.ShapeDtypeStruct(s, jnp.float3...  19.9 us
    unnamed x34, local copies, waits for them, and re-layouts  4.79 us
    pallas_call x1, Pallas kernels, column_solve(): pl.pallas_call(functools.partial(solve_kernel, levels), out_shape=[jax.Sh...  2.84 us
    pallas_call x1, Pallas kernels, faces_by_kernel(): pl.pallas_call(functools.partial(faces_kernel, parts), out_shape=[jax.Sha...  1.88 us

profile of v17, /device:TPU:121, one launch (start us, length us, event | category | flops | bytes accessed | tf_op | source)
XLA Modules:
  0.0 77.0 jit_solution(6963688175147487756)
XLA Ops:
  1.3 19.9 %shard_map.113 = (f32[10,16,8,128]{3,2,1,0:T(8,128)}, f32[3,16,128]{2,1,0:T(8,128)}, f32[3,16,128]{2,1,0:T(8,128)}, f32[3,16,8]{2,1,0:T(8,128)}, f32[3,16,8]{2,1...) custom-call(s32[1,1]{1,0:T(1,128)} %bitcast.72.count_ref, f32[6,24576]{1,0:T(8,128)} %st_ref.1, ...), custom_call_target="tpu_custom_call" | custom-call | flops 16106127360 | bytes 1933312 | tf_op jit(solution)/shard_map/pallas_call | solution.py:106
  21.2 0.0 copy-start
  21.2 12.8 %shard_map.114 = (f32[3,16,128]{2,1,0:T(8,128)}, f32[3,16,128]{2,1,0:T(8,128)}, f32[3,16,8]{2,1,0:T(8,128)}, f32[3,16,8]{2,1,0:T(8,128)}, f32[3,8,128]{2,1,0:T(8...) custom-call(f32[3,16,128]{2,1,0:T(8,128)} %get-tuple-element.40.refs_0_, ...), custom_call_target="tpu_custom_call" | custom-call | tf_op jit(solution)/shard_map/pallas_call | solution.py:362
  34.0 0.8 %fusion.25 = (f32[1,16,128]{2,1,0:T(8,128)S(1)}, f32[1,16,128]{2,1,0:T(8,128)S(1)}, f32[1,16,128]{2,1,0:T(8,128)S(1)}, f32[1,16,128]{2,1,0:T(8,128)S(1)}, f32[1,...) fusion(f32[3,16,128]{2,1,0:T(8,128)} %get-tuple-element.47, f32[3,16,128]{2,1,0:T(8,128)} %get-tuple-element.46), kind=kLoop, calls=%fused_computation.64 | loop fusion | bytes 98304 | tf_op jit(solution)/shard_map/slice | solution.py:510
  34.8 0.0 copy-start.4
  34.8 0.0 copy-start.5
  34.8 1.0 %fusion.24 = (f32[1,16,7,128]{3,2,1,0:T(8,128)S(1)}, f32[1,16,7,128]{3,2,1,0:T(8,128)S(1)}, f32[1,16,7,128]{3,2,1,0:T(8,128)S(1)}, f32[1,16,7,128]{3,2,1,0:T(8,1...) fusion(f32[10,16,8,128]{3,2,1,0:T(8,128)} %get-tuple-element.39), kind=kLoop, calls=%fused_computation.63 | loop fusion | bytes 688128 | tf_op jit(solution)/shard_map/slice | solution.py:481
  35.8 0.0 copy-done.4
  35.8 0.0 copy-done.5
  35.9 0.2 copy.21
  36.0 0.0 copy-done
  36.0 0.1 fusion.23
  36.1 0.0 copy-start.6
  36.2 0.0 copy-start.7
  36.2 0.2 copy.23
  36.3 0.5 copy-done.6
  36.9 0.0 copy-done.7
  36.9 0.1 fusion.15
  37.0 0.2 copy.17
  37.2 0.2 copy.19
  37.4 0.1 fusion.10
  37.5 0.2 copy.13
  37.7 0.2 copy.15
  37.8 0.1 fusion.5
  37.9 0.7 pad_maximum_fusion.cells_ref
  38.6 1.9 %shard_map.115 = (f32[1,16,128]{2,1,0:T(8,128)}, f32[1,16,128]{2,1,0:T(8,128)}, f32[1,16,8]{2,1,0:T(8,128)}, f32[1,16,8]{2,1,0:T(8,128)}, f32[1,8,128]{2,1,0:T(8,128)}, /*index=5*/f32[1,8,128]{2,1,0:T(8,128)}) custom-call(f32[3,16,8,128]{3,2,1,0:T(8,128)} %pad_maximum_fusion.cells_ref), custom_call_target="tpu_custom_call" | custom-call | tf_op jit(solution)/shard_map/pallas_call | solution.py:408
  40.5 9.2 %shard_map.116 = (f32[1,16,128]{2,1,0:T(8,128)}, f32[1,16,128]{2,1,0:T(8,128)}, f32[1,16,8]{2,1,0:T(8,128)}, f32[1,16,8]{2,1,0:T(8,128)}, f32[1,8,128]{2,1,0:T(8,128)}, /*index=5*/f32[1,8,128]{2,1,0:T(8,128)}) custom-call(f32[1,16,128]{2,1,0:T(8,128)} %get-tuple-element.54.refs_0_, f32[1,16,128]{2,1,0:T(8,128)} %get-tuple-element.55.refs_1_, ...), custom_call_target="tpu_custom_call" | custom-call | tf_op jit(solution)/shard_map/pallas_call | solution.py:362
  49.8 0.0 copy-start.11
  49.8 0.7 copy-done.11
  50.5 0.2 copy.25
  50.6 0.0 copy-start.10
  50.6 0.1 slice_bitcast_fusion
  50.7 0.6 copy-done.10
  51.3 0.2 copy.27
  51.5 0.0 copy-start.2
  51.5 0.0 copy-start.8
  51.5 0.0 copy-start.9
  51.5 0.0 copy-start.16
  51.5 0.0 copy-start.15
  51.5 0.8 %copy-done.2 = f32[16,8,128]{2,1,0:T(8,128)S(1)} copy-done((f32[16,8,128]{2,1,0:T(8,128)S(1)}, f32[16,8,128]{2,1,0:T(8,128)}, u32[]{:S(2)}) %copy-start.2) | copy-done | bytes 65560
  52.3 0.0 copy-done.8
  52.3 0.0 copy-done.9
  52.3 0.0 copy-done.16
  52.3 0.0 copy-done.15
  52.3 0.7 fusion.19.refs_0_
  53.1 8.3 %shard_map.117 = f32[4,16,8,128]{3,2,1,0:T(8,128)} custom-call(f32[16,8,128]{2,1,0:T(8,128)} %fusion.19.refs_0_), custom_call_target="tpu_custom_call" | custom-call | tf_op jit(solution)/shard_map/pallas_call | solution.py:362
  61.4 2.8 %shard_map.118 = (f32[16,8,128]{2,1,0:T(8,128)}, f32[16,8,128]{2,1,0:T(8,128)}, f32[16,128]{1,0:T(8,128)}, f32[16,128]{1,0:T(8,128)}, f32[16,8]{1,0:T(8,128)}, /*index=5*/f32[16,8]{1,0:T(8,128)}) custom-call(f32[64,8,128]{2,1,0:T(8,128)} %bitcast.74, f32[64,8,128]{2,1,0:T(8,128)} %bitcast.75, f32[64,8,128]{2,1,0:T(8,128)} %bitcast.73), custom_call_target="tpu_custom_call" | custom-call | tf_op jit(solution)/shard_map/pallas_call | solution.py:448
  64.2 0.0 copy-start.1
  64.2 8.7 %shard_map.119 = (f32[16,128]{1,0:T(8,128)}, f32[16,128]{1,0:T(8,128)}, f32[16,8]{1,0:T(8,128)}, f32[16,8]{1,0:T(8,128)}) custom-call(f32[16,128]{1,0:T(8,128)} %get-tuple-element.67.refs_0_, f32[16,128]{1,0:T(8,128)} %get-tuple-element.68.refs_1_, f32[16,8]{1,0:T(8,128)} %get-tuple-element.69.refs_2_, f32[16,8]{1,0:T(8,128)} %get-tuple-element.70.refs_3_), custom_call_target="tpu_custom_call" | custom-call | tf_op jit(solution)/shard_map/pallas_call | solution.py:362
  72.9 0.9 %copy.31 = f32[1,16,8,1]{3,2,1,0:T(8,128)S(1)} copy(f32[1,16,8,1]{2,1,3,0:T(8,128)} %bitcast.88) | data formatting | bytes 1024 | tf_op jit(solution)/shard_map/concatenate | solution.py:480
  73.8 0.0 copy-done.1
  73.8 0.0 copy-start.12
  73.8 0.1 slice_bitcast_fusion.4
  73.9 0.6 copy-done.12
  74.5 0.2 copy.33
  74.7 0.1 fusion.21
  74.8 0.0 copy-start.13
  74.8 0.0 copy-start.14
  74.8 0.7 copy-done.13
  75.5 0.0 copy-done.14
  75.5 0.0 copy-start.3
  75.5 0.8 %copy-done.3 = f32[16,8,128]{2,1,0:T(8,128)S(1)} copy-done((f32[16,8,128]{2,1,0:T(8,128)S(1)}, f32[16,8,128]{2,1,0:T(8,128)}, u32[]{:S(2)}) %copy-start.3) | copy-done | bytes 65560
  76.3 0.7 fusion
  (7 shorter events, 0.1 us)
Async XLA Ops:
  21.2 14.9 %copy-start = (f32[10,16,8,128]{3,2,1,0:T(8,128)S(1)}, f32[10,16,8,128]{3,2,1,0:T(8,128)}, u32[]{:S(2)}) copy-start(f32[10,16,8,128]{3,2,1,0:T(8,128)} %get-tuple-element.39) | copy-start | bytes 1966084
  34.8 1.1 %copy-start.4 = (f32[3,16,8]{2,1,0:T(8,128)S(1)}, f32[3,16,8]{2,1,0:T(8,128)}, u32[]{:S(2)}) copy-start(f32[3,16,8]{2,1,0:T(8,128)} %get-tuple-element.49) | copy-start | bytes 4612
  34.8 1.1 %copy-start.5 = (f32[3,16,8]{2,1,0:T(8,128)S(1)}, f32[3,16,8]{2,1,0:T(8,128)}, u32[]{:S(2)}) copy-start(f32[3,16,8]{2,1,0:T(8,128)} %get-tuple-element.48) | copy-start | bytes 4612
  36.1 0.7 copy-start.6
  36.2 0.7 copy-start.7
  49.8 0.7 copy-start.11
  50.6 0.7 copy-start.10
  51.5 0.8 %copy-start.2 = (f32[16,8,128]{2,1,0:T(8,128)S(1)}, f32[16,8,128]{2,1,0:T(8,128)}, u32[]{:S(2)}) copy-start(f32[16,8,128]{2,1,0:T(8,128)} %refs_6_.1) | copy-start | bytes 196612
  51.5 0.8 %copy-start.8 = (f32[1,16,128]{2,1,0:T(8,128)S(1)}, f32[1,16,128]{2,1,0:T(8,128)}, u32[]{:S(2)}) copy-start(f32[1,16,128]{2,1,0:T(8,128)} %get-tuple-element.61) | copy-start | bytes 24580
  51.5 0.8 %copy-start.9 = (f32[1,16,128]{2,1,0:T(8,128)S(1)}, f32[1,16,128]{2,1,0:T(8,128)}, u32[]{:S(2)}) copy-start(f32[1,16,128]{2,1,0:T(8,128)} %get-tuple-element.60) | copy-start | bytes 24580
  51.5 0.8 %copy-start.16 = (f32[1,8,128]{2,1,0:T(8,128)S(1)}, f32[1,8,128]{2,1,0:T(8,128)}, u32[]{:S(2)}) copy-start(f32[1,8,128]{2,1,0:T(8,128)} %get-tuple-element.64) | copy-start | bytes 12292
  51.5 0.8 %copy-start.15 = (f32[1,8,128]{2,1,0:T(8,128)S(1)}, f32[1,8,128]{2,1,0:T(8,128)}, u32[]{:S(2)}) copy-start(f32[1,8,128]{2,1,0:T(8,128)} %get-tuple-element.65) | copy-start | bytes 12292
  64.2 9.6 %copy-start.1 = (f32[16,8,128]{2,1,0:T(8,128)S(1)}, f32[16,8,128]{2,1,0:T(8,128)}, u32[]{:S(2)}) copy-start(f32[16,8,128]{2,1,0:T(8,128)} %get-tuple-element.38) | copy-start | bytes 196612
  73.8 0.7 copy-start.12
  74.8 0.7 copy-start.13
  74.8 0.7 copy-start.14
  75.5 0.8 %copy-start.3 = (f32[16,8,128]{2,1,0:T(8,128)S(1)}, f32[16,8,128]{2,1,0:T(8,128)}, u32[]{:S(2)}) copy-start(f32[16,8,128]{2,1,0:T(8,128)} %get-tuple-element.75) | copy-start | bytes 196612

commit v18 on v16

--- a/solution.py
+++ b/solution.py
@@ -501,9 +501,7 @@
     )
     sides = (("gx", 2), ("gy", 3), ("gz", 1))
     stress_sums = cell_sums[:6]
-    sf, (all_porosity, all_permeability) = exchange(
-        stress_sums, sides, 0, (porosity, permeability), given=stress_faces
-    )
+    sf, (all_porosity,) = exchange(stress_sums, sides, 0, (porosity,), given=stress_faces)
     height = all_porosity.shape[0]
     def part(dim, parts, c):
         s = parts.index(c)
@@ -523,7 +521,9 @@
             (cell_sums[8] + time_step * force_z) / floored,
         ]
     )
-    vf, _ = exchange(velocity, sides, 1, given=faces_by_kernel(velocity, ((0,), (1,), (2,))))
+    vf, (all_permeability,) = exchange(
+        velocity, sides, 1, (permeability,), given=faces_by_kernel(velocity, ((0,), (1,), (2,)))
+    )
     dilation = (
         along(velocity[0:1], {2: vf[2]}, 2)[0]
         + along(velocity[1:2], {3: vf[3]}, 3)[0]

time: 78.3 us -> 77.9 us (level)
  the two profiles are of different devices: /device:TPU:121 before, /device:TPU:230 now
where the time goes in v18:
time: 77.9 us; the launch traced here: 76.9 us
  Pallas kernels  63.5 us (82%)
  local copies, waits for them, and re-layouts  9.33 us (12%)
  other arithmetic  2.62 us (3%)
  between operations  1.46 us (2%)
    pallas_call x4, Pallas kernels, exchange(): pl.pallas_call(functools.partial(halo_kernel, axes, sizes, len(gathers),...  38.9 us
    pallas_call x1, Pallas kernels, cell_sums_of(): pl.pallas_call(sums_kernel, out_shape=[jax.ShapeDtypeStruct(s, jnp.float3...  19.8 us
    unnamed x34, local copies, waits for them, and re-layouts  4.79 us
    pallas_call x1, Pallas kernels, column_solve(): pl.pallas_call(functools.partial(solve_kernel, levels), out_shape=[jax.Sh...  2.85 us
    pallas_call x1, Pallas kernels, faces_by_kernel(): pl.pallas_call(functools.partial(faces_kernel, parts), out_shape=[jax.Sha...  1.88 us

profile of v18, /device:TPU:230, one launch (start us, length us, event | category | flops | bytes accessed | tf_op | source)
XLA Modules:
  0.0 76.9 jit_solution(9725614094339248994)
XLA Ops:
  1.3 19.8 %shard_map.113 = (f32[10,16,8,128]{3,2,1,0:T(8,128)}, f32[3,16,128]{2,1,0:T(8,128)}, f32[3,16,128]{2,1,0:T(8,128)}, f32[3,16,8]{2,1,0:T(8,128)}, f32[3,16,8]{2,1...) custom-call(s32[1,1]{1,0:T(1,128)} %bitcast.72.count_ref, f32[6,24576]{1,0:T(8,128)} %st_ref.1, ...), custom_call_target="tpu_custom_call" | custom-call | flops 16106127360 | bytes 1933312 | tf_op jit(solution)/shard_map/pallas_call | solution.py:106
  21.1 0.0 copy-start
  21.1 11.5 %shard_map.114 = (f32[3,16,128]{2,1,0:T(8,128)}, f32[3,16,128]{2,1,0:T(8,128)}, f32[3,16,8]{2,1,0:T(8,128)}, f32[3,16,8]{2,1,0:T(8,128)}, f32[3,8,128]{2,1,0:T(8...) custom-call(f32[3,16,128]{2,1,0:T(8,128)} %get-tuple-element.40.refs_0_, ...), custom_call_target="tpu_custom_call" | custom-call | tf_op jit(solution)/shard_map/pallas_call | solution.py:362
  32.6 0.8 %fusion.25 = (f32[1,16,128]{2,1,0:T(8,128)S(1)}, f32[1,16,128]{2,1,0:T(8,128)S(1)}, f32[1,16,128]{2,1,0:T(8,128)S(1)}, f32[1,16,128]{2,1,0:T(8,128)S(1)}, f32[1,...) fusion(f32[3,16,128]{2,1,0:T(8,128)} %get-tuple-element.47, f32[3,16,128]{2,1,0:T(8,128)} %get-tuple-element.46), kind=kLoop, calls=%fused_computation.64 | loop fusion | bytes 98304 | tf_op jit(solution)/shard_map/slice | solution.py:508
  33.4 0.0 copy-start.4
  33.4 0.0 copy-start.5
  33.4 1.0 %fusion.24 = (f32[1,16,7,128]{3,2,1,0:T(8,128)S(1)}, f32[1,16,7,128]{3,2,1,0:T(8,128)S(1)}, f32[1,16,7,128]{3,2,1,0:T(8,128)S(1)}, f32[1,16,7,128]{3,2,1,0:T(8,1...) fusion(f32[10,16,8,128]{3,2,1,0:T(8,128)} %get-tuple-element.39), kind=kLoop, calls=%fused_computation.63 | loop fusion | bytes 688128 | tf_op jit(solution)/shard_map/slice | solution.py:481
  34.4 0.0 copy-done.4
  34.4 0.0 copy-done.5
  34.5 0.2 copy.21
  34.6 0.0 copy-done
  34.6 0.1 fusion.23
  34.7 0.0 copy-start.6
  34.8 0.0 copy-start.7
  34.8 0.2 copy.23
  34.9 0.5 copy-done.6
  35.5 0.0 copy-done.7
  35.5 0.1 fusion.15
  35.6 0.2 copy.17
  35.8 0.2 copy.19
  36.0 0.1 fusion.10
  36.1 0.2 copy.13
  36.2 0.2 copy.15
  36.4 0.1 fusion.5
  36.5 0.7 pad_maximum_fusion.cells_ref
  37.2 1.9 %shard_map.115 = (f32[1,16,128]{2,1,0:T(8,128)}, f32[1,16,128]{2,1,0:T(8,128)}, f32[1,16,8]{2,1,0:T(8,128)}, f32[1,16,8]{2,1,0:T(8,128)}, f32[1,8,128]{2,1,0:T(8,128)}, /*index=5*/f32[1,8,128]{2,1,0:T(8,128)}) custom-call(f32[3,16,8,128]{3,2,1,0:T(8,128)} %pad_maximum_fusion.cells_ref), custom_call_target="tpu_custom_call" | custom-call | tf_op jit(solution)/shard_map/pallas_call | solution.py:408
  39.1 9.8 %shard_map.116 = (f32[1,16,128]{2,1,0:T(8,128)}, f32[1,16,128]{2,1,0:T(8,128)}, f32[1,16,8]{2,1,0:T(8,128)}, f32[1,16,8]{2,1,0:T(8,128)}, f32[1,8,128]{2,1,0:T(8...) custom-call(f32[1,16,128]{2,1,0:T(8,128)} %get-tuple-element.53.refs_0_, ...), custom_call_target="tpu_custom_call" | custom-call | tf_op jit(solution)/shard_map/pallas_call | solution.py:362
  48.9 0.0 copy-start.11
  48.9 0.7 copy-done.11
  49.6 0.2 copy.25
  49.8 0.0 copy-start.10
  49.8 0.1 slice_bitcast_fusion
  49.9 0.6 copy-done.10
  50.5 0.2 copy.27
  50.7 0.0 copy-start.2
  50.7 0.0 copy-start.8
  50.7 0.0 copy-start.9
  50.7 0.0 copy-start.16
  50.7 0.0 copy-start.15
  50.7 0.8 %copy-done.2 = f32[16,8,128]{2,1,0:T(8,128)S(1)} copy-done((f32[16,8,128]{2,1,0:T(8,128)S(1)}, f32[16,8,128]{2,1,0:T(8,128)}, u32[]{:S(2)}) %copy-start.2) | copy-done | bytes 65560
  51.5 0.0 copy-done.8
  51.5 0.0 copy-done.9
  51.5 0.0 copy-done.16
  51.5 0.0 copy-done.15
  51.5 0.7 fusion.19.refs_0_
  52.3 7.5 %shard_map.117 = f32[4,16,8,128]{3,2,1,0:T(8,128)} custom-call(f32[16,8,128]{2,1,0:T(8,128)} %fusion.19.refs_0_), custom_call_target="tpu_custom_call" | custom-call | tf_op jit(solution)/shard_map/pallas_call | solution.py:362
  59.7 2.8 %shard_map.118 = (f32[16,8,128]{2,1,0:T(8,128)}, f32[16,8,128]{2,1,0:T(8,128)}, f32[16,128]{1,0:T(8,128)}, f32[16,128]{1,0:T(8,128)}, f32[16,8]{1,0:T(8,128)}, /*index=5*/f32[16,8]{1,0:T(8,128)}) custom-call(f32[64,8,128]{2,1,0:T(8,128)} %bitcast.74, f32[64,8,128]{2,1,0:T(8,128)} %bitcast.75, f32[64,8,128]{2,1,0:T(8,128)} %bitcast.73), custom_call_target="tpu_custom_call" | custom-call | tf_op jit(solution)/shard_map/pallas_call | solution.py:448
  62.6 0.0 copy-start.1
  62.6 10.2 %shard_map.119 = (f32[16,128]{1,0:T(8,128)}, f32[16,128]{1,0:T(8,128)}, f32[16,8]{1,0:T(8,128)}, f32[16,8]{1,0:T(8,128)}) custom-call(f32[16,128]{1,0:T(8,128)} %get-tuple-element.67.refs_0_, f32[16,128]{1,0:T(8,128)} %get-tuple-element.68.refs_1_, f32[16,8]{1,0:T(8,128)} %get-tuple-element.69.refs_2_, f32[16,8]{1,0:T(8,128)} %get-tuple-element.70.refs_3_), custom_call_target="tpu_custom_call" | custom-call | tf_op jit(solution)/shard_map/pallas_call | solution.py:362
  72.8 0.9 %copy.31 = f32[1,16,8,1]{3,2,1,0:T(8,128)S(1)} copy(f32[1,16,8,1]{2,1,3,0:T(8,128)} %bitcast.88) | data formatting | bytes 1024 | tf_op jit(solution)/shard_map/concatenate | solution.py:480
  73.6 0.0 copy-done.1
  73.6 0.0 copy-start.12
  73.6 0.1 slice_bitcast_fusion.4
  73.7 0.6 copy-done.12
  74.3 0.2 copy.33
  74.5 0.1 fusion.21
  74.6 0.0 copy-start.13
  74.6 0.0 copy-start.14
  74.6 0.7 copy-done.13
  75.3 0.0 copy-done.14
  75.3 0.0 copy-start.3
  75.4 0.8 %copy-done.3 = f32[16,8,128]{2,1,0:T(8,128)S(1)} copy-done((f32[16,8,128]{2,1,0:T(8,128)S(1)}, f32[16,8,128]{2,1,0:T(8,128)}, u32[]{:S(2)}) %copy-start.3) | copy-done | bytes 65560
  76.2 0.7 fusion
  (7 shorter events, 0.1 us)
Async XLA Ops:
  21.1 13.6 %copy-start = (f32[10,16,8,128]{3,2,1,0:T(8,128)S(1)}, f32[10,16,8,128]{3,2,1,0:T(8,128)}, u32[]{:S(2)}) copy-start(f32[10,16,8,128]{3,2,1,0:T(8,128)} %get-tuple-element.39) | copy-start | bytes 1966084
  33.4 1.1 %copy-start.4 = (f32[3,16,8]{2,1,0:T(8,128)S(1)}, f32[3,16,8]{2,1,0:T(8,128)}, u32[]{:S(2)}) copy-start(f32[3,16,8]{2,1,0:T(8,128)} %get-tuple-element.49) | copy-start | bytes 4612
  33.4 1.1 %copy-start.5 = (f32[3,16,8]{2,1,0:T(8,128)S(1)}, f32[3,16,8]{2,1,0:T(8,128)}, u32[]{:S(2)}) copy-start(f32[3,16,8]{2,1,0:T(8,128)} %get-tuple-element.48) | copy-start | bytes 4612
  34.7 0.7 copy-start.6
  34.8 0.7 copy-start.7
  48.9 0.7 copy-start.11
  49.8 0.7 copy-start.10
  50.7 0.8 %copy-start.2 = (f32[16,8,128]{2,1,0:T(8,128)S(1)}, f32[16,8,128]{2,1,0:T(8,128)}, u32[]{:S(2)}) copy-start(f32[16,8,128]{2,1,0:T(8,128)} %refs_6_.2) | copy-start | bytes 196612
  50.7 0.8 %copy-start.8 = (f32[1,16,128]{2,1,0:T(8,128)S(1)}, f32[1,16,128]{2,1,0:T(8,128)}, u32[]{:S(2)}) copy-start(f32[1,16,128]{2,1,0:T(8,128)} %get-tuple-element.61) | copy-start | bytes 24580
  50.7 0.8 %copy-start.9 = (f32[1,16,128]{2,1,0:T(8,128)S(1)}, f32[1,16,128]{2,1,0:T(8,128)}, u32[]{:S(2)}) copy-start(f32[1,16,128]{2,1,0:T(8,128)} %get-tuple-element.60) | copy-start | bytes 24580
  50.7 0.8 %copy-start.16 = (f32[1,8,128]{2,1,0:T(8,128)S(1)}, f32[1,8,128]{2,1,0:T(8,128)}, u32[]{:S(2)}) copy-start(f32[1,8,128]{2,1,0:T(8,128)} %get-tuple-element.64) | copy-start | bytes 12292
  50.7 0.8 %copy-start.15 = (f32[1,8,128]{2,1,0:T(8,128)S(1)}, f32[1,8,128]{2,1,0:T(8,128)}, u32[]{:S(2)}) copy-start(f32[1,8,128]{2,1,0:T(8,128)} %get-tuple-element.65) | copy-start | bytes 12292
  62.6 11.0 %copy-start.1 = (f32[16,8,128]{2,1,0:T(8,128)S(1)}, f32[16,8,128]{2,1,0:T(8,128)}, u32[]{:S(2)}) copy-start(f32[16,8,128]{2,1,0:T(8,128)} %get-tuple-element.38) | copy-start | bytes 196612
  73.6 0.7 copy-start.12
  74.6 0.7 copy-start.13
  74.6 0.7 copy-start.14
  75.3 0.8 %copy-start.3 = (f32[16,8,128]{2,1,0:T(8,128)S(1)}, f32[16,8,128]{2,1,0:T(8,128)}, u32[]{:S(2)}) copy-start(f32[16,8,128]{2,1,0:T(8,128)} %get-tuple-element.75) | copy-start | bytes 196612

commit v19 on v18

--- a/solution.py
+++ b/solution.py
@@ -501,8 +501,7 @@
     )
     sides = (("gx", 2), ("gy", 3), ("gz", 1))
     stress_sums = cell_sums[:6]
-    sf, (all_porosity,) = exchange(stress_sums, sides, 0, (porosity,), given=stress_faces)
-    height = all_porosity.shape[0]
+    sf, _ = exchange(stress_sums, sides, 0, given=stress_faces)
     def part(dim, parts, c):
         s = parts.index(c)
         return {dim: (sf[dim][0][s:s + 1], sf[dim][1][s:s + 1])}
@@ -530,7 +529,7 @@
         + along(velocity[2:3], {1: vf[1]}, 1)[0]
     )
     right_side = -source_rate * (1.0 - porosity) * dilation
-    _, (all_right,) = exchange(right_side, (), 3, (right_side,))
+    _, (all_right, all_porosity) = exchange(right_side, (), 3, (right_side, porosity))
     zero_level = jnp.zeros((1, extent, breadth), jnp.float32)
     pressure, rise, *pressure_faces = column_solve(all_porosity, all_permeability, all_right, levels)
     pf, _ = exchange(pressure, (("gx", 1), ("gy", 2)), 2, given=pressure_faces)

time: 77.9 us -> 79.4 us (1.019)
  the two profiles are of different devices: /device:TPU:230 before, /device:TPU:248 now
where the time goes in v19:
time: 79.4 us; the launch traced here: 78.5 us
  Pallas kernels  64 us (81%)
  local copies, waits for them, and re-layouts  9.68 us (12%)
  other arithmetic  3.37 us (4%)
  between operations  1.44 us (2%)
    pallas_call x4, Pallas kernels, exchange(): pl.pallas_call(functools.partial(halo_kernel, axes, sizes, len(gathers),...  39.5 us
    pallas_call x1, Pallas kernels, cell_sums_of(): pl.pallas_call(sums_kernel, out_shape=[jax.ShapeDtypeStruct(s, jnp.float3...  19.8 us
    concatenate x12, local copies, waits for them, and re-layouts, along(): jnp.concatenate([lower, lax.slice_in_dim(cells, 0, size - 1, axis=dim)],...  3.44 us
    pallas_call x1, Pallas kernels, column_solve(): pl.pallas_call(functools.partial(solve_kernel, levels), out_shape=[jax.Sh...  2.84 us
    unnamed x22, local copies, waits for them, and re-layouts  2.74 us
    pallas_call x1, Pallas kernels, faces_by_kernel(): pl.pallas_call(functools.partial(faces_kernel, parts), out_shape=[jax.Sha...  1.87 us

profile of v19, /device:TPU:248, one launch (start us, length us, event | category | flops | bytes accessed | tf_op | source)
XLA Modules:
  0.0 78.5 jit_solution(16128087049902739820)
XLA Ops:
  1.3 19.8 %shard_map.113 = (f32[10,16,8,128]{3,2,1,0:T(8,128)}, f32[3,16,128]{2,1,0:T(8,128)}, f32[3,16,128]{2,1,0:T(8,128)}, f32[3,16,8]{2,1,0:T(8,128)}, f32[3,16,8]{2,1...) custom-call(s32[1,1]{1,0:T(1,128)} %bitcast.72.count_ref, f32[6,24576]{1,0:T(8,128)} %st_ref.1, ...), custom_call_target="tpu_custom_call" | custom-call | flops 16106127360 | bytes 1933312 | tf_op jit(solution)/shard_map/pallas_call | solution.py:106
  21.1 0.0 copy-start
  21.1 10.0 %shard_map.114 = (f32[3,16,128]{2,1,0:T(8,128)}, f32[3,16,128]{2,1,0:T(8,128)}, f32[3,16,8]{2,1,0:T(8,128)}, f32[3,16,8]{2,1,0:T(8,128)}, f32[3,8,128]{2,1,0:T(8,128)}, /*index=5*/f32[3,8,128]{2,1,0:T(8,128)}) custom-call(f32[3,16,128]{2,1,0:T(8,128)} %get-tuple-element.41.refs_0_, f32[3,16,128]{2,1,0:T(8,128)} %get-tuple-element.42.refs_1_, ...), custom_call_target="tpu_custom_call" | custom-call | tf_op jit(solution)/shard_map/pallas_call | solution.py:362
  31.1 0.7 slice_bitcast_fusion.20
  31.8 0.8 %slice_bitcast_fusion.14 = (f32[1,16,8,1]{2,1,3,0:T(8,128)S(1)}, f32[1,16,8,1]{2,1,3,0:T(8,128)S(1)}, f32[1,16,8,1]{2,1,3,0:T(8,128)S(1)}, f32[1,16,8,1]{2,1,3,0...) fusion(f32[3,16,8]{2,1,0:T(8,128)} %get-tuple-element.50, f32[3,16,8]{2,1,0:T(8,128)} %get-tuple-element.49), kind=kLoop, calls=%fused_computation.53 | loop fusion | bytes 6144 | tf_op jit(solution)/shard_map/concatenate | solution.py:481
  32.6 0.2 copy.13
  32.8 0.2 copy.15
  33.0 0.8 %fusion.25 = (f32[1,16,128]{2,1,0:T(8,128)S(1)}, f32[1,16,128]{2,1,0:T(8,128)S(1)}, f32[1,16,128]{2,1,0:T(8,128)S(1)}, f32[1,16,128]{2,1,0:T(8,128)S(1)}, f32[1,...) fusion(f32[3,16,128]{2,1,0:T(8,128)} %get-tuple-element.48, f32[3,16,128]{2,1,0:T(8,128)} %get-tuple-element.47), kind=kLoop, calls=%fused_computation.64 | loop fusion | bytes 98304 | tf_op jit(solution)/shard_map/slice | solution.py:507
  33.7 1.1 %fusion.23 = (f32[1,16,8,127]{3,2,1,0:T(8,128)S(1)}, f32[1,16,8,127]{3,2,1,0:T(8,128)S(1)}, f32[1,16,8,127]{3,2,1,0:T(8,128)S(1)}, f32[1,16,8,127]{3,2,1,0:T(8,1...) fusion(f32[10,16,8,128]{3,2,1,0:T(8,128)} %get-tuple-element.40), kind=kLoop, calls=%fused_computation.62 | loop fusion | bytes 780288 | tf_op jit(solution)/shard_map/slice | solution.py:481
  34.9 0.0 copy-done
  35.0 0.1 fusion.5
  35.1 0.2 copy.17
  35.2 0.2 copy.19
  35.4 0.1 fusion.10
  35.5 0.2 copy.21
  35.7 0.2 copy.23
  35.9 0.1 fusion.15
  36.0 0.7 pad_maximum_fusion.cells_ref
  36.7 1.9 %shard_map.115 = (f32[1,16,128]{2,1,0:T(8,128)}, f32[1,16,128]{2,1,0:T(8,128)}, f32[1,16,8]{2,1,0:T(8,128)}, f32[1,16,8]{2,1,0:T(8,128)}, f32[1,8,128]{2,1,0:T(8,128)}, /*index=5*/f32[1,8,128]{2,1,0:T(8,128)}) custom-call(f32[3,16,8,128]{3,2,1,0:T(8,128)} %pad_maximum_fusion.cells_ref), custom_call_target="tpu_custom_call" | custom-call | tf_op jit(solution)/shard_map/pallas_call | solution.py:408
  38.5 10.2 %shard_map.116 = (f32[1,16,128]{2,1,0:T(8,128)}, f32[1,16,128]{2,1,0:T(8,128)}, f32[1,16,8]{2,1,0:T(8,128)}, f32[1,16,8]{2,1,0:T(8,128)}, f32[1,8,128]{2,1,0:T(8...) custom-call(f32[1,16,128]{2,1,0:T(8,128)} %get-tuple-element.53.refs_0_, ...), custom_call_target="tpu_custom_call" | custom-call | tf_op jit(solution)/shard_map/pallas_call | solution.py:362
  48.8 0.0 copy-start.8
  48.8 0.9 %copy.25 = f32[16,8,1]{2,1,0:T(8,128)S(1)} copy(f32[16,8,1]{1,0,2:T(8,128)} %bitcast.88) | data formatting | bytes 1024 | tf_op jit(solution)/shard_map/concatenate | solution.py:480
  49.7 0.0 copy-done.8
  49.7 0.2 copy.27
  49.8 0.1 slice_bitcast_fusion
  49.9 0.0 copy-start.2
  49.9 0.0 copy-start.4
  49.9 0.0 copy-start.5
  49.9 0.0 copy-start.9
  50.0 0.0 copy-start.10
  50.0 0.8 copy-done.2
  50.8 0.0 copy-done.4
  50.8 0.0 copy-done.5
  50.8 0.0 copy-done.9
  50.8 0.0 copy-done.10
  50.8 0.7 fusion.19.refs_0_
  51.5 9.2 %shard_map.117 = (f32[4,16,8,128]{3,2,1,0:T(8,128)}, f32[4,16,8,128]{3,2,1,0:T(8,128)}) custom-call(f32[16,8,128]{2,1,0:T(8,128)} %fusion.19.refs_0_, f32[16,8,128]{2,1,0:T(8,128)} %refs_1_.1), custom_call_target="tpu_custom_call" | custom-call | tf_op jit(solution)/shard_map/pallas_call | solution.py:362
  60.7 2.8 %shard_map.118 = (f32[16,8,128]{2,1,0:T(8,128)}, f32[16,8,128]{2,1,0:T(8,128)}, f32[16,128]{1,0:T(8,128)}, f32[16,128]{1,0:T(8,128)}, f32[16,8]{1,0:T(8,128)}, /*index=5*/f32[16,8]{1,0:T(8,128)}) custom-call(f32[64,8,128]{2,1,0:T(8,128)} %bitcast.75, f32[64,8,128]{2,1,0:T(8,128)} %bitcast.73, f32[64,8,128]{2,1,0:T(8,128)} %bitcast.74), custom_call_target="tpu_custom_call" | custom-call | tf_op jit(solution)/shard_map/pallas_call | solution.py:448
  63.5 0.9 %slice_bitcast_fusion.6 = (f32[1,16,7,128]{3,2,1,0:T(8,128)S(1)}, f32[1,16,7,128]{3,2,1,0:T(8,128)S(1)}) fusion(f32[16,8,128]{2,1,0:T(8,128)} %get-tuple-element.39), kind=kLoop, calls=%fused_computation.44 | loop fusion | bytes 229376 | tf_op jit(solution)/shard_map/concatenate | solution.py:481
  64.5 10.0 %shard_map.119 = (f32[16,128]{1,0:T(8,128)}, f32[16,128]{1,0:T(8,128)}, f32[16,8]{1,0:T(8,128)}, f32[16,8]{1,0:T(8,128)}) custom-call(f32[16,128]{1,0:T(8,128)} %get-tuple-element.69.refs_0_, f32[16,128]{1,0:T(8,128)} %get-tuple-element.70.refs_1_, f32[16,8]{1,0:T(8,128)} %get-tuple-element.71.refs_2_, f32[16,8]{1,0:T(8,128)} %get-tuple-element.72.refs_3_), custom_call_target="tpu_custom_call" | custom-call | tf_op jit(solution)/shard_map/pallas_call | solution.py:362
  74.5 0.0 copy-start.1
  74.5 0.8 fusion.20
  75.3 0.0 copy-done.1
  75.4 0.0 copy-start.7
  75.4 0.1 slice_bitcast_fusion.4
  75.4 0.6 copy-done.7
  76.0 0.0 copy-start.6
  76.1 0.2 copy.31
  76.2 0.5 copy-done.6
  76.7 0.2 copy.33
  76.9 0.0 copy-start.3
  76.9 0.1 fusion.21
  77.0 0.7 copy-done.3
  77.8 0.7 fusion
  (4 shorter events, 0.1 us)
Async XLA Ops:
  21.1 13.8 %copy-start = (f32[10,16,8,128]{3,2,1,0:T(8,128)S(1)}, f32[10,16,8,128]{3,2,1,0:T(8,128)}, u32[]{:S(2)}) copy-start(f32[10,16,8,128]{3,2,1,0:T(8,128)} %get-tuple-element.40) | copy-start | bytes 1966084
  48.8 0.9 %copy-start.8 = (f32[1,16,8]{2,1,0:T(8,128)S(1)}, f32[1,16,8]{2,1,0:T(8,128)}, u32[]{:S(2)}) copy-start(f32[1,16,8]{2,1,0:T(8,128)} %get-tuple-element.62) | copy-start | bytes 1540
  49.9 0.8 %copy-start.2 = (f32[16,8,128]{2,1,0:T(8,128)S(1)}, f32[16,8,128]{2,1,0:T(8,128)}, u32[]{:S(2)}) copy-start(f32[16,8,128]{2,1,0:T(8,128)} %refs_1_.1) | copy-start | bytes 196612
  49.9 0.8 %copy-start.4 = (f32[1,16,128]{2,1,0:T(8,128)S(1)}, f32[1,16,128]{2,1,0:T(8,128)}, u32[]{:S(2)}) copy-start(f32[1,16,128]{2,1,0:T(8,128)} %get-tuple-element.60) | copy-start | bytes 24580
  49.9 0.8 %copy-start.5 = (f32[1,16,128]{2,1,0:T(8,128)S(1)}, f32[1,16,128]{2,1,0:T(8,128)}, u32[]{:S(2)}) copy-start(f32[1,16,128]{2,1,0:T(8,128)} %get-tuple-element.59) | copy-start | bytes 24580
  49.9 0.8 %copy-start.9 = (f32[1,8,128]{2,1,0:T(8,128)S(1)}, f32[1,8,128]{2,1,0:T(8,128)}, u32[]{:S(2)}) copy-start(f32[1,8,128]{2,1,0:T(8,128)} %get-tuple-element.64) | copy-start | bytes 12292
  50.0 0.8 %copy-start.10 = (f32[1,8,128]{2,1,0:T(8,128)S(1)}, f32[1,8,128]{2,1,0:T(8,128)}, u32[]{:S(2)}) copy-start(f32[1,8,128]{2,1,0:T(8,128)} %get-tuple-element.63) | copy-start | bytes 12292
  74.5 0.8 %copy-start.1 = (f32[16,8,128]{2,1,0:T(8,128)S(1)}, f32[16,8,128]{2,1,0:T(8,128)}, u32[]{:S(2)}) copy-start(f32[16,8,128]{2,1,0:T(8,128)} %get-tuple-element.39) | copy-start | bytes 196612
  75.4 0.7 copy-start.7
  76.0 0.7 copy-start.6
  76.9 0.8 %copy-start.3 = (f32[16,8,128]{2,1,0:T(8,128)S(1)}, f32[16,8,128]{2,1,0:T(8,128)}, u32[]{:S(2)}) copy-start(f32[16,8,128]{2,1,0:T(8,128)} %get-tuple-element.77) | copy-start | bytes 196612
